TPU v7x, 128 devices: a whole 4x4x4 slice. The times are simulated.
128 devices in a mesh: dp: 32 (over x, z, core), label: 4 (over y).
Axes of the slice: x: 4, y: 4, z: 4, core: 2. Of those that a mesh axis runs over, the one named last changes fastest.
Arguments:
- queries: bfloat16 [131072, 256], P('dp'), may hold values from -6 to 6
- cluster: int32 [131072, 1], P('dp'), may hold values from 0 to 63; in each aligned block of 4096 rows (0 to 4095, 4096 to 8191, ...) at most 128 rows name the same one
- anchor_latent: bfloat16 [131072, 256], P('dp'), may hold values from -6 to 6
- anchor_labels: bfloat16 [131072, 1024], P('dp', 'label'), may hold values from -6 to 6
- tile_list: int32 [64, 16], P('dp'), may hold values from 0 to 1023, as said below
Outputs:
- predicted: bfloat16 [131072, 1024], P('dp', 'label')
Inputs may be any that keep to these rules, and one draw needn't show every extreme that they name: `tile_list`: the 32 tiles listed in the rows of the blocks that one index of dp owns (rows d * 2 to d * 2 + 1 for index d) include at most 2 tiles held by any one index of dp (tile t is held by index t // 32), and exactly 2 from some index, for every d. `cluster`: among the rows of one index of dp no block is named more than 128 times; some block is named exactly 128 times. Block b is owned by index b // 2.
All inputs are finite; a program needn't handle non-finite values.
Results may differ from a plain program's by a relative error of at most 0.0097.
Values may be sent and summed in bfloat16 or wider, within the bound.
No kernel may reach another device: no remote copies, remote signals or barrier semaphores. Data moves between devices by JAX's collectives and lax.ppermute only.
A program may use at most 128 MiB of HBM per device.

v0:
```python
import jax
import jax.numpy as jnp
from jax import lax
from jax.sharding import PartitionSpec as P

TILE = 128


kernel_width = 0.025
norm_epsilon = 1e-05


def unit_rows(values):
    widened = values.astype(jnp.float32)
    scaled = widened * lax.rsqrt(jnp.mean(widened * widened, axis=-1, keepdims=True) + norm_epsilon)
    return scaled.astype(jnp.bfloat16)


def transfer_block(row_block, latent_keys, label_values):
    similarity = (
        jnp.einsum("rl,al->ra", row_block, latent_keys, preferred_element_type=jnp.float32)
        / latent_keys.shape[1]
    )
    kernel = jnp.exp(similarity / kernel_width)
    totals = jnp.sum(kernel, axis=1, keepdims=True)
    weighted = jnp.dot(
        kernel.astype(jnp.bfloat16), label_values, preferred_element_type=jnp.float32
    )
    return (weighted / totals).astype(jnp.bfloat16)


def rank_within(targets, target_count):
    target_hits = (targets[:, None] == jnp.arange(target_count, dtype=jnp.int32)[None, :]).astype(
        jnp.int32
    )
    return jnp.sum((jnp.cumsum(target_hits, axis=0) - 1) * target_hits, axis=1)


def shards(queries, cluster, anchor_latent, anchor_labels, tile_list):
    dp_count = lax.axis_size("dp")
    query_count = queries.shape[0]
    latent_width = queries.shape[1]
    blocks_here = tile_list.shape[0]
    tiles_each = tile_list.shape[1]
    block_total = blocks_here * dp_count
    capacity = 2 * query_count // block_total
    tiles_here = anchor_latent.shape[0] // TILE
    column_count = anchor_labels.shape[1]
    request_count = blocks_here * tiles_each
    fetch_slots = max(2, (2 * request_count + dp_count - 1) // dp_count)
    block_ids = cluster[:, 0]
    ranking = rank_within(block_ids, block_total)
    dest_dev = block_ids // blocks_here
    dest_slot = block_ids % blocks_here * capacity + ranking
    normed = unit_rows(queries)
    packed = (
        jnp.zeros((dp_count, blocks_here * capacity, latent_width), jnp.bfloat16)
        .at[dest_dev, dest_slot]
        .set(normed)
    )
    arrived = lax.all_to_all(packed, "dp", split_axis=0, concat_axis=0, tiled=True)
    wanted = tile_list.reshape(request_count)
    source_dev = wanted // tiles_here
    source_tile = wanted % tiles_here
    source_rank = rank_within(source_dev, dp_count)
    asking = (
        jnp.zeros((dp_count, fetch_slots), jnp.int32).at[source_dev, source_rank].set(source_tile)
    )
    asked_for = lax.all_to_all(asking, "dp", split_axis=0, concat_axis=0, tiled=True)
    anchor_normed = unit_rows(anchor_latent).reshape(tiles_here, TILE, latent_width)
    label_tiles = anchor_labels.reshape(tiles_here, TILE, column_count)
    label_out = label_tiles[asked_for]
    got_latent, got_labels = (
        lax.all_to_all(anchor_normed[asked_for], "dp", split_axis=0, concat_axis=0, tiled=True),
        lax.all_to_all(label_out, "dp", split_axis=0, concat_axis=0, tiled=True),
    )
    key_latent = got_latent[source_dev, source_rank].reshape(
        blocks_here, tiles_each * TILE, latent_width
    )
    key_labels = got_labels[source_dev, source_rank].reshape(
        blocks_here, tiles_each * TILE, column_count
    )
    row_total = dp_count * capacity
    pieces = row_total // 1024
    results = []
    for block_no in range(blocks_here):
        row_block = arrived[:, block_no * capacity : (block_no + 1) * capacity, :].reshape(
            pieces, row_total // pieces, latent_width
        )
        latent_keys = key_latent[block_no]
        label_values = key_labels[block_no]
        scored = lax.map(
            lambda piece_rows: transfer_block(piece_rows, latent_keys, label_values), row_block
        )
        results.append(scored.reshape(dp_count, capacity, column_count))
    answers = jnp.concatenate(results, axis=1)
    returned = lax.all_to_all(answers, "dp", split_axis=0, concat_axis=0, tiled=True)
    return returned[dest_dev, dest_slot]


def solution(mesh):
    placed = (P("dp", None), P("dp", None), P("dp", None), P("dp", "label"), P("dp", None))
    return jax.shard_map(
        shards, mesh=mesh, in_specs=placed, out_specs=P("dp", "label"), check_vma=False
    )
```

profile of v0, /device:TPU:1, one launch (start us, length us, event | category | flops | bytes accessed | tf_op | source)
XLA Modules:
  0.0 431.2 jit_solution(18164515050969909678)
XLA Ops:
  0.0 0.0 copy-start
  0.0 0.9 reshape.205
  0.9 0.8 reshape.204
  1.7 0.1 fusion.49
  1.8 0.1 reduce_window_sum.25
  1.8 0.2 select_reduce_fusion
  2.0 2.0 scatter_fusion
  4.1 0.7 copy.12
  4.8 9.4 %all-to-all-start.1 = ((s32[32,1,2]{2,1,0:T(1,128)}), s32[32,1,2]{2,1,0:T(1,128)S(1)}, u32[]{:S(2)}, u32[]{:S(2)}) async-start(s32[32,1,2]{2,1,0:T(1,128)} %copy.12), calls=%async_computation.1 | async-start | bytes 32768 | tf_op jit(solution)/shard_map/all_to_all | solution.py:69
  14.2 1.8 fusion.46
  16.0 32.3 %reduce-window.6 = s32[64,32,128]{2,1,0:T(8,128)S(1)} reduce-window(s32[64,32,128]{2,1,0:T(8,128)} %fusion.46, s32[]{:T(128)} %copy.34), window={size=1x1x128 pad=0_0x0_0x127_0}, to_apply=%region_0.0 | reduce-window | flops 33292288 | bytes 2097156 | tf_op jit(solution)/shard_map/reduce-window
  48.3 1.3 slice.48
  49.6 1.7 copy.15
  51.3 0.2 reduce-window.9
  51.5 0.3 add_add_fusion
  51.9 0.8 fusion.45
  52.7 0.2 shift-left_or_fusion
  52.9 0.1 multiply_reduce_fusion
  53.1 0.1 and_reduce_fusion
  53.2 0.6 fusion.36
  53.8 22.7 %scatter_custom_fusion.1 = bf16[8192,256]{1,0:T(8,128)(2,1)} fusion(s32[4096]{0:T(1024)S(1)} %broadcast_select_fusion, bf16[4096,256]{1,0:T(8,128)(2,1)} %param.9, bf16[]{:T(256)} %constant.138.clone.1, f32[4096]{0:T(1024)S(1)} %add_rsqrt_fusion.1), kind=kCustom, calls=%fused_computation.42 | custom fusion | flops 3145728 | bytes 6307842
  76.6 0.0 all-to-all-done.1
  76.6 7.4 %all-to-all-start = ((bf16[32,256,256]{2,1,0:T(8,128)(2,1)}), bf16[32,256,256]{2,1,0:T(8,128)(2,1)}, u32[]{:S(2)}, u32[]{:S(2)}) async-start(bf16[32,256,256]{2,1,0:T(8,128)(2,1)} %bitcast.96), calls=%async_computation | async-start | bytes 8388608 | tf_op jit(solution)/shard_map/all_to_all | solution.py:61
  84.0 0.0 copy-start.3
  84.1 2.4 fusion.38
  86.4 1.7 fusion.39
  88.1 0.1 copy.13
  88.2 0.1 copy.14
  88.3 0.1 reshape.216
  88.4 4.3 %gather_fusion = bf16[64,128,256]{2,1,0:T(8,128)(2,1)} fusion(bf16[32,128,256]{2,1,0:T(8,128)(2,1)} %bitcast.95, s32[1024]{0:T(1024)S(1)} %pad_clamp_fusion), kind=kCustom, calls=%fused_computation | custom fusion | bytes 8388864 | tf_op jit(solution)/shard_map/gather | solution.py:74
  92.8 43.4 %all-to-all-done = bf16[32,256,256]{2,1,0:T(8,128)(2,1)} async-done(((bf16[32,256,256]{2,1,0:T(8,128)(2,1)}), bf16[32,256,256]{2,1,0:T(8,128)(2,1)}, u32[]{:S(2)}, u32[]{:S(2)}) %all-to-all-start) | async-done | bytes 4194336 | tf_op jit(solution)/shard_map/all_to_all | solution.py:61
  136.2 7.1 %all-to-all-start.2 = ((bf16[32,2,128,256]{3,2,1,0:T(8,128)(2,1)}), bf16[32,2,128,256]{3,2,1,0:T(8,128)(2,1)}, u32[]{:S(2)}, u32[]{:S(2)}) async-start(bf16[32,2,128,256]{3,2,1,0:T(8,128)(2,1)} %bitcast.98), calls=%async_computation.2 | async-start | bytes 8388608 | tf_op jit(solution)/shard_map/all_to_all | solution.py:74
  143.3 2.8 gather_fusion.2
  146.1 49.3 %all-to-all-done.2 = bf16[32,2,128,256]{3,2,1,0:T(8,128)(2,1)} async-done(((bf16[32,2,128,256]{3,2,1,0:T(8,128)(2,1)}), bf16[32,2,128,256]{3,2,1,0:T(8,128)(2,1)}, u32[]{:S(2)}, u32[]{:S(2)}) %all-to-all-start.2) | async-done | bytes 4194336 | tf_op jit(solution)/shard_map/all_to_all | solution.py:74
  195.4 7.1 %all-to-all-start.3 = ((bf16[32,2,128,256]{3,2,1,0:T(8,128)(2,1)}), bf16[32,2,128,256]{3,2,1,0:T(8,128)(2,1)}, u32[]{:S(2)}, u32[]{:S(2)}) async-start(bf16[32,2,128,256]{3,2,1,0:T(8,128)(2,1)} %bitcast.97), calls=%async_computation.3 | async-start | bytes 8388608 | tf_op jit(solution)/shard_map/all_to_all | solution.py:75
  202.5 4.8 %fusion.53 = (bf16[32,128,256]{2,1,0:T(8,128)(2,1)}, bf16[32,128,256]{2,1,0:T(8,128)(2,1)}) fusion(bf16[32,256,256]{2,1,0:T(8,128)(2,1)} %all-to-all-done), kind=kLoop, calls=%fused_computation.90 | loop fusion | bytes 8388608 | tf_op jit(solution)/shard_map/slice | solution.py:87
  207.2 4.2 gather_fusion.1
  211.5 1.7 fusion.55
  213.2 41.4 %all-to-all-done.3 = bf16[32,2,128,256]{3,2,1,0:T(8,128)(2,1)} async-done(((bf16[32,2,128,256]{3,2,1,0:T(8,128)(2,1)}), bf16[32,2,128,256]{3,2,1,0:T(8,128)(2,1)}, u32[]{:S(2)}, u32[]{:S(2)}) %all-to-all-start.3) | async-done | bytes 4194336 | tf_op jit(solution)/shard_map/all_to_all | solution.py:75
  254.6 4.2 gather_fusion.3
  258.8 2.7 fusion.54
  261.5 1.5 broadcast.246.clone.1
  263.0 18.9 %while.24 = (s32[]{:T(128)}, bf16[4,1024,256]{2,1,0:T(8,128)(2,1)}, bf16[4,1024,256]{2,1,0:T(8,128)(2,1)}, bf16[2048,256]{1,0:T(8,128)(2,1)S(1)}, bf16[2048,256]{1,0:T(8,128)(2,1)}, /*index=5*/s32[]{:T(128)}) while((s32[]{:T(128)}, bf16[4,1024,256]{2,1,0:T(8,128)(2,1)}, bf16[4,1024,256]{2,1,0:T(8,128)(2,1)}, ...), condition=%wide.region_11.12_spmd, body=%wide.region_9.11_spmd.sunk | while | flops 2156395520 | bytes 24126560 | solution.py:92
  263.0 2.6 fusion.73
  265.6 2.1 fusion.74
  267.7 2.6 fusion.73
  270.3 2.1 fusion.74
  272.5 2.6 fusion.73
  275.1 2.1 fusion.74
  277.2 2.6 fusion.73
  279.8 2.1 fusion.74
  281.9 1.5 broadcast.246.clone
  283.4 18.4 %while.25 = (s32[]{:T(128)}, bf16[4,1024,256]{2,1,0:T(8,128)(2,1)}, bf16[4,1024,256]{2,1,0:T(8,128)(2,1)}, bf16[2048,256]{1,0:T(8,128)(2,1)S(1)}, bf16[2048,256]{1,0:T(8,128)(2,1)S(1)}, /*index=5*/s32[]{:T(128)}) while((s32[]{:T(128)}, bf16[4,1024,256]{2,1,0:T(8,128)(2,1)}, bf16[4,1024,256]{2,1,0:T(8,128)(2,1)}, ...), condition=%wide.region_14.15_spmd, body=%wide.region_12.14_spmd.sunk | while | flops 2156395520 | bytes 19932228 | solution.py:92
  283.4 2.5 fusion.78
  285.9 2.1 fusion.79
  288.0 2.5 fusion.78
  290.5 2.1 fusion.79
  292.6 2.5 fusion.78
  295.1 2.1 fusion.79
  297.2 2.5 fusion.78
  299.7 2.1 fusion.79
  301.8 2.6 pad_maximum_fusion
  304.5 57.6 %all_to_all.32 = bf16[32,256,256]{2,1,0:T(8,128)(2,1)} all-to-all(bf16[32,256,256]{2,1,0:T(8,128)(2,1)S(1)} %pad_maximum_fusion), channel_id=1, replica_groups=mesh['dp'=32,'label'=4] {'dp'}, dimensions={0} | all-to-all | bytes 8388608 | tf_op jit(solution)/shard_map/all_to_all | solution.py:97
  362.1 69.1 %gather_fusion.4 = bf16[4096,256]{1,0:T(8,128)(2,1)} fusion(bf16[32,256,256]{2,1,0:T(8,128)(2,1)} %all_to_all.32, s32[4096]{0:T(1024)S(1)} %bitcast.91), kind=kCustom, calls=%fused_computation.4 | custom fusion | bytes 4227072 | tf_op jit(solution)/shard_map/gather | solution.py:98
  (29 shorter events, 0.1 us)
Async XLA Ops:
  0.0 143.3 %copy-start = (bf16[4096,256]{1,0:T(8,128)(2,1)S(1)}, bf16[4096,256]{1,0:T(8,128)(2,1)}, u32[]{:S(2)}) copy-start(bf16[4096,256]{1,0:T(8,128)(2,1)} %param.12) | copy-start | bytes 6291460
  4.8 71.8 %all-to-all-start.1 = ((s32[32,1,2]{2,1,0:T(1,128)}), s32[32,1,2]{2,1,0:T(1,128)S(1)}, u32[]{:S(2)}, u32[]{:S(2)}) async-start(s32[32,1,2]{2,1,0:T(1,128)} %copy.12), calls=%async_computation.1 | async-start | bytes 32768 | tf_op jit(solution)/shard_map/all_to_all | solution.py:69
  49.6 2.3 copy-start.5
  49.6 3.3 copy-start.7
  49.6 3.4 copy-start.6
  51.5 1.6 copy-start.2
  76.6 59.6 %all-to-all-start = ((bf16[32,256,256]{2,1,0:T(8,128)(2,1)}), bf16[32,256,256]{2,1,0:T(8,128)(2,1)}, u32[]{:S(2)}, u32[]{:S(2)}) async-start(bf16[32,256,256]{2,1,0:T(8,128)(2,1)} %bitcast.96), calls=%async_computation | async-start | bytes 8388608 | tf_op jit(solution)/shard_map/all_to_all | solution.py:61
  84.0 2.4 copy-start.3
  136.2 59.2 %all-to-all-start.2 = ((bf16[32,2,128,256]{3,2,1,0:T(8,128)(2,1)}), bf16[32,2,128,256]{3,2,1,0:T(8,128)(2,1)}, u32[]{:S(2)}, u32[]{:S(2)}) async-start(bf16[32,2,128,256]{3,2,1,0:T(8,128)(2,1)} %bitcast.98), calls=%async_computation.2 | async-start | bytes 8388608 | tf_op jit(solution)/shard_map/all_to_all | solution.py:74
  195.4 59.2 %all-to-all-start.3 = ((bf16[32,2,128,256]{3,2,1,0:T(8,128)(2,1)}), bf16[32,2,128,256]{3,2,1,0:T(8,128)(2,1)}, u32[]{:S(2)}, u32[]{:S(2)}) async-start(bf16[32,2,128,256]{3,2,1,0:T(8,128)(2,1)} %bitcast.97), calls=%async_computation.3 | async-start | bytes 8388608 | tf_op jit(solution)/shard_map/all_to_all | solution.py:75
  263.0 2.6 copy-start.4
  267.7 2.6 copy-start.4
  272.5 2.6 copy-start.4
  277.2 2.6 copy-start.4
  362.0 69.1 %copy-start.1 = (bf16[4096,256]{1,0:T(8,128)(2,1)S(1)}, bf16[4096,256]{1,0:T(8,128)(2,1)}, u32[]{:S(2)}) copy-start(bf16[4096,256]{1,0:T(8,128)(2,1)} %param.12) | copy-start | bytes 6291460
where the time goes:
time: 435 us; the launch traced here: 431 us
  waiting for transfers between devices  134 us (31%)
  local copies, waits for them, and re-layouts  105 us (24%)
  other arithmetic  66.4 us (15%)
  blocking collectives  57.6 us (13%)
  matrix products  37.3 us (9%)
  starting transfers between devices  31 us (7%)
    gather x1, local copies, waits for them, and re-layouts, shards(): return returned[dest_dev, dest_slot]  69.1 us
    all_to_all x1, blocking collectives, shards(): lax.all_to_all(answers, 'dp', split_axis=0, concat_axis=0, tiled=True)  57.6 us
    all_to_all x1, waiting for transfers between devices, shards(): lax.all_to_all(anchor_normed[asked_for], 'dp', split_axis=0, concat_axis=...  49.3 us
    all_to_all x1, waiting for transfers between devices, shards(): lax.all_to_all(packed, 'dp', split_axis=0, concat_axis=0, tiled=True)  43.4 us
    all_to_all x1, waiting for transfers between devices, shards(): lax.all_to_all(label_out, 'dp', split_axis=0, concat_axis=0, tiled=True)  41.4 us
    another operation x2, other arithmetic  32.5 us
    unnamed x4, other arithmetic  23 us
    dot_general x8, matrix products, transfer_block(): jnp.einsum('rl,al->ra', row_block, latent_keys, preferred_element_type=jn...  20.3 us
  transfers between devices with their start and end apart: 4, of which 3 were waited for; matrix products, arithmetic and copies ran while one was open for 20% of the time, Pallas kernels for 0%

commit v1 on v0

v1 whole, which is shorter than its diff:
```python
import functools
import jax
import jax.numpy as jnp
from jax import lax
from jax.sharding import PartitionSpec as P
from jax.experimental import pallas as pl
from jax.experimental.pallas import tpu as pltpu

TILE = 128
kernel_width = 0.025
norm_epsilon = 1e-05
PLANES = 4
LOG2E = 1.4426950408889634
VMEM = pl.BlockSpec(memory_space=pltpu.VMEM)
ANY = pl.BlockSpec(memory_space=pl.ANY)
SMEM = pl.BlockSpec(memory_space=pltpu.SMEM)


def unit_rows(values):
    widened = values.astype(jnp.float32)
    scaled = widened * lax.rsqrt(jnp.mean(widened * widened, axis=-1, keepdims=True) + norm_epsilon)
    return scaled.astype(jnp.bfloat16)


def params(**kw):
    return pltpu.CompilerParams(vmem_limit_bytes=56 * 1024 * 1024, **kw)


def rank_kernel(blocks, part, half, y_ref, ids_ref, inv_ref, pos_ref):
    y = y_ref[0]
    count = ids_ref.shape[1]
    step = 256
    upper = (
        lax.broadcasted_iota(jnp.int32, (step, step), 0)
        <= lax.broadcasted_iota(jnp.int32, (step, step), 1)
    ).astype(jnp.bfloat16)
    block_no = lax.broadcasted_iota(jnp.int32, (blocks, step), 0)
    slot_no = lax.broadcasted_iota(jnp.int32, (part, step), 0) + part * y
    lane = lax.broadcasted_iota(jnp.int32, (1, step), 1)
    carry = jnp.zeros((blocks, 1), jnp.float32)
    high = jnp.zeros((blocks, part), jnp.float32)
    low = jnp.zeros((blocks, part), jnp.float32)
    nt = (((1,), (1,)), ((), ()))
    for c in range(count // step):
        ids = ids_ref[:, c * step : (c + 1) * step]
        hit = block_no == ids
        hits = hit.astype(jnp.bfloat16)
        upto = jnp.dot(hits, upper, preferred_element_type=jnp.float32)
        rank = jnp.sum(jnp.where(hit, upto + carry, 0.0), axis=0, keepdims=True)
        rank = rank.astype(jnp.int32) - 1
        carry = carry + upto[:, step - 1 : step]
        turn = (y + PLANES - rank // part) % PLANES
        place = jnp.where(turn < 2, turn, 5 - turn)
        pos_ref[:, c * step : (c + 1) * step] = (
            place // 2 * half + ids // 2 * (4 * part) + place % 2 * (2 * part) + ids % 2 * part + rank % part
        )
        row = lane + c * step
        chosen = (slot_no == rank).astype(jnp.bfloat16)
        row_high = (row // 64).astype(jnp.float32)
        row_low = (row % 64).astype(jnp.float32)
        high += lax.dot_general(
            jnp.where(hit, row_high, 0.0).astype(jnp.bfloat16), chosen, nt, preferred_element_type=jnp.float32
        )
        low += lax.dot_general(
            jnp.where(hit, row_low, 0.0).astype(jnp.bfloat16), chosen, nt, preferred_element_type=jnp.float32
        )
    inv_ref[...] = high.astype(jnp.int32) * 64 + low.astype(jnp.int32)


def pack_kernel(inv_ref, x_ref, out_ref, rows, packed):
    count = x_ref.shape[0]
    lanes = 128
    step = 256

    @pl.loop(0, count // step)
    def _(c):
        at = pl.ds(pl.multiple_of(c * step, step), step)
        v = x_ref[at, :].astype(jnp.float32)
        v = v * lax.rsqrt(jnp.mean(v * v, axis=-1, keepdims=True) + norm_epsilon)
        rows[at, 0, :] = v[:, :lanes]
        rows[at, 1, :] = v[:, lanes:]

    blocks, part = inv_ref.shape

    @pl.loop(0, blocks)
    def _(b):
        for r in range(part):
            packed[b * part + r] = rows[inv_ref[b, r]]

    @pl.loop(0, blocks * part // step)
    def _(c):
        at = pl.ds(pl.multiple_of(c * step, step), step)
        out_ref[at, :lanes] = packed[at, 0, :].astype(jnp.bfloat16)
        out_ref[at, lanes:] = packed[at, 1, :].astype(jnp.bfloat16)


def tiles_kernel(asked_ref, tiles_ref, out_ref, sem):
    dests, slots = asked_ref.shape
    for d in range(dests):
        for s in range(slots):
            pltpu.make_async_copy(tiles_ref.at[asked_ref[d, s]], out_ref.at[d, s], sem).start()
    pltpu.make_async_copy(out_ref, out_ref, sem).wait()


def similar_kernel(scale, q_ref, k0_ref, k1_ref, k3_ref, k2a_ref, k2b_ref, out_ref, total_ref):
    block = pl.program_id(0)
    sources, part, width = q_ref.shape
    q = q_ref[...].reshape(sources * part, width)
    keys = k0_ref.shape[0]
    nt = (((1,), (1,)), ((), ()))
    total = jnp.zeros((sources * part, 1), jnp.float32)
    k2 = jnp.where(block == 0, k2a_ref[...], k2b_ref[...])
    for at, k in enumerate((k0_ref[...], k1_ref[...], k2, k3_ref[...])):
        s = lax.dot_general(q, k, nt, preferred_element_type=jnp.float32)
        e = jnp.exp2(s * scale)
        total = total + jnp.sum(e, axis=1, keepdims=True)
        out_ref[0, :, at * keys : (at + 1) * keys] = e.astype(jnp.bfloat16)
    total_ref[0] = jnp.broadcast_to(1.0 / total, total_ref.shape[1:])


def weigh_kernel(y_ref, slot_ref, ka_ref, kb_ref, ta_ref, tb_ref, got_ref, out_ref, values):
    block = pl.program_id(0)
    y = y_ref[0]
    tiles = slot_ref.shape[1]
    part = TILE // PLANES
    for turn in range(PLANES):
        row = pl.multiple_of((y + PLANES - turn) % PLANES * part, part)
        for j in range(tiles):
            at = (turn * tiles + j) * part
            values[at : at + part, :] = got_ref[slot_ref[block, j], pl.ds(row, part), :]
    sources = out_ref.shape[0]
    for p, (k_ref, t_ref) in enumerate(((ka_ref, ta_ref), (kb_ref, tb_ref))):
        w = jnp.dot(k_ref[0], values[...], preferred_element_type=jnp.float32)
        w = (w * t_ref[0][:, :1]).astype(jnp.bfloat16).reshape(sources, part, w.shape[1])
        at = pl.multiple_of((2 * p + block) * part, part)
        out_ref[:, pl.ds(at, part), :] = w


def unpack_kernel(pos_ref, a_ref, b_ref, out_ref, table, rows):
    lanes = 128
    step = 256
    half = a_ref.shape[0]
    for n, ref in enumerate((a_ref, b_ref)):

        @pl.loop(0, half // step)
        def _(c):
            at = pl.ds(pl.multiple_of(c * step, step), step)
            to = pl.ds(pl.multiple_of(c * step + n * half, step), step)
            v = ref[at, :].astype(jnp.float32)
            table[to, 0, :] = v[:, :lanes]
            table[to, 1, :] = v[:, lanes:]

    count = out_ref.shape[0]

    @pl.loop(0, count // 32)
    def _(c):
        for r in range(32):
            i = c * 32 + r
            rows[i] = table[pos_ref[0, i]]

    @pl.loop(0, count // step)
    def _(c):
        at = pl.ds(pl.multiple_of(c * step, step), step)
        out_ref[at, :lanes] = rows[at, 0, :].astype(jnp.bfloat16)
        out_ref[at, lanes:] = rows[at, 1, :].astype(jnp.bfloat16)


def shards(queries, cluster, anchor_latent, anchor_labels, tile_list):
    dp_count = lax.axis_size("dp")
    y = lax.axis_index("label").astype(jnp.int32)
    y1 = y.reshape(1)
    query_count, width = queries.shape
    blocks_here, tiles_each = tile_list.shape
    blocks = blocks_here * dp_count
    capacity = 2 * query_count // blocks
    part = capacity // PLANES
    tiles_here = anchor_latent.shape[0] // TILE
    tile_part = TILE // PLANES
    columns = anchor_labels.shape[1]
    wanted_count = blocks_here * tiles_each
    slots = 2
    half = dp_count * blocks_here * capacity // 2

    wanted = tile_list.reshape(wanted_count)
    source = wanted // tiles_here
    number = jnp.arange(wanted_count, dtype=jnp.int32)
    order = jnp.sum(
        ((source[:, None] == source[None, :]) & (number[None, :] < number[:, None])).astype(jnp.int32), axis=1
    )
    slot_of = source * slots + order
    asking = jnp.sum(
        jnp.where(
            slot_of[None, :] == jnp.arange(dp_count * slots, dtype=jnp.int32)[:, None], (wanted % tiles_here)[None, :], 0
        ),
        axis=1,
    ).reshape(dp_count, slots)
    asked = lax.all_to_all(asking, "dp", split_axis=0, concat_axis=0, tiled=True)
    slot_table = slot_of.reshape(blocks_here, tiles_each)

    inv, pos = pl.pallas_call(
        functools.partial(rank_kernel, blocks, part, half),
        in_specs=[SMEM, VMEM],
        out_specs=[VMEM, VMEM],
        out_shape=[
            jax.ShapeDtypeStruct((blocks, part), jnp.int32),
            jax.ShapeDtypeStruct((1, query_count), jnp.int32),
        ],
        compiler_params=params(),
        name="rank",
    )(y1, cluster.reshape(1, query_count))
    packed = pl.pallas_call(
        pack_kernel,
        in_specs=[SMEM, VMEM],
        out_specs=VMEM,
        out_shape=jax.ShapeDtypeStruct((blocks * part, width), jnp.bfloat16),
        scratch_shapes=[
            pltpu.VMEM((query_count, 2, 128), jnp.float32),
            pltpu.VMEM((blocks * part, 2, 128), jnp.float32),
        ],
        compiler_params=params(),
        name="pack",
    )(inv, queries)

    quarter = lax.dynamic_slice_in_dim(anchor_latent.reshape(tiles_here, TILE, width), y * tile_part, tile_part, axis=1)
    latent_out = unit_rows(quarter)[asked].reshape(dp_count, slots * tile_part, width)
    sent = jnp.concatenate([packed.reshape(dp_count, blocks_here * part, width), latent_out], axis=1)
    arrived = lax.all_to_all(sent, "dp", split_axis=0, concat_axis=0, tiled=True)

    label_out = pl.pallas_call(
        tiles_kernel,
        in_specs=[SMEM, VMEM],
        out_specs=ANY,
        out_shape=jax.ShapeDtypeStruct((dp_count, slots, TILE, columns), jnp.bfloat16),
        scratch_shapes=[pltpu.SemaphoreType.DMA],
        compiler_params=params(),
        name="label_tiles",
    )(asked, anchor_labels.reshape(tiles_here, TILE, columns))
    got_labels = lax.all_to_all(label_out, "dp", split_axis=0, concat_axis=0, tiled=True)
    got_labels = got_labels.reshape(dp_count * slots, TILE, columns)

    def shift(v, by):
        return lax.ppermute(v, "label", [(i, (i + by) % PLANES) for i in range(PLANES)])

    k0 = arrived[:, blocks_here * part :].reshape(dp_count * slots, tile_part, width)[slot_of]
    k1, k3 = shift(k0, 1), shift(k0, 3)
    k2a, k2b = shift(k1[:tiles_each], 1), shift(k3[tiles_each:], 3)
    q0 = arrived[:, : blocks_here * part]
    q1, q3 = shift(q0, 1), shift(q0, 3)
    mid = dp_count // 2
    q2 = jnp.concatenate([shift(q1[:mid], 1), shift(q3[mid:], 3)], axis=0)

    rows = dp_count * part
    keys = tiles_each * tile_part

    def similar(q):
        flat = blocks_here * keys
        return pl.pallas_call(
            functools.partial(similar_kernel, LOG2E / (width * kernel_width)),
            grid=(blocks_here,),
            in_specs=[pl.BlockSpec((dp_count, part, width), lambda b: (0, b, 0))]
            + [pl.BlockSpec((keys, width), lambda b: (b, 0))] * 3
            + [pl.BlockSpec((keys, width), lambda b: (0, 0))] * 2,
            out_specs=[
                pl.BlockSpec((1, rows, PLANES * keys), lambda b: (b, 0, 0)),
                pl.BlockSpec((1, rows, 128), lambda b: (b, 0, 0)),
            ],
            out_shape=[
                jax.ShapeDtypeStruct((blocks_here, rows, PLANES * keys), jnp.bfloat16),
                jax.ShapeDtypeStruct((blocks_here, rows, 128), jnp.float32),
            ],
            compiler_params=params(),
            cost_estimate=pl.CostEstimate(
                flops=2 * blocks_here * rows * PLANES * keys * width,
                transcendentals=blocks_here * rows * PLANES * keys,
                bytes_accessed=2 * blocks_here * rows * PLANES * keys,
            ),
            name="similar",
        )(q, k0.reshape(flat, width), k1.reshape(flat, width), k3.reshape(flat, width),
          k2a.reshape(keys, width), k2b.reshape(keys, width))

    def weigh(a, b):
        big = pl.BlockSpec((1, rows, PLANES * keys), lambda n: (n, 0, 0))
        tot = pl.BlockSpec((1, rows, 128), lambda n: (n, 0, 0))
        return pl.pallas_call(
            weigh_kernel,
            grid=(blocks_here,),
            in_specs=[SMEM, SMEM, big, big, tot, tot, VMEM],
            out_specs=pl.BlockSpec((dp_count, 2 * blocks_here * part, columns), lambda n: (0, 0, 0)),
            out_shape=jax.ShapeDtypeStruct((dp_count, 2 * blocks_here * part, columns), jnp.bfloat16),
            scratch_shapes=[pltpu.VMEM((tiles_each * TILE, columns), jnp.bfloat16)],
            compiler_params=params(),
            cost_estimate=pl.CostEstimate(
                flops=4 * blocks_here * rows * PLANES * keys * columns,
                transcendentals=0,
                bytes_accessed=4 * blocks_here * rows * PLANES * keys,
            ),
            name="weigh",
        )(y1, slot_table, a[0], b[0], a[1], b[1], got_labels)

    s0, s1, s3, s2 = similar(q0), similar(q1), similar(q3), similar(q2)
    back0 = lax.all_to_all(weigh(s0, s1), "dp", split_axis=0, concat_axis=0, tiled=True)
    back1 = lax.all_to_all(weigh(s3, s2), "dp", split_axis=0, concat_axis=0, tiled=True)
    return pl.pallas_call(
        unpack_kernel,
        in_specs=[SMEM, VMEM, VMEM],
        out_specs=VMEM,
        out_shape=jax.ShapeDtypeStruct((query_count, columns), jnp.bfloat16),
        scratch_shapes=[
            pltpu.VMEM((2 * half, 2, 128), jnp.float32),
            pltpu.VMEM((query_count, 2, 128), jnp.float32),
        ],
        compiler_params=params(),
        name="unpack",
    )(pos, back0.reshape(half, columns), back1.reshape(half, columns))


def solution(mesh):
    placed = (P("dp", None), P("dp", None), P("dp", None), P("dp", "label"), P("dp", None))
    return jax.shard_map(
        shards, mesh=mesh, in_specs=placed, out_specs=P("dp", "label"), check_vma=False
    )
```

time: 435 us -> 246 us (0.57)
  local copies, waits for them, and re-layouts: 105 us -> 9.64 us
  Pallas kernels: 0 us -> 89.9 us
  waiting for transfers between devices: 134 us -> 64.2 us
  other arithmetic: 66.4 us -> 5.95 us
  matrix products: 37.3 us -> 0 us
  blocking collectives: 57.6 us -> 34 us
  starting transfers between devices: 31 us -> 40.7 us
    pallas_call x0 -> x10, Pallas kernels: none -> 89.9 us  [the longest x2 27 us: weigh(): pl.pallas_call(weigh_kernel, grid=(blocks_here,), in_specs=[SMEM, SMEM, b...]
    gather x5 -> x2, local copies, waits for them, and re-layouts: 84.7 us -> 1.19 us  [the longest x1 0.61 us: shards(): unit_rows(quarter)[asked].reshape(dp_count, slots * tile_part, width)]
    all_to_all x2, waiting for transfers between devices: 92.7 us -> 25.7 us  [the longest x1 24 us: shards(): lax.all_to_all(sent, 'dp', split_axis=0, concat_axis=0, tiled=True)]
    all_to_all x1, waiting for transfers between devices: 41.4 us -> 0.01 us  [shards(): lax.all_to_all(label_out, 'dp', split_axis=0, concat_axis=0, tiled=True)]
    ppermute x0 -> x8, waiting for transfers between devices: none -> 38.6 us  [shift(): lax.ppermute(v, 'label', [(i, (i + by) % PLANES) for i in range(PLANES)])]
    dot_general x16 -> x0, matrix products: 37.3 us -> none  [the longest x8 20.3 us: transfer_block(): jnp.einsum('rl,al->ra', row_block, latent_keys, preferred_element_type=jn...]
    another operation x3 -> x0, other arithmetic: 32.6 us -> none
    all_to_all x1, blocking collectives: 57.6 us -> 34 us  [shards(): lax.all_to_all(weigh(s0, s1), 'dp', split_axis=0, concat_axis=0, tiled=True)]
  transfers between devices with their start and end apart: 4 -> 12, of which waited for: 3 -> 5; matrix products, arithmetic and copies ran while one was open for 20% -> 4% of each run, Pallas kernels for 0% -> 24%
where the time goes in v1:
time: 246 us; the launch traced here: 245 us
  Pallas kernels  89.9 us (37%)
  waiting for transfers between devices  64.2 us (26%)
  starting transfers between devices  40.7 us (17%)
  blocking collectives  34 us (14%)
  local copies, waits for them, and re-layouts  9.64 us (4%)
  other arithmetic  5.95 us (2%)
    ppermute x8, waiting for transfers between devices, shift(): lax.ppermute(v, 'label', [(i, (i + by) % PLANES) for i in range(PLANES)])  38.6 us
    all_to_all x1, blocking collectives, shards(): lax.all_to_all(weigh(s0, s1), 'dp', split_axis=0, concat_axis=0, tiled=True)  34 us
    pallas_call x2, Pallas kernels, weigh(): pl.pallas_call(weigh_kernel, grid=(blocks_here,), in_specs=[SMEM, SMEM, b...  27 us
    pallas_call x4, Pallas kernels, similar(): pl.pallas_call(functools.partial(similar_kernel, LOG2E / (width * kernel_...  26.3 us
    all_to_all x1, waiting for transfers between devices, shards(): lax.all_to_all(sent, 'dp', split_axis=0, concat_axis=0, tiled=True)  24 us
    pallas_call x1, Pallas kernels, shards(): pl.pallas_call(unpack_kernel, in_specs=[SMEM, VMEM, VMEM], out_specs=VMEM...  17.5 us
    pallas_call x1, Pallas kernels, shards(): pl.pallas_call(pack_kernel, in_specs=[SMEM, VMEM], out_specs=VMEM, out_sh...  11.1 us
    ppermute x8, starting transfers between devices, shift(): lax.ppermute(v, 'label', [(i, (i + by) % PLANES) for i in range(PLANES)])  10.3 us
  transfers between devices with their start and end apart: 12, of which 5 were waited for; matrix products, arithmetic and copies ran while one was open for 4% of the time, Pallas kernels for 24%

profile of v1, /device:TPU:1, one launch (start us, length us, event | category | flops | bytes accessed | tf_op | source)
XLA Modules:
  0.0 244.7 jit_solution(23766856457337723)
XLA Ops:
  0.0 0.8 reshape.269
  0.8 0.2 convert_reduce_fusion
  1.0 0.1 select_reduce_fusion
  1.1 0.7 all_to_all.21
  1.8 9.4 %all-to-all-start = ((s32[32,1,2]{2,1,0:T(1,128)}), s32[32,1,2]{2,1,0:T(1,128)S(1)}, u32[]{:S(2)}, u32[]{:S(2)}) async-start(s32[32,1,2]{2,1,0:T(1,128)} %bitcast.4), calls=%async_computation | async-start | bytes 32768 | tf_op jit(solution)/shard_map/all_to_all | solution.py:197
  11.2 1.3 fusion
  12.5 1.3 fusion.1
  13.8 4.4 %rank.1 = (s32[64,32]{1,0:T(8,128)}, s32[1,4096]{1,0:T(1,128)}) custom-call(s32[1]{0:T(128)} %bitcast.y_ref, s32[1,4096]{1,0:T(1,128)} %bitcast.47), custom_call_target="tpu_custom_call" | custom-call | tf_op jit(solution)/shard_map/rank/pallas_call | solution.py:200
  18.1 11.1 %pack.1 = bf16[2048,256]{1,0:T(8,128)(2,1)} custom-call(s32[64,32]{1,0:T(8,128)} %get-tuple-element.16.inv_ref, bf16[4096,256]{1,0:T(8,128)(2,1)} %x_ref.1), custom_call_target="tpu_custom_call" | custom-call | tf_op jit(solution)/shard_map/pack/pallas_call | solution.py:211
  29.2 0.0 all-to-all-done
  29.2 0.1 copy.20
  29.3 0.1 copy.21
  29.4 0.1 reshape.286
  29.5 0.6 gather_fusion
  30.1 0.3 copy-done.1
  30.4 1.5 pad_maximum_fusion
  31.9 7.4 %all-to-all-start.1 = ((bf16[32,128,256]{2,1,0:T(8,128)(2,1)}), bf16[32,128,256]{2,1,0:T(8,128)(2,1)S(1)}, u32[]{:S(2)}, u32[]{:S(2)}) async-start(bf16[32,128,256]{2,1,0:T(8,128)(2,1)} %pad_maximum_fusion), calls=%async_computation.1 | async-start | bytes 4194304 | tf_op jit(solution)/shard_map/all_to_all | solution.py:227
  39.3 0.7 copy.23.asked_ref
  40.0 3.6 %label_tiles.1 = bf16[32,2,128,256]{3,2,1,0:T(8,128)(2,1)} custom-call(s32[32,2]{1,0:T(8,128)} %copy.23.asked_ref, bf16[32,128,256]{2,1,0:T(8,128)(2,1)} %bitcast.32), custom_call_target="tpu_custom_call" | custom-call | tf_op jit(solution)/shard_map/label_tiles/pallas_call | solution.py:229
  43.6 24.0 %all-to-all-done.1 = bf16[32,128,256]{2,1,0:T(8,128)(2,1)S(1)} async-done(((bf16[32,128,256]{2,1,0:T(8,128)(2,1)}), bf16[32,128,256]{2,1,0:T(8,128)(2,1)S(1)}, u32[]{:S(2)}, u32[]{:S(2)}) %all-to-all-start.1) | async-done | bytes 2097184 | tf_op jit(solution)/shard_map/all_to_all | solution.py:227
  67.6 5.3 %all-to-all-start.2 = ((bf16[32,2,128,256]{3,2,1,0:T(8,128)(2,1)}), bf16[32,2,128,256]{3,2,1,0:T(8,128)(2,1)}, u32[]{:S(2)}, u32[]{:S(2)}) async-start(bf16[32,2,128,256]{3,2,1,0:T(8,128)(2,1)} %label_tiles.1), calls=%async_computation.2 | async-start | bytes 8388608 | tf_op jit(solution)/shard_map/all_to_all | solution.py:238
  72.9 0.0 copy-start.5
  72.9 1.2 fusion.4
  74.1 1.3 collective-permute-start.4
  75.4 1.4 collective-permute-start.5
  76.8 0.0 copy-done.5
  76.8 0.1 reshape.274
  76.9 0.6 gather_fusion.1
  77.5 0.0 copy-start.2
  77.5 0.1 collective-permute-start
  77.6 2.7 %collective-permute-start.1 = (bf16[32,32,256]{2,1,0:T(8,128)(2,1)S(1)}, bf16[32,32,256]{2,1,0:T(8,128)(2,1)S(1)}, u32[]{:S(2)}, u32[]{:S(2)}) collective-permute-start(bf16[32,32,256]{2,1,0:T(8,128)(2,1)S(1)} %gather_fusion.1), channel_id=1, source_target_pairs={{0,3},{1,0},{2,1},{3,2},{4,7},{5,4},{6,5},{7,6},{8,11},{9,8},{10,9... | collective-permute-start | bytes 1572872 | tf_op jit(solution)/shard_map/ppermute | solution.py:242
  80.3 19.7 %collective-permute-done.4.q_ref = bf16[32,64,256]{2,1,0:T(8,128)(2,1)} collective-permute-done((bf16[32,64,256]{2,1,0:T(8,128)(2,1)}, bf16[32,64,256]{2,1,0:T(8,128)(2,1)}, u32[]{:S(2)}, u32[]{:S(2)}) %collective-permute-start.4) | collective-permute-done | bytes 1048608 | tf_op jit(solution)/shard_map/ppermute | solution.py:242
  100.0 1.1 slice.32
  101.1 0.1 collective-permute-start.6
  101.2 0.0 collective-permute-done.5.q_ref
  101.2 1.1 slice.33
  102.3 2.7 %collective-permute-start.7 = (bf16[16,64,256]{2,1,0:T(8,128)(2,1)S(1)}, bf16[16,64,256]{2,1,0:T(8,128)(2,1)S(1)}, u32[]{:S(2)}, u32[]{:S(2)}) collective-permute-start(bf16[16,64,256]{2,1,0:T(8,128)(2,1)S(1)} %slice.33), channel_id=1, source_target_pairs={{0,3},{1,0},{2,1},{3,2},{4,7},{5,4},{6,5},{7,6},{8,11},{9,8},{10,9... | collective-permute-start | bytes 1572872 | tf_op jit(solution)/shard_map/ppermute | solution.py:242
  105.0 6.3 %collective-permute-done = bf16[32,32,256]{2,1,0:T(8,128)(2,1)S(1)} collective-permute-done((bf16[32,32,256]{2,1,0:T(8,128)(2,1)S(1)}, bf16[32,32,256]{2,1,0:T(8,128)(2,1)S(1)}, u32[]{:S(2)}, u32[]{:S(2)}) %collective-permute-start) | collective-permute-done | bytes 524320 | tf_op jit(solution)/shard_map/ppermute | solution.py:242
  111.3 0.1 collective-permute-start.2
  111.4 0.0 collective-permute-done.1
  111.4 0.7 copy-done.3
  112.1 0.8 copy-done.4
  112.9 2.0 collective-permute-start.3
  114.8 0.1 reduce_sum.32
  114.9 0.5 multiply_add_fusion.slot_ref
  115.5 12.5 %collective-permute-done.2 = bf16[16,32,256]{2,1,0:T(8,128)(2,1)S(1)} collective-permute-done((bf16[16,32,256]{2,1,0:T(8,128)(2,1)S(1)}, bf16[16,32,256]{2,1,0:T(8,128)(2,1)S(1)}, u32[]{:S(2)}, u32[]{:S(2)}) %collective-permute-start.2) | collective-permute-done | bytes 262176 | tf_op jit(solution)/shard_map/ppermute | solution.py:242
  128.0 0.0 collective-permute-done.3
  128.0 0.0 copy-done.2
  128.0 0.7 copy-done.6
  128.7 6.6 %similar.6 = (bf16[2,1024,2048]{2,1,0:T(8,128)(2,1)}, f32[2,1024,128]{2,1,0:T(8,128)}) custom-call(bf16[32,64,256]{2,1,0:T(8,128)(2,1)} %collective-permute-done.5.q_ref, bf16[1024,256]{1,0:T(8,128)(2,1)} %bitcast.35, bf16[1024,256]{1,0:T(8,128)(2,1)} %bitcast.39, bf16[1024,256]{1,0:T(8,128)(2,1)} %bitcast.43, bf16[512,256]{1,0:T(8,128)(2,1)} %bitcast.49, ...), custom_call_target="tpu_custom_call" | custom-call | flops 2147483648 | bytes 8388608 | tf_op jit(solution)/shard_map/similar/pallas_call | solution.py:257
  135.3 0.0 collective-permute-done.6
  135.3 0.0 collective-permute-done.7
  135.3 1.1 pad_maximum_fusion.1.q_ref
  136.4 6.5 %similar.7 = (bf16[2,1024,2048]{2,1,0:T(8,128)(2,1)}, f32[2,1024,128]{2,1,0:T(8,128)}) custom-call(bf16[32,64,256]{2,1,0:T(8,128)(2,1)} %pad_maximum_fusion.1.q_ref, bf16[1024,256]{1,0:T(8,128)(2,1)} %bitcast.36, bf16[1024,256]{1,0:T(8,128)(2,1)} %bitcast.40, bf16[1024,256]{1,0:T(8,128)(2,1)} %bitcast.44, bf16[512,256]{1,0:T(8,128)(2,1)} %bitcast.50, ...), custom_call_target="tpu_custom_call" | custom-call | flops 2147483648 | bytes 8388608 | tf_op jit(solution)/shard_map/similar/pallas_call | solution.py:257
  143.0 0.0 all-to-all-done.2
  143.0 13.5 %weigh.3 = bf16[32,128,256]{2,1,0:T(8,128)(2,1)} custom-call(s32[1]{0:T(128)} %bitcast.y_ref, s32[2,16]{1,0:T(2,128)} %multiply_add_fusion.slot_ref, bf16[2,1024,2048]{2,1,0:T(8,128)(2,1)} %get-tuple-element.21.ka_ref, bf16[2,1024,2048]{2,1,0:T(8,128)(2,1)} %get-tuple-element.22.kb_ref, f32[2,1024,128]{2,1,0:T(8,128)} %get-tuple-element.23.ta_ref, ...), custom_call_target="tpu_custom_call" | custom-call | flops 4294967296 | bytes 16777216 | tf_op jit(solution)/shard_map/weigh/pallas_call | solution.py:284
  156.5 8.3 %all-to-all-start.4 = ((bf16[32,128,256]{2,1,0:T(8,128)(2,1)}), bf16[32,128,256]{2,1,0:T(8,128)(2,1)S(1)}, u32[]{:S(2)}, u32[]{:S(2)}) async-start(bf16[32,128,256]{2,1,0:T(8,128)(2,1)} %weigh.3), calls=%async_computation.4 | async-start | bytes 4194304 | tf_op jit(solution)/shard_map/all_to_all | solution.py:302
  164.8 6.6 %similar.4 = (bf16[2,1024,2048]{2,1,0:T(8,128)(2,1)}, f32[2,1024,128]{2,1,0:T(8,128)}) custom-call(bf16[32,64,256]{2,1,0:T(8,128)(2,1)} %get-tuple-element.26.q_ref, bf16[1024,256]{1,0:T(8,128)(2,1)} %bitcast.37, bf16[1024,256]{1,0:T(8,128)(2,1)} %bitcast.41, bf16[1024,256]{1,0:T(8,128)(2,1)} %bitcast.45, bf16[512,256]{1,0:T(8,128)(2,1)} %bitcast.51, ...), custom_call_target="tpu_custom_call" | custom-call | flops 2147483648 | bytes 8388608 | tf_op jit(solution)/shard_map/similar/pallas_call | solution.py:257
  171.5 6.6 %similar.5 = (bf16[2,1024,2048]{2,1,0:T(8,128)(2,1)}, f32[2,1024,128]{2,1,0:T(8,128)}) custom-call(bf16[32,64,256]{2,1,0:T(8,128)(2,1)} %collective-permute-done.4.q_ref, bf16[1024,256]{1,0:T(8,128)(2,1)} %bitcast.38, bf16[1024,256]{1,0:T(8,128)(2,1)} %bitcast.42, bf16[1024,256]{1,0:T(8,128)(2,1)} %bitcast.46, bf16[512,256]{1,0:T(8,128)(2,1)} %bitcast.52, ...), custom_call_target="tpu_custom_call" | custom-call | flops 2147483648 | bytes 8388608 | tf_op jit(solution)/shard_map/similar/pallas_call | solution.py:257
  178.0 13.5 %weigh.2 = bf16[32,128,256]{2,1,0:T(8,128)(2,1)} custom-call(s32[1]{0:T(128)} %bitcast.y_ref, s32[2,16]{1,0:T(2,128)} %multiply_add_fusion.slot_ref, bf16[2,1024,2048]{2,1,0:T(8,128)(2,1)} %get-tuple-element.17.ka_ref, bf16[2,1024,2048]{2,1,0:T(8,128)(2,1)} %get-tuple-element.18.kb_ref, f32[2,1024,128]{2,1,0:T(8,128)} %get-tuple-element.19.ta_ref, ...), custom_call_target="tpu_custom_call" | custom-call | flops 4294967296 | bytes 16777216 | tf_op jit(solution)/shard_map/weigh/pallas_call | solution.py:284
  191.5 1.6 all-to-all-done.4
  193.2 34.0 %all_to_all.34 = bf16[32,128,256]{2,1,0:T(8,128)(2,1)} all-to-all(bf16[32,128,256]{2,1,0:T(8,128)(2,1)} %weigh.2), channel_id=1, replica_groups=mesh['dp'=32,'label'=4] {'dp'}, dimensions={0} | all-to-all | bytes 4194304 | tf_op jit(solution)/shard_map/all_to_all | solution.py:301
  227.2 0.0 copy-done
  227.2 17.5 %unpack.1 = bf16[4096,256]{1,0:T(8,128)(2,1)} custom-call(s32[1,4096]{1,0:T(1,128)} %get-tuple-element.15.pos_ref, bf16[4096,256]{1,0:T(8,128)(2,1)} %bitcast.28, bf16[4096,256]{1,0:T(8,128)(2,1)} %bitcast.27), custom_call_target="tpu_custom_call" | custom-call | tf_op jit(solution)/shard_map/unpack/pallas_call | solution.py:303
  (14 shorter events, 0.1 us)
Async XLA Ops:
  1.8 27.4 %all-to-all-start = ((s32[32,1,2]{2,1,0:T(1,128)}), s32[32,1,2]{2,1,0:T(1,128)S(1)}, u32[]{:S(2)}, u32[]{:S(2)}) async-start(s32[32,1,2]{2,1,0:T(1,128)} %bitcast.4), calls=%async_computation | async-start | bytes 32768 | tf_op jit(solution)/shard_map/all_to_all | solution.py:197
  29.2 1.2 copy-start.1
  31.9 35.7 %all-to-all-start.1 = ((bf16[32,128,256]{2,1,0:T(8,128)(2,1)}), bf16[32,128,256]{2,1,0:T(8,128)(2,1)S(1)}, u32[]{:S(2)}, u32[]{:S(2)}) async-start(bf16[32,128,256]{2,1,0:T(8,128)(2,1)} %pad_maximum_fusion), calls=%async_computation.1 | async-start | bytes 4194304 | tf_op jit(solution)/shard_map/all_to_all | solution.py:227
  67.6 75.3 %all-to-all-start.2 = ((bf16[32,2,128,256]{3,2,1,0:T(8,128)(2,1)}), bf16[32,2,128,256]{3,2,1,0:T(8,128)(2,1)}, u32[]{:S(2)}, u32[]{:S(2)}) async-start(bf16[32,2,128,256]{3,2,1,0:T(8,128)(2,1)} %label_tiles.1), calls=%async_computation.2 | async-start | bytes 8388608 | tf_op jit(solution)/shard_map/all_to_all | solution.py:238
  72.9 3.9 %copy-start.5 = (s32[2,16]{1,0:T(2,128)S(1)}, s32[2,16]{1,0:T(2,128)}, u32[]{:S(2)}) copy-start(s32[2,16]{1,0:T(2,128)} %param.9) | copy-start | bytes 388
  74.1 25.9 %collective-permute-start.4 = (bf16[32,64,256]{2,1,0:T(8,128)(2,1)}, bf16[32,64,256]{2,1,0:T(8,128)(2,1)}, u32[]{:S(2)}, u32[]{:S(2)}) collective-permute-start(bf16[32,64,256]{2,1,0:T(8,128)(2,1)} %get-tuple-element.26.q_ref), channel_id=1, source_target_pairs={{0,1},{1,2},{2,3},{3,0},{4,5},{5,6},{6,7},{7,4},{8,9},{9,10},{10,1... | collective-permute-start | bytes 3145736 | tf_op jit(solution)/shard_map/ppermute | solution.py:242
  75.4 25.8 %collective-permute-start.5 = (bf16[32,64,256]{2,1,0:T(8,128)(2,1)}, bf16[32,64,256]{2,1,0:T(8,128)(2,1)}, u32[]{:S(2)}, u32[]{:S(2)}) collective-permute-start(bf16[32,64,256]{2,1,0:T(8,128)(2,1)} %get-tuple-element.26.q_ref), channel_id=1, source_target_pairs={{0,3},{1,0},{2,1},{3,2},{4,7},{5,4},{6,5},{7,6},{8,11},{9,8},{10,9... | collective-permute-start | bytes 3145736 | tf_op jit(solution)/shard_map/ppermute | solution.py:242
  77.5 50.5 %copy-start.2 = (bf16[32,32,256]{2,1,0:T(8,128)(2,1)}, bf16[32,32,256]{2,1,0:T(8,128)(2,1)S(1)}, u32[]{:S(2)}) copy-start(bf16[32,32,256]{2,1,0:T(8,128)(2,1)S(1)} %gather_fusion.1) | copy-start | bytes 1572868
  77.5 33.7 %collective-permute-start = (bf16[32,32,256]{2,1,0:T(8,128)(2,1)S(1)}, bf16[32,32,256]{2,1,0:T(8,128)(2,1)S(1)}, u32[]{:S(2)}, u32[]{:S(2)}) collective-permute-start(bf16[32,32,256]{2,1,0:T(8,128)(2,1)S(1)} %gather_fusion.1), channel_id=1, source_target_pairs={{0,1},{1,2},{2,3},{3,0},{4,5},{5,6},{6,7},{7,4},{8,9},{9,10},{10,1... | collective-permute-start | bytes 1572872 | tf_op jit(solution)/shard_map/ppermute | solution.py:242
  77.6 33.7 %collective-permute-start.1 = (bf16[32,32,256]{2,1,0:T(8,128)(2,1)S(1)}, bf16[32,32,256]{2,1,0:T(8,128)(2,1)S(1)}, u32[]{:S(2)}, u32[]{:S(2)}) collective-permute-start(bf16[32,32,256]{2,1,0:T(8,128)(2,1)S(1)} %gather_fusion.1), channel_id=1, source_target_pairs={{0,3},{1,0},{2,1},{3,2},{4,7},{5,4},{6,5},{7,6},{8,11},{9,8},{10,9... | collective-permute-start | bytes 1572872 | tf_op jit(solution)/shard_map/ppermute | solution.py:242
  101.1 34.2 %collective-permute-start.6 = (bf16[16,64,256]{2,1,0:T(8,128)(2,1)S(1)}, bf16[16,64,256]{2,1,0:T(8,128)(2,1)S(1)}, u32[]{:S(2)}, u32[]{:S(2)}) collective-permute-start(bf16[16,64,256]{2,1,0:T(8,128)(2,1)S(1)} %slice.32), channel_id=1, source_target_pairs={{0,1},{1,2},{2,3},{3,0},{4,5},{5,6},{6,7},{7,4},{8,9},{9,10},{10,1... | collective-permute-start | bytes 1572872 | tf_op jit(solution)/shard_map/ppermute | solution.py:242
  102.3 33.1 %collective-permute-start.7 = (bf16[16,64,256]{2,1,0:T(8,128)(2,1)S(1)}, bf16[16,64,256]{2,1,0:T(8,128)(2,1)S(1)}, u32[]{:S(2)}, u32[]{:S(2)}) collective-permute-start(bf16[16,64,256]{2,1,0:T(8,128)(2,1)S(1)} %slice.33), channel_id=1, source_target_pairs={{0,3},{1,0},{2,1},{3,2},{4,7},{5,4},{6,5},{7,6},{8,11},{9,8},{10,9... | collective-permute-start | bytes 1572872 | tf_op jit(solution)/shard_map/ppermute | solution.py:242
  111.2 0.8 copy-start.3
  111.3 16.7 %collective-permute-start.2 = (bf16[16,32,256]{2,1,0:T(8,128)(2,1)S(1)}, bf16[16,32,256]{2,1,0:T(8,128)(2,1)S(1)}, u32[]{:S(2)}, u32[]{:S(2)}) collective-permute-start(bf16[16,32,256]{2,1,0:T(8,128)(2,1)S(1)} %slice.30), channel_id=1, source_target_pairs={{0,1},{1,2},{2,3},{3,0},{4,5},{5,6},{6,7},{7,4},{8,9},{9,10},{10,1... | collective-permute-start | bytes 786440 | tf_op jit(solution)/shard_map/ppermute | solution.py:242
  112.1 0.8 copy-start.4
  112.9 15.1 %collective-permute-start.3 = (bf16[16,32,256]{2,1,0:T(8,128)(2,1)S(1)}, bf16[16,32,256]{2,1,0:T(8,128)(2,1)}, u32[]{:S(2)}, u32[]{:S(2)}) collective-permute-start(bf16[16,32,256]{2,1,0:T(8,128)(2,1)S(1)} %slice.31), channel_id=1, source_target_pairs={{0,3},{1,0},{2,1},{3,2},{4,7},{5,4},{6,5},{7,6},{8,11},{9,8},{10,9... | collective-permute-start | bytes 786440 | tf_op jit(solution)/shard_map/ppermute | solution.py:242
  128.0 0.7 copy-start.6
  156.5 36.7 %all-to-all-start.4 = ((bf16[32,128,256]{2,1,0:T(8,128)(2,1)}), bf16[32,128,256]{2,1,0:T(8,128)(2,1)S(1)}, u32[]{:S(2)}, u32[]{:S(2)}) async-start(bf16[32,128,256]{2,1,0:T(8,128)(2,1)} %weigh.3), calls=%async_computation.4 | async-start | bytes 4194304 | tf_op jit(solution)/shard_map/all_to_all | solution.py:302
  193.2 34.0 %copy-start = (bf16[32,128,256]{2,1,0:T(8,128)(2,1)}, bf16[32,128,256]{2,1,0:T(8,128)(2,1)S(1)}, u32[]{:S(2)}) copy-start(bf16[32,128,256]{2,1,0:T(8,128)(2,1)S(1)} %all-to-all-done.4) | copy-start | bytes 6291460

commit v2 on v1

v2 whole, which is shorter than its diff:
```python
import functools
import jax
import jax.numpy as jnp
from jax import lax
from jax.sharding import PartitionSpec as P
from jax.experimental import pallas as pl
from jax.experimental.pallas import tpu as pltpu

TILE = 128
kernel_width = 0.025
norm_epsilon = 1e-05
PLANES = 4
LOG2E = 1.4426950408889634
VMEM = pl.BlockSpec(memory_space=pltpu.VMEM)
ANY = pl.BlockSpec(memory_space=pl.ANY)
SMEM = pl.BlockSpec(memory_space=pltpu.SMEM)


def unit_rows(values):
    widened = values.astype(jnp.float32)
    scaled = widened * lax.rsqrt(jnp.mean(widened * widened, axis=-1, keepdims=True) + norm_epsilon)
    return scaled.astype(jnp.bfloat16)


def params(mib, **kw):
    return pltpu.CompilerParams(vmem_limit_bytes=mib * 1024 * 1024, **kw)


def pack_kernel(
    blocks, part, tiles_here, y_ref, ids_ref, list_ref, x_ref,
    out_ref, pos_ref, rows, left, right, got_left, got_right, place, inv, row_sem, inv_sem,
):
    load = pltpu.make_async_copy(x_ref, rows, row_sem)
    load.start()
    y = y_ref[0]
    lanes = 128
    own = 2 * part
    wanted = list_ref[...]
    wanted = jnp.concatenate([wanted[n : n + 1] for n in range(wanted.shape[0])], axis=1)
    many = wanted.shape[1]
    across = lax.broadcasted_iota(jnp.int32, (many, many), 1)
    down = lax.broadcasted_iota(jnp.int32, (many, many), 0)
    source = wanted // tiles_here
    upright = jnp.sum(jnp.where(across == down, source.astype(jnp.float32), 0.0), axis=1, keepdims=True)
    same = (upright.astype(jnp.int32) == source) & (down < across)
    order = jnp.sum(same.astype(jnp.float32), axis=0, keepdims=True)
    holders, told_rows = out_ref.shape[0], out_ref.shape[1] - own
    holder = lax.broadcasted_iota(jnp.int32, (holders, many), 0) == source
    number = (wanted % tiles_here).astype(jnp.float32)
    for k in range(2):
        told = jnp.sum(jnp.where(holder & (order == k), number, 0.0), axis=1, keepdims=True)
        told = jnp.broadcast_to(told[:, :, None], (holders, told_rows, lanes))
        out_ref[:, own:, k * lanes : (k + 1) * lanes] = told.astype(jnp.bfloat16)

    count = ids_ref.shape[1]
    step = 256
    upper = (
        lax.broadcasted_iota(jnp.int32, (step, step), 0)
        <= lax.broadcasted_iota(jnp.int32, (step, step), 1)
    ).astype(jnp.bfloat16)
    block_no = lax.broadcasted_iota(jnp.int32, (blocks, step), 0)
    slot_no = lax.broadcasted_iota(jnp.int32, (lanes, step), 0) + part * y
    lane = lax.broadcasted_iota(jnp.int32, (1, step), 1)
    carry = jnp.zeros((blocks, 1), jnp.float32)
    high = jnp.zeros((blocks, lanes), jnp.float32)
    low = jnp.zeros((blocks, lanes), jnp.float32)
    nt = (((1,), (1,)), ((), ()))
    for c in range(count // step):
        ids = ids_ref[:, c * step : (c + 1) * step]
        hit = block_no == ids
        hits = hit.astype(jnp.bfloat16)
        upto = jnp.dot(hits, upper, preferred_element_type=jnp.float32)
        rank = jnp.sum(jnp.where(hit, upto + carry, 0.0), axis=0, keepdims=True)
        rank = rank.astype(jnp.int32) - 1
        carry = carry + upto[:, step - 1 : step]
        turn = (y + PLANES - rank // part) % PLANES
        piece = jnp.where(turn == 1, 0, jnp.where(turn == 3, 1, 2))
        within = ids % 2 * part + rank % part
        first = ids // 2 * (2 * part) + within
        later = blocks * part + ids // 2 * (6 * part) + piece * (2 * part) + within
        pos_ref[:, c * step : (c + 1) * step] = jnp.where(turn == 0, first, later)
        row = lane + c * step
        chosen = (slot_no == rank).astype(jnp.bfloat16)
        row_high = (row // 64).astype(jnp.float32)
        row_low = (row % 64).astype(jnp.float32)
        high += lax.dot_general(
            jnp.where(hit, row_high, 0.0).astype(jnp.bfloat16), chosen, nt, preferred_element_type=jnp.float32
        )
        low += lax.dot_general(
            jnp.where(hit, row_low, 0.0).astype(jnp.bfloat16), chosen, nt, preferred_element_type=jnp.float32
        )
    place[...] = high.astype(jnp.int32) * 64 + low.astype(jnp.int32)
    tell = pltpu.make_async_copy(place, inv, inv_sem)
    tell.start()
    load.wait()

    @pl.loop(0, count // step)
    def _(c):
        at = pl.ds(pl.multiple_of(c * step, step), step)
        left[at, :] = rows[at, :lanes].astype(jnp.float32)
        right[at, :] = rows[at, lanes:].astype(jnp.float32)

    tell.wait()

    @pl.loop(0, blocks)
    def _(b):
        at = pl.multiple_of(b * part, part)
        for r in range(part):
            i = inv[b, r]
            got_left[pl.ds(at + r, 1), :] = left[pl.ds(i, 1), :]
            got_right[pl.ds(at + r, 1), :] = right[pl.ds(i, 1), :]

    width = 2 * lanes
    some = 4

    @pl.loop(0, out_ref.shape[0] // some)
    def _(g):
        at = pl.ds(pl.multiple_of(g * some * own, some * own), some * own)
        a, b = got_left[at, :], got_right[at, :]
        scale = lax.rsqrt(jnp.sum(a * a + b * b, axis=-1, keepdims=True) / width + norm_epsilon)
        to = pl.ds(g * some, some)
        out_ref[to, :own, :lanes] = (a * scale).astype(jnp.bfloat16).reshape(some, own, lanes)
        out_ref[to, :own, lanes:] = (b * scale).astype(jnp.bfloat16).reshape(some, own, lanes)


def first_kernel(asked_ref, latent_ref, label_ref, out_ref, sem):
    dests, slots = asked_ref.shape
    part, rows = latent_ref.shape[1], label_ref.shape[1]
    for d in range(dests):
        for s in range(slots):
            pltpu.make_async_copy(
                latent_ref.at[asked_ref[d, s]], out_ref.at[d, pl.ds(s * part, part)], sem
            ).start()
        pltpu.make_async_copy(
            label_ref.at[asked_ref[d, 0]], out_ref.at[d, pl.ds(slots * part, rows)], sem
        ).start()
    pltpu.make_async_copy(out_ref, out_ref, sem).wait()


def second_kernel(asked_ref, label_ref, out_ref, sem):
    for d in range(asked_ref.shape[0]):
        pltpu.make_async_copy(label_ref.at[asked_ref[d, 1]], out_ref.at[d], sem).start()
    pltpu.make_async_copy(out_ref, out_ref, sem).wait()


def pick_kernel(slot_ref, arrived_ref, out_ref, sem):
    blocks, tiles = slot_ref.shape
    part = out_ref.shape[1]
    for n in range(blocks):
        for j in range(tiles):
            slot = slot_ref[n, j]
            row = pl.multiple_of(slot % 2 * part, part)
            pltpu.make_async_copy(
                arrived_ref.at[slot // 2, pl.ds(row, part)], out_ref.at[n * tiles + j], sem
            ).start()
    pltpu.make_async_copy(out_ref, out_ref, sem).wait()


def answer_kernel(scale, pieces, skip, y_ref, slot_ref, *refs):
    (k0_ref, k1_ref, k3_ref, k2a_ref, k2b_ref, first_ref, second_ref) = refs[-12:-5]
    out_ref, keys, values, key_sem, sems = refs[-5:]
    y = y_ref[0]
    blocks, tiles = slot_ref.shape
    rows = keys.shape[2]
    tile_part = rows // PLANES

    @pl.when((pl.program_id(0) == 0) & (pl.program_id(1) == 0))
    def _():
        for n in range(blocks):
            for turn, ref in enumerate((k0_ref, k1_ref, (k2a_ref, k2b_ref)[n], k3_ref)):
                row = pl.multiple_of((y + PLANES - turn) % PLANES * tile_part, tile_part)
                source = ref if turn == 2 else ref.at[pl.ds(n * tiles, tiles)]
                pltpu.make_async_copy(source, keys.at[n, :, pl.ds(row, tile_part)], key_sem.at[n]).start()
            for j in range(tiles):
                slot = slot_ref[n, j]
                to = values.at[n, pl.ds(j * rows, rows)]

                @pl.when(slot % 2 == 0)
                def _():
                    pltpu.make_async_copy(first_ref.at[slot // 2, pl.ds(skip, rows)], to, sems.at[n]).start()

                @pl.when(slot % 2 == 1)
                def _():
                    pltpu.make_async_copy(second_ref.at[slot // 2], to, sems.at[n]).start()

    block = pl.program_id(1)

    @pl.when(pl.program_id(0) == 0)
    def _():
        pltpu.make_async_copy(keys.at[block], keys.at[block], key_sem.at[block]).wait()

    nt = (((1,), (1,)), ((), ()))
    group = 4
    span = group * rows
    sources = out_ref.shape[0]
    for p in range(pieces):
        if p < 2:
            q = refs[p][...]
        else:
            q = jnp.where(pl.program_id(0) == 0, refs[2][...], refs[3][...])
        part, width = q.shape[1:]
        q = q.reshape(sources * part, width)
        total = jnp.zeros((sources * part, 1), jnp.float32)
        weighted = jnp.zeros((sources * part, values.shape[2]), jnp.float32)
        for at in range(tiles // group):
            k = keys[block, at * group : (at + 1) * group].reshape(span, width)
            s = lax.dot_general(q, k, nt, preferred_element_type=jnp.float32)
            e = jnp.exp2(s * scale)
            total = total + jnp.sum(e, axis=1, keepdims=True)
            if p == 0 and at == 0:

                @pl.when(pl.program_id(0) == 0)
                def _():
                    pltpu.make_async_copy(values.at[block], values.at[block], sems.at[block]).wait()

            weighted = weighted + jnp.dot(
                e.astype(jnp.bfloat16), values[block, at * span : (at + 1) * span], preferred_element_type=jnp.float32
            )
        answer = (weighted / total).astype(jnp.bfloat16).reshape(sources, part, values.shape[2])
        at = pl.multiple_of((2 * p + block) * part, part)
        out_ref[:, pl.ds(at, part), :] = answer


def unpack_kernel(pos_ref, a_ref, b_ref, out_ref, left, right, got_left, got_right):
    lanes = 128
    step = 256
    start = 0
    for ref in (a_ref, b_ref):

        @pl.loop(0, ref.shape[0] // step)
        def _(c):
            at = pl.ds(pl.multiple_of(c * step, step), step)
            to = pl.ds(pl.multiple_of(c * step + start, step), step)
            left[to, :] = ref[at, :lanes].astype(jnp.float32)
            right[to, :] = ref[at, lanes:].astype(jnp.float32)

        start += ref.shape[0]

    count = out_ref.shape[0]

    @pl.loop(0, count // 32)
    def _(c):
        at = pl.multiple_of(c * 32, 32)
        for r in range(32):
            i = pos_ref[0, at + r]
            got_left[pl.ds(at + r, 1), :] = left[pl.ds(i, 1), :]
            got_right[pl.ds(at + r, 1), :] = right[pl.ds(i, 1), :]

    @pl.loop(0, count // step)
    def _(c):
        at = pl.ds(pl.multiple_of(c * step, step), step)
        out_ref[at, :lanes] = got_left[at, :].astype(jnp.bfloat16)
        out_ref[at, lanes:] = got_right[at, :].astype(jnp.bfloat16)


def shards(queries, cluster, anchor_latent, anchor_labels, tile_list):
    dp_count = lax.axis_size("dp")
    y = lax.axis_index("label").astype(jnp.int32)
    y1 = y.reshape(1)
    query_count, width = queries.shape
    blocks_here, tiles_each = tile_list.shape
    blocks = blocks_here * dp_count
    capacity = 2 * query_count // blocks
    part = capacity // PLANES
    tiles_here = anchor_latent.shape[0] // TILE
    tile_part = TILE // PLANES
    columns = anchor_labels.shape[1]
    wanted_count = blocks_here * tiles_each
    slots = 2

    wanted = tile_list.reshape(wanted_count)
    source = wanted // tiles_here
    number = jnp.arange(wanted_count, dtype=jnp.int32)
    order = jnp.sum(
        ((source[:, None] == source[None, :]) & (number[None, :] < number[:, None])).astype(jnp.int32), axis=1
    )
    slot_of = source * slots + order
    slot_table = slot_of.reshape(blocks_here, tiles_each)

    own = blocks_here * part
    sent, pos = pl.pallas_call(
        functools.partial(pack_kernel, blocks, part, tiles_here),
        in_specs=[SMEM, VMEM, VMEM, ANY],
        out_specs=[VMEM, VMEM],
        out_shape=[
            jax.ShapeDtypeStruct((dp_count, own + 8, width), jnp.bfloat16),
            jax.ShapeDtypeStruct((1, query_count), jnp.int32),
        ],
        scratch_shapes=[
            pltpu.VMEM((query_count, width), jnp.bfloat16),
            pltpu.VMEM((query_count, 128), jnp.float32),
            pltpu.VMEM((query_count, 128), jnp.float32),
            pltpu.VMEM((blocks * part, 128), jnp.float32),
            pltpu.VMEM((blocks * part, 128), jnp.float32),
            pltpu.VMEM((blocks, 128), jnp.int32),
            pltpu.SMEM((blocks, 128), jnp.int32),
            pltpu.SemaphoreType.DMA,
            pltpu.SemaphoreType.DMA,
        ],
        compiler_params=params(60),
        name="pack",
    )(y1, cluster.reshape(1, query_count), tile_list, queries)
    arrived = lax.all_to_all(sent, "dp", split_axis=0, concat_axis=0, tiled=True)
    asked = arrived[:, own, :: width // slots].astype(jnp.int32)

    quarter = lax.dynamic_slice_in_dim(anchor_latent.reshape(tiles_here, TILE, width), y * tile_part, tile_part, axis=1)
    label_tiles = anchor_labels.reshape(tiles_here, TILE, columns)
    skip = slots * tile_part
    first_out = pl.pallas_call(
        first_kernel,
        in_specs=[SMEM, VMEM, VMEM],
        out_specs=ANY,
        out_shape=jax.ShapeDtypeStruct((dp_count, skip + TILE, columns), jnp.bfloat16),
        scratch_shapes=[pltpu.SemaphoreType.DMA],
        compiler_params=params(60),
        name="first_tiles",
    )(asked, unit_rows(quarter), label_tiles)
    got_first = lax.all_to_all(first_out, "dp", split_axis=0, concat_axis=0, tiled=True)
    second_out = pl.pallas_call(
        second_kernel,
        in_specs=[SMEM, VMEM],
        out_specs=ANY,
        out_shape=jax.ShapeDtypeStruct((dp_count, TILE, columns), jnp.bfloat16),
        scratch_shapes=[pltpu.SemaphoreType.DMA],
        compiler_params=params(60),
        name="second_tiles",
    )(asked, label_tiles)

    def shift(v, by):
        return lax.ppermute(v, "label", [(i, (i + by) % PLANES) for i in range(PLANES)])

    q0 = arrived[:, :own]
    q1, q3 = shift(q0, 1), shift(q0, 3)
    mid = dp_count // 2
    q2a, q2b = shift(q1[:mid], 1), shift(q3[mid:], 3)
    second_out = lax.optimization_barrier((second_out, q1, q3))[0]
    got_second = lax.all_to_all(second_out, "dp", split_axis=0, concat_axis=0, tiled=True)
    k0 = pl.pallas_call(
        pick_kernel,
        in_specs=[SMEM, ANY],
        out_specs=VMEM,
        out_shape=jax.ShapeDtypeStruct((wanted_count, tile_part, width), jnp.bfloat16),
        scratch_shapes=[pltpu.SemaphoreType.DMA],
        compiler_params=params(60),
        name="pick",
    )(slot_table, got_first)
    k1, k3 = shift(k0, 1), shift(k0, 3)
    k2a, k2b = shift(k1[:tiles_each], 1), shift(k3[tiles_each:], 3)

    rows = dp_count * part
    keys = tiles_each * TILE
    cuts = 2

    def answers(pieces, *pieces_in):
        piece = pl.BlockSpec((dp_count // cuts, part, width), lambda r, n: (r, n, 0))
        half = pl.BlockSpec((dp_count // cuts, part, width), lambda r, n: (0, n, 0))
        specs = [piece] if pieces == 1 else [piece, piece, half, half]
        answer = pieces * own
        return pl.pallas_call(
            functools.partial(answer_kernel, LOG2E / (width * kernel_width), pieces, skip),
            grid=(cuts, blocks_here),
            in_specs=[SMEM, SMEM] + specs + [ANY] * 7,
            out_specs=pl.BlockSpec((dp_count // cuts, answer, columns), lambda r, n: (r, 0, 0)),
            out_shape=jax.ShapeDtypeStruct((dp_count, answer, columns), jnp.bfloat16),
            scratch_shapes=[
                pltpu.VMEM((blocks_here, tiles_each, TILE, width), jnp.bfloat16),
                pltpu.VMEM((blocks_here, keys, columns), jnp.bfloat16),
                pltpu.SemaphoreType.DMA((blocks_here,)),
                pltpu.SemaphoreType.DMA((blocks_here,)),
            ],
            compiler_params=params(60),
            cost_estimate=pl.CostEstimate(
                flops=2 * pieces * blocks_here * rows * keys * (width + columns),
                transcendentals=pieces * blocks_here * rows * keys,
                bytes_accessed=2 * blocks_here * keys * (width + columns),
            ),
            name="answers",
        )(y1, slot_table, *pieces_in, k0, k1, k3, k2a, k2b, got_first, got_second)

    first = answers(1, arrived)
    back0 = lax.all_to_all(first, "dp", split_axis=0, concat_axis=0, tiled=True)
    rest = answers(3, *lax.optimization_barrier((q1, q3, q2a, q2b, first))[:4])
    back1 = lax.all_to_all(rest, "dp", split_axis=0, concat_axis=0, tiled=True)
    count0, count1 = (back.shape[0] * back.shape[1] for back in (back0, back1))
    return pl.pallas_call(
        unpack_kernel,
        in_specs=[SMEM, VMEM, VMEM],
        out_specs=VMEM,
        out_shape=jax.ShapeDtypeStruct((query_count, columns), jnp.bfloat16),
        scratch_shapes=[
            pltpu.VMEM((count0 + count1, 128), jnp.float32),
            pltpu.VMEM((count0 + count1, 128), jnp.float32),
            pltpu.VMEM((query_count, 128), jnp.float32),
            pltpu.VMEM((query_count, 128), jnp.float32),
        ],
        compiler_params=params(60),
        name="unpack",
    )(pos, back0.reshape(count0, columns), back1.reshape(count1, columns))


def solution(mesh):
    placed = (P("dp", None), P("dp", None), P("dp", None), P("dp", "label"), P("dp", None))
    return jax.shard_map(
        shards, mesh=mesh, in_specs=placed, out_specs=P("dp", "label"), check_vma=False
    )
```

time: 246 us -> 222 us (0.902)
  Pallas kernels: 89.9 us -> 61 us
  blocking collectives: 34 us -> 46.9 us
  other arithmetic: 5.95 us -> 2.8 us
    pallas_call x9 -> x6, Pallas kernels: 72.4 us -> 51.4 us  [the longest x2 32.7 us: answers(): pl.pallas_call(functools.partial(answer_kernel, LOG2E / (width * kernel_w...]
    all_to_all x1, blocking collectives: 34 us -> 46.9 us  [shards(): back1 = lax.all_to_all(rest, 'dp', split_axis=0, concat_axis=0, tiled=True)]
    all_to_all x3, waiting for transfers between devices: 1.64 us -> 11.4 us  [the longest x1 9.05 us: shards(): lax.all_to_all(first_out, 'dp', split_axis=0, concat_axis=0, tiled=True)]
    pallas_call x1, Pallas kernels: 17.5 us -> 9.53 us  [shards(): pl.pallas_call(unpack_kernel, in_specs=[SMEM, VMEM, VMEM], out_specs=VMEM...]
    all_to_all x1, waiting for transfers between devices: 24 us -> 17.1 us  [shards(): lax.all_to_all(sent, 'dp', split_axis=0, concat_axis=0, tiled=True)]
    all_to_all x3, starting transfers between devices: 23 us -> 18.6 us  [the longest x1 9.68 us: shards(): back0 = lax.all_to_all(first, 'dp', split_axis=0, concat_axis=0, tiled=True)]
    ppermute x8, waiting for transfers between devices: 38.6 us -> 34.2 us  [shift(): lax.ppermute(v, 'label', [(i, (i + by) % PLANES) for i in range(PLANES)])]
    concatenate x2 -> x0, other arithmetic: 2.54 us -> none  [the longest x1 1.45 us: shards(): jnp.concatenate([packed.reshape(dp_count, blocks_here * part, width), lat...]
  transfers between devices with their start and end apart: 12 -> 12, of which waited for: 5 -> 7; matrix products, arithmetic and copies ran while one was open for 4% -> 3% of each run, Pallas kernels for 24% -> 17%
where the time goes in v2:
time: 222 us; the launch traced here: 221 us
  waiting for transfers between devices  62.7 us (28%)
  Pallas kernels  61 us (27%)
  blocking collectives  46.9 us (21%)
  starting transfers between devices  39.9 us (18%)
  local copies, waits for them, and re-layouts  7.87 us (4%)
  other arithmetic  2.8 us (1%)
    all_to_all x1, blocking collectives, shards(): back1 = lax.all_to_all(rest, 'dp', split_axis=0, concat_axis=0, tiled=True)  46.9 us
    ppermute x8, waiting for transfers between devices, shift(): lax.ppermute(v, 'label', [(i, (i + by) % PLANES) for i in range(PLANES)])  34.2 us
    pallas_call x2, Pallas kernels, answers(): pl.pallas_call(functools.partial(answer_kernel, LOG2E / (width * kernel_w...  32.7 us
    all_to_all x1, waiting for transfers between devices, shards(): lax.all_to_all(sent, 'dp', split_axis=0, concat_axis=0, tiled=True)  17.1 us
    ppermute x8, starting transfers between devices, shift(): lax.ppermute(v, 'label', [(i, (i + by) % PLANES) for i in range(PLANES)])  11.8 us
    pallas_call x1, Pallas kernels, shards(): pl.pallas_call(functools.partial(pack_kernel, blocks, part, tiles_here),...  9.87 us
    all_to_all x1, starting transfers between devices, shards(): back0 = lax.all_to_all(first, 'dp', split_axis=0, concat_axis=0, tiled=True)  9.68 us
    pallas_call x1, Pallas kernels, shards(): pl.pallas_call(unpack_kernel, in_specs=[SMEM, VMEM, VMEM], out_specs=VMEM...  9.53 us
  transfers between devices with their start and end apart: 12, of which 7 were waited for; matrix products, arithmetic and copies ran while one was open for 3% of the time, Pallas kernels for 17%

profile of v2, /device:TPU:1, one launch (start us, length us, event | category | flops | bytes accessed | tf_op | source)
XLA Modules:
  0.0 221.3 jit_solution(17688945396931349297)
XLA Ops:
  0.0 0.0 copy-start.3
  0.0 9.9 %pack.1 = (bf16[32,72,256]{2,1,0:T(8,128)(2,1)}, s32[1,4096]{1,0:T(1,128)}) custom-call(s32[1]{0:T(128)} %bitcast.y_ref, s32[1,4096]{1,0:T(1,128)} %bitcast.15, s32[2,16]{1,0:T(2,128)} %list_ref.1, bf16[4096,256]{1,0:T(8,128)(2,1)} %x_ref.1), custom_call_target="tpu_custom_call" | custom-call | tf_op jit(solution)/shard_map/pack/pallas_call | solution.py:281
  9.9 9.4 %all-to-all-start = ((bf16[32,72,256]{2,1,0:T(8,128)(2,1)}), bf16[32,72,256]{2,1,0:T(8,128)(2,1)S(1)}, u32[]{:S(2)}, u32[]{:S(2)}) async-start(bf16[32,72,256]{2,1,0:T(8,128)(2,1)} %get-tuple-element.13), calls=%async_computation | async-start | bytes 2359296 | tf_op jit(solution)/shard_map/all_to_all | solution.py:303
  19.3 0.0 copy-done.3
  19.3 0.2 fusion
  19.6 1.0 fusion.1.latent_ref
  20.6 17.1 %all-to-all-done.refs_0_ = bf16[32,72,256]{2,1,0:T(8,128)(2,1)S(1)} async-done(((bf16[32,72,256]{2,1,0:T(8,128)(2,1)}), bf16[32,72,256]{2,1,0:T(8,128)(2,1)S(1)}, u32[]{:S(2)}, u32[]{:S(2)}) %all-to-all-start) | async-done | bytes 1179680 | tf_op jit(solution)/shard_map/all_to_all | solution.py:303
  37.7 0.0 copy-start.1
  37.7 0.2 slice.18
  37.9 0.8 convert_element_type.19
  38.7 3.4 %first_tiles.1 = bf16[32,192,256]{2,1,0:T(8,128)(2,1)} custom-call(s32[32,2]{1,0:T(8,128)} %bitcast.13, bf16[32,32,256]{2,1,0:T(8,128)(2,1)} %fusion.1.latent_ref, bf16[32,128,256]{2,1,0:T(8,128)(2,1)} %bitcast.8), custom_call_target="tpu_custom_call" | custom-call | tf_op jit(solution)/shard_map/first_tiles/pallas_call | solution.py:309
  42.1 0.0 copy-done.1
  42.1 3.9 %all-to-all-start.1 = ((bf16[32,192,256]{2,1,0:T(8,128)(2,1)}), bf16[32,192,256]{2,1,0:T(8,128)(2,1)S(1)}, u32[]{:S(2)}, u32[]{:S(2)}) async-start(bf16[32,192,256]{2,1,0:T(8,128)(2,1)} %first_tiles.1), calls=%async_computation.1 | async-start | bytes 6291456 | tf_op jit(solution)/shard_map/all_to_all | solution.py:318
  46.0 2.3 %slice.26 = bf16[32,64,256]{2,1,0:T(8,128)(2,1)} slice(bf16[32,72,256]{2,1,0:T(8,128)(2,1)} %copy-done.1), slice={[0:32], [0:64], [0:256]} | slice | bytes 2097152 | tf_op jit(solution)/shard_map/slice | solution.py:332
  48.4 2.7 %collective-permute-start.5 = (bf16[32,64,256]{2,1,0:T(8,128)(2,1)}, bf16[32,64,256]{2,1,0:T(8,128)(2,1)}, u32[]{:S(2)}, u32[]{:S(2)}) collective-permute-start(bf16[32,64,256]{2,1,0:T(8,128)(2,1)} %slice.26), channel_id=1, source_target_pairs={{0,3},{1,0},{2,1},{3,2},{4,7},{5,4},{6,5},{7,6},{8,11},{9,8},{10,9... | collective-permute-start | bytes 3145736 | tf_op jit(solution)/shard_map/ppermute | solution.py:330
  51.1 0.0 collective-permute-start.4
  51.1 2.9 %second_tiles.1 = bf16[32,128,256]{2,1,0:T(8,128)(2,1)} custom-call(s32[32,2]{1,0:T(8,128)} %bitcast.14, bf16[32,128,256]{2,1,0:T(8,128)(2,1)} %bitcast.9), custom_call_target="tpu_custom_call" | custom-call | tf_op jit(solution)/shard_map/second_tiles/pallas_call | solution.py:319
  54.0 0.0 copy-start.6
  54.0 19.6 %collective-permute-done.5.refs_1_ = bf16[32,64,256]{2,1,0:T(8,128)(2,1)} collective-permute-done((bf16[32,64,256]{2,1,0:T(8,128)(2,1)}, bf16[32,64,256]{2,1,0:T(8,128)(2,1)}, u32[]{:S(2)}, u32[]{:S(2)}) %collective-permute-start.5) | collective-permute-done | bytes 1048608 | tf_op jit(solution)/shard_map/ppermute | solution.py:330
  73.6 3.1 %collective-permute-done.4.refs_0_ = bf16[32,64,256]{2,1,0:T(8,128)(2,1)} collective-permute-done((bf16[32,64,256]{2,1,0:T(8,128)(2,1)}, bf16[32,64,256]{2,1,0:T(8,128)(2,1)}, u32[]{:S(2)}, u32[]{:S(2)}) %collective-permute-start.4) | collective-permute-done | bytes 1048608 | tf_op jit(solution)/shard_map/ppermute | solution.py:330
  76.8 9.1 %all-to-all-done.1.arrived_ref.refs_6_.refs_9_ = bf16[32,192,256]{2,1,0:T(8,128)(2,1)S(1)} async-done(((bf16[32,192,256]{2,1,0:T(8,128)(2,1)}), bf16[32,192,256]{2,1,0:T(8,128)(2,1)S(1)}, u32[]{:S(2)}, u32[]{:S(2)}) %all-to-all-start.1) | async-done | bytes 3145760 | tf_op jit(solution)/shard_map/all_to_all | solution.py:318
  85.8 0.0 copy-start
  85.8 1.7 copy-done
  87.5 5.1 %all-to-all-start.2 = ((bf16[32,128,256]{2,1,0:T(8,128)(2,1)}), bf16[32,128,256]{2,1,0:T(8,128)(2,1)}, u32[]{:S(2)}, u32[]{:S(2)}) async-start(bf16[32,128,256]{2,1,0:T(8,128)(2,1)} %second_tiles.1), calls=%async_computation.2 | async-start | bytes 4194304 | tf_op jit(solution)/shard_map/all_to_all | solution.py:337
  92.6 0.0 copy-done.6
  92.6 0.1 reshape.91
  92.7 0.2 convert_reduce_fusion
  92.9 0.1 reduce_sum.21
  93.0 0.6 multiply_add_fusion.slot_ref
  93.6 2.6 %pick.1.refs_1_.refs_4_ = bf16[32,32,256]{2,1,0:T(8,128)(2,1)} custom-call(s32[2,16]{1,0:T(2,128)} %multiply_add_fusion.slot_ref, bf16[32,192,256]{2,1,0:T(8,128)(2,1)} %copy-done), custom_call_target="tpu_custom_call" | custom-call | tf_op jit(solution)/shard_map/pick/pallas_call | solution.py:338
  96.1 2.8 %collective-permute-start.1 = (bf16[32,32,256]{2,1,0:T(8,128)(2,1)}, bf16[32,32,256]{2,1,0:T(8,128)(2,1)S(1)}, u32[]{:S(2)}, u32[]{:S(2)}) collective-permute-start(bf16[32,32,256]{2,1,0:T(8,128)(2,1)} %pick.1.refs_1_.refs_4_), channel_id=1, source_target_pairs={{0,3},{1,0},{2,1},{3,2},{4,7},{5,4},{6,5},{7,6},{8,11},{9,8},{10,9... | collective-permute-start | bytes 1572872 | tf_op jit(solution)/shard_map/ppermute | solution.py:330
  98.9 0.0 collective-permute-start
  98.9 11.2 %collective-permute-done.1.refs_3_.refs_6_ = bf16[32,32,256]{2,1,0:T(8,128)(2,1)S(1)} collective-permute-done((bf16[32,32,256]{2,1,0:T(8,128)(2,1)}, bf16[32,32,256]{2,1,0:T(8,128)(2,1)S(1)}, u32[]{:S(2)}, u32[]{:S(2)}) %collective-permute-start.1) | collective-permute-done | bytes 524320 | tf_op jit(solution)/shard_map/ppermute | solution.py:330
  110.1 0.0 copy-start.4
  110.1 3.5 %collective-permute-start.3 = (bf16[16,32,256]{2,1,0:T(8,128)(2,1)S(1)}, bf16[16,32,256]{2,1,0:T(8,128)(2,1)S(1)}, u32[]{:S(2)}, u32[]{:S(2)}) collective-permute-start(bf16[16,32,256]{2,1,0:T(8,128)(2,1)S(1)} %slice.25), channel_id=1, source_target_pairs={{0,3},{1,0},{2,1},{3,2},{4,7},{5,4},{6,5},{7,6},{8,11},{9,8},{10,9... | collective-permute-start | bytes 786440 | tf_op jit(solution)/shard_map/ppermute | solution.py:330
  113.6 0.0 collective-permute-done.refs_2_.refs_5_
  113.6 0.0 copy-start.5
  113.6 0.1 collective-permute-start.2
  113.7 1.2 slice.28
  114.9 2.6 %collective-permute-start.7 = (bf16[16,64,256]{2,1,0:T(8,128)(2,1)S(1)}, bf16[16,64,256]{2,1,0:T(8,128)(2,1)}, u32[]{:S(2)}, u32[]{:S(2)}) collective-permute-start(bf16[16,64,256]{2,1,0:T(8,128)(2,1)S(1)} %slice.28), channel_id=1, source_target_pairs={{0,3},{1,0},{2,1},{3,2},{4,7},{5,4},{6,5},{7,6},{8,11},{9,8},{10,9... | collective-permute-start | bytes 1572872 | tf_op jit(solution)/shard_map/ppermute | solution.py:330
  117.5 1.1 slice.27
  118.6 0.1 collective-permute-start.6
  118.7 2.4 %all-to-all-done.2.refs_7_.refs_10_ = bf16[32,128,256]{2,1,0:T(8,128)(2,1)} async-done(((bf16[32,128,256]{2,1,0:T(8,128)(2,1)}), bf16[32,128,256]{2,1,0:T(8,128)(2,1)}, u32[]{:S(2)}, u32[]{:S(2)}) %all-to-all-start.2) | async-done | bytes 2097184 | tf_op jit(solution)/shard_map/all_to_all | solution.py:337
  121.1 0.0 collective-permute-done.3.refs_5_.refs_8_
  121.1 0.0 copy-start.7
  121.1 0.3 collective-permute-done.2.refs_4_.refs_7_
  121.3 0.0 copy-done.4
  121.3 0.0 copy-done.5
  121.3 0.4 copy-done.7
  121.8 0.0 copy-start.8
  121.8 0.7 copy-done.8
  122.5 11.6 %answers.2 = bf16[32,64,256]{2,1,0:T(8,128)(2,1)} custom-call(s32[1]{0:T(128)} %bitcast.y_ref, s32[2,16]{1,0:T(2,128)} %multiply_add_fusion.slot_ref, bf16[32,72,256]{2,1,0:T(8,128)(2,1)} %copy-done.1, bf16[32,32,256]{2,1,0:T(8,128)(2,1)} %pick.1.refs_1_.refs_4_, bf16[32,32,256]{2,1,0:T(8,128)(2,1)} %copy-done.5, bf16[32,32,256]{2,1,0:T(8,128)(2,1)} %copy-done.4, ...), custom_call_target="tpu_custom_call" | custom-call | flops 4294967296 | bytes 4194304 | tf_op jit(solution)/shard_map/answers/pallas_call | solution.py:359
  134.1 9.7 %all-to-all-start.3 = ((bf16[32,64,256]{2,1,0:T(8,128)(2,1)}), bf16[32,64,256]{2,1,0:T(8,128)(2,1)S(1)}, u32[]{:S(2)}, u32[]{:S(2)}) async-start(bf16[32,64,256]{2,1,0:T(8,128)(2,1)} %answers.2), calls=%async_computation.3 | async-start | bytes 2097152 | tf_op jit(solution)/shard_map/all_to_all | solution.py:381
  143.8 0.0 collective-permute-done.7.refs_3_
  143.8 0.0 collective-permute-done.6.refs_2_
  143.8 21.1 %answers.3 = bf16[32,192,256]{2,1,0:T(8,128)(2,1)} custom-call(s32[1]{0:T(128)} %bitcast.y_ref, s32[2,16]{1,0:T(2,128)} %multiply_add_fusion.slot_ref, bf16[32,64,256]{2,1,0:T(8,128)(2,1)} %collective-permute-done.4.refs_0_, bf16[32,64,256]{2,1,0:T(8,128)(2,1)} %collective-permute-done.5.refs_1_, bf16[16,64,256]{2,1,0:T(8,128)(2,1)} %collective-permute-done.6.refs_2_, ...), custom_call_target="tpu_custom_call" | custom-call | flops 12884901888 | bytes 4194304 | tf_op jit(solution)/shard_map/answers/pallas_call | solution.py:359
  164.9 0.0 all-to-all-done.3
  164.9 0.0 copy-start.2
  164.9 46.9 %all_to_all.25 = bf16[32,192,256]{2,1,0:T(8,128)(2,1)} all-to-all(bf16[32,192,256]{2,1,0:T(8,128)(2,1)} %answers.3), channel_id=1, replica_groups=mesh['dp'=32,'label'=4] {'dp'}, dimensions={0} | all-to-all | bytes 6291456 | tf_op jit(solution)/shard_map/all_to_all | solution.py:383
  211.8 0.0 copy-done.2
  211.8 9.5 %unpack.1 = bf16[4096,256]{1,0:T(8,128)(2,1)} custom-call(s32[1,4096]{1,0:T(1,128)} %get-tuple-element.12.pos_ref, bf16[2048,256]{1,0:T(8,128)(2,1)} %bitcast.10, bf16[6144,256]{1,0:T(8,128)(2,1)} %bitcast.7), custom_call_target="tpu_custom_call" | custom-call | tf_op jit(solution)/shard_map/unpack/pallas_call | solution.py:385
  (4 shorter events, 0.1 us)
Async XLA Ops:
  0.0 19.3 %copy-start.3 = (bf16[4096,256]{1,0:T(8,128)(2,1)S(1)}, bf16[4096,256]{1,0:T(8,128)(2,1)}, u32[]{:S(2)}) copy-start(bf16[4096,256]{1,0:T(8,128)(2,1)} %param.7) | copy-start | bytes 6291460
  9.9 27.8 %all-to-all-start = ((bf16[32,72,256]{2,1,0:T(8,128)(2,1)}), bf16[32,72,256]{2,1,0:T(8,128)(2,1)S(1)}, u32[]{:S(2)}, u32[]{:S(2)}) async-start(bf16[32,72,256]{2,1,0:T(8,128)(2,1)} %get-tuple-element.13), calls=%async_computation | async-start | bytes 2359296 | tf_op jit(solution)/shard_map/all_to_all | solution.py:303
  37.7 4.5 %copy-start.1 = (bf16[32,72,256]{2,1,0:T(8,128)(2,1)}, bf16[32,72,256]{2,1,0:T(8,128)(2,1)S(1)}, u32[]{:S(2)}) copy-start(bf16[32,72,256]{2,1,0:T(8,128)(2,1)S(1)} %all-to-all-done.refs_0_) | copy-start | bytes 3538948
  42.1 43.7 %all-to-all-start.1 = ((bf16[32,192,256]{2,1,0:T(8,128)(2,1)}), bf16[32,192,256]{2,1,0:T(8,128)(2,1)S(1)}, u32[]{:S(2)}, u32[]{:S(2)}) async-start(bf16[32,192,256]{2,1,0:T(8,128)(2,1)} %first_tiles.1), calls=%async_computation.1 | async-start | bytes 6291456 | tf_op jit(solution)/shard_map/all_to_all | solution.py:318
  48.4 25.3 %collective-permute-start.5 = (bf16[32,64,256]{2,1,0:T(8,128)(2,1)}, bf16[32,64,256]{2,1,0:T(8,128)(2,1)}, u32[]{:S(2)}, u32[]{:S(2)}) collective-permute-start(bf16[32,64,256]{2,1,0:T(8,128)(2,1)} %slice.26), channel_id=1, source_target_pairs={{0,3},{1,0},{2,1},{3,2},{4,7},{5,4},{6,5},{7,6},{8,11},{9,8},{10,9... | collective-permute-start | bytes 3145736 | tf_op jit(solution)/shard_map/ppermute | solution.py:330
  51.1 25.7 %collective-permute-start.4 = (bf16[32,64,256]{2,1,0:T(8,128)(2,1)}, bf16[32,64,256]{2,1,0:T(8,128)(2,1)}, u32[]{:S(2)}, u32[]{:S(2)}) collective-permute-start(bf16[32,64,256]{2,1,0:T(8,128)(2,1)} %slice.26), channel_id=1, source_target_pairs={{0,1},{1,2},{2,3},{3,0},{4,5},{5,6},{6,7},{7,4},{8,9},{9,10},{10,1... | collective-permute-start | bytes 3145736 | tf_op jit(solution)/shard_map/ppermute | solution.py:330
  54.0 38.6 %copy-start.6 = (s32[2,16]{1,0:T(2,128)S(1)}, s32[2,16]{1,0:T(2,128)}, u32[]{:S(2)}) copy-start(s32[2,16]{1,0:T(2,128)} %list_ref.1) | copy-start | bytes 388
  85.8 1.7 copy-start
  87.5 33.5 %all-to-all-start.2 = ((bf16[32,128,256]{2,1,0:T(8,128)(2,1)}), bf16[32,128,256]{2,1,0:T(8,128)(2,1)}, u32[]{:S(2)}, u32[]{:S(2)}) async-start(bf16[32,128,256]{2,1,0:T(8,128)(2,1)} %second_tiles.1), calls=%async_computation.2 | async-start | bytes 4194304 | tf_op jit(solution)/shard_map/all_to_all | solution.py:337
  96.1 14.0 %collective-permute-start.1 = (bf16[32,32,256]{2,1,0:T(8,128)(2,1)}, bf16[32,32,256]{2,1,0:T(8,128)(2,1)S(1)}, u32[]{:S(2)}, u32[]{:S(2)}) collective-permute-start(bf16[32,32,256]{2,1,0:T(8,128)(2,1)} %pick.1.refs_1_.refs_4_), channel_id=1, source_target_pairs={{0,3},{1,0},{2,1},{3,2},{4,7},{5,4},{6,5},{7,6},{8,11},{9,8},{10,9... | collective-permute-start | bytes 1572872 | tf_op jit(solution)/shard_map/ppermute | solution.py:330
  98.9 14.7 %collective-permute-start = (bf16[32,32,256]{2,1,0:T(8,128)(2,1)}, bf16[32,32,256]{2,1,0:T(8,128)(2,1)S(1)}, u32[]{:S(2)}, u32[]{:S(2)}) collective-permute-start(bf16[32,32,256]{2,1,0:T(8,128)(2,1)} %pick.1.refs_1_.refs_4_), channel_id=1, source_target_pairs={{0,1},{1,2},{2,3},{3,0},{4,5},{5,6},{6,7},{7,4},{8,9},{9,10},{10,1... | collective-permute-start | bytes 1572872 | tf_op jit(solution)/shard_map/ppermute | solution.py:330
  110.1 11.2 %copy-start.4 = (bf16[32,32,256]{2,1,0:T(8,128)(2,1)}, bf16[32,32,256]{2,1,0:T(8,128)(2,1)S(1)}, u32[]{:S(2)}) copy-start(bf16[32,32,256]{2,1,0:T(8,128)(2,1)S(1)} %collective-permute-done.1.refs_3_.refs_6_) | copy-start | bytes 1572868
  110.1 10.9 %collective-permute-start.3 = (bf16[16,32,256]{2,1,0:T(8,128)(2,1)S(1)}, bf16[16,32,256]{2,1,0:T(8,128)(2,1)S(1)}, u32[]{:S(2)}, u32[]{:S(2)}) collective-permute-start(bf16[16,32,256]{2,1,0:T(8,128)(2,1)S(1)} %slice.25), channel_id=1, source_target_pairs={{0,3},{1,0},{2,1},{3,2},{4,7},{5,4},{6,5},{7,6},{8,11},{9,8},{10,9... | collective-permute-start | bytes 786440 | tf_op jit(solution)/shard_map/ppermute | solution.py:330
  113.6 7.7 %copy-start.5 = (bf16[32,32,256]{2,1,0:T(8,128)(2,1)}, bf16[32,32,256]{2,1,0:T(8,128)(2,1)S(1)}, u32[]{:S(2)}) copy-start(bf16[32,32,256]{2,1,0:T(8,128)(2,1)S(1)} %collective-permute-done.refs_2_.refs_5_) | copy-start | bytes 1572868
  113.6 7.7 %collective-permute-start.2 = (bf16[16,32,256]{2,1,0:T(8,128)(2,1)S(1)}, bf16[16,32,256]{2,1,0:T(8,128)(2,1)S(1)}, u32[]{:S(2)}, u32[]{:S(2)}) collective-permute-start(bf16[16,32,256]{2,1,0:T(8,128)(2,1)S(1)} %slice.24), channel_id=1, source_target_pairs={{0,1},{1,2},{2,3},{3,0},{4,5},{5,6},{6,7},{7,4},{8,9},{9,10},{10,1... | collective-permute-start | bytes 786440 | tf_op jit(solution)/shard_map/ppermute | solution.py:330
  114.9 28.9 %collective-permute-start.7 = (bf16[16,64,256]{2,1,0:T(8,128)(2,1)S(1)}, bf16[16,64,256]{2,1,0:T(8,128)(2,1)}, u32[]{:S(2)}, u32[]{:S(2)}) collective-permute-start(bf16[16,64,256]{2,1,0:T(8,128)(2,1)S(1)} %slice.28), channel_id=1, source_target_pairs={{0,3},{1,0},{2,1},{3,2},{4,7},{5,4},{6,5},{7,6},{8,11},{9,8},{10,9... | collective-permute-start | bytes 1572872 | tf_op jit(solution)/shard_map/ppermute | solution.py:330
  118.6 25.2 %collective-permute-start.6 = (bf16[16,64,256]{2,1,0:T(8,128)(2,1)S(1)}, bf16[16,64,256]{2,1,0:T(8,128)(2,1)}, u32[]{:S(2)}, u32[]{:S(2)}) collective-permute-start(bf16[16,64,256]{2,1,0:T(8,128)(2,1)S(1)} %slice.27), channel_id=1, source_target_pairs={{0,1},{1,2},{2,3},{3,0},{4,5},{5,6},{6,7},{7,4},{8,9},{9,10},{10,1... | collective-permute-start | bytes 1572872 | tf_op jit(solution)/shard_map/ppermute | solution.py:330
  121.1 0.7 copy-start.7
  121.8 0.7 copy-start.8
  134.1 30.8 %all-to-all-start.3 = ((bf16[32,64,256]{2,1,0:T(8,128)(2,1)}), bf16[32,64,256]{2,1,0:T(8,128)(2,1)S(1)}, u32[]{:S(2)}, u32[]{:S(2)}) async-start(bf16[32,64,256]{2,1,0:T(8,128)(2,1)} %answers.2), calls=%async_computation.3 | async-start | bytes 2097152 | tf_op jit(solution)/shard_map/all_to_all | solution.py:381
  164.9 46.9 %copy-start.2 = (bf16[32,64,256]{2,1,0:T(8,128)(2,1)}, bf16[32,64,256]{2,1,0:T(8,128)(2,1)S(1)}, u32[]{:S(2)}) copy-start(bf16[32,64,256]{2,1,0:T(8,128)(2,1)S(1)} %all-to-all-done.3) | copy-start | bytes 3145732

commit v3 on v2

v3 whole, which is shorter than its diff:
```python
import functools
import jax
import jax.numpy as jnp
from jax import lax
from jax.sharding import PartitionSpec as P
from jax.experimental import pallas as pl
from jax.experimental.pallas import tpu as pltpu

TILE = 128
kernel_width = 0.025
norm_epsilon = 1e-05
PLANES = 4
FULL = 64
LOG2E = 1.4426950408889634
VMEM = pl.BlockSpec(memory_space=pltpu.VMEM)
ANY = pl.BlockSpec(memory_space=pl.ANY)
SMEM = pl.BlockSpec(memory_space=pltpu.SMEM)


def unit_rows(values):
    widened = values.astype(jnp.float32)
    scaled = widened * lax.rsqrt(jnp.mean(widened * widened, axis=-1, keepdims=True) + norm_epsilon)
    return scaled.astype(jnp.bfloat16)


def params(mib, **kw):
    return pltpu.CompilerParams(vmem_limit_bytes=min(mib * 1024 * 1024, 67043328), **kw)


def pack_kernel(
    blocks, part, tiles_here, y_ref, ids_ref, list_ref, x_ref,
    out_ref, pos_ref, rows, table, got, hold, inv, row_sem, inv_sem,
):
    load = pltpu.make_async_copy(x_ref, rows, row_sem)
    load.start()
    y = y_ref[0]
    lanes = 128
    own = 2 * part
    wanted = list_ref[...]
    wanted = jnp.concatenate([wanted[n : n + 1] for n in range(wanted.shape[0])], axis=1)
    many = wanted.shape[1]
    across = lax.broadcasted_iota(jnp.int32, (many, many), 1)
    down = lax.broadcasted_iota(jnp.int32, (many, many), 0)
    source = wanted // tiles_here
    upright = jnp.sum(jnp.where(across == down, source.astype(jnp.float32), 0.0), axis=1, keepdims=True)
    same = (upright.astype(jnp.int32) == source) & (down < across)
    order = jnp.sum(same.astype(jnp.float32), axis=0, keepdims=True)
    holders, told_rows = out_ref.shape[0], out_ref.shape[1] - own
    holder = lax.broadcasted_iota(jnp.int32, (holders, many), 0) == source
    number = (wanted % tiles_here).astype(jnp.float32)
    for k in range(2):
        told = jnp.sum(jnp.where(holder & (order == k), number, 0.0), axis=1, keepdims=True)
        told = jnp.broadcast_to(told[:, :, None], (holders, told_rows, lanes))
        out_ref[:, own:, k * lanes : (k + 1) * lanes] = told.astype(jnp.bfloat16)

    count = ids_ref.shape[1]
    step = 256
    upper = (
        lax.broadcasted_iota(jnp.int32, (step, step), 0)
        <= lax.broadcasted_iota(jnp.int32, (step, step), 1)
    ).astype(jnp.bfloat16)
    block_no = lax.broadcasted_iota(jnp.int32, (blocks, step), 0)
    slot_no = lax.broadcasted_iota(jnp.int32, (lanes, step), 0) + part * y
    lane = lax.broadcasted_iota(jnp.int32, (1, step), 1)
    carry = jnp.zeros((blocks, 1), jnp.float32)
    high = jnp.zeros((blocks, lanes), jnp.float32)
    low = jnp.zeros((blocks, lanes), jnp.float32)
    nt = (((1,), (1,)), ((), ()))
    for c in range(count // step):
        ids = ids_ref[:, c * step : (c + 1) * step]
        hit = block_no == ids
        hits = hit.astype(jnp.bfloat16)
        upto = jnp.dot(hits, upper, preferred_element_type=jnp.float32)
        rank = jnp.sum(jnp.where(hit, upto + carry, 0.0), axis=0, keepdims=True)
        rank = rank.astype(jnp.int32) - 1
        carry = carry + upto[:, step - 1 : step]
        turn = (y + PLANES - rank // part) % PLANES
        place = jnp.where(turn < 2, turn, 5 - turn)
        pos_ref[:, c * step : (c + 1) * step] = 2 * (
            place // 2 * (2 * blocks * part)
            + ids // 2 * (4 * part)
            + place % 2 * (2 * part)
            + ids % 2 * part
            + rank % part
        )
        row = lane + c * step
        chosen = (slot_no == rank).astype(jnp.bfloat16)
        row_high = (row // 64).astype(jnp.float32)
        row_low = (row % 64).astype(jnp.float32)
        high += lax.dot_general(
            jnp.where(hit, row_high, 0.0).astype(jnp.bfloat16), chosen, nt, preferred_element_type=jnp.float32
        )
        low += lax.dot_general(
            jnp.where(hit, row_low, 0.0).astype(jnp.bfloat16), chosen, nt, preferred_element_type=jnp.float32
        )
    hold[...] = high.astype(jnp.int32) * 128 + low.astype(jnp.int32) * 2
    tell = pltpu.make_async_copy(hold, inv, inv_sem)
    tell.start()
    load.wait()

    @pl.loop(0, count // step)
    def _(c):
        at = pl.ds(pl.multiple_of(c * step, step), step)
        to = pl.multiple_of(2 * c * step, 2 * step)
        table[pl.ds(to, step, stride=2), :] = rows[at, :lanes].astype(jnp.float32)
        table[pl.ds(to + 1, step, stride=2), :] = rows[at, lanes:].astype(jnp.float32)

    tell.wait()

    @pl.loop(0, blocks)
    def _(b):
        at = pl.multiple_of(2 * b * part, 2 * part)
        for r in range(part):
            i = pl.multiple_of(inv[b, r], 2)
            got[pl.ds(at + 2 * r, 2), :] = table[pl.ds(i, 2), :]

    width = 2 * lanes
    some = 4

    @pl.loop(0, out_ref.shape[0] // some)
    def _(g):
        at = pl.multiple_of(2 * g * some * own, 2 * some * own)
        a = got[pl.ds(at, some * own, stride=2), :]
        b = got[pl.ds(at + 1, some * own, stride=2), :]
        scale = lax.rsqrt(jnp.sum(a * a + b * b, axis=-1, keepdims=True) / width + norm_epsilon)
        to = pl.ds(g * some, some)
        out_ref[to, :own, :lanes] = (a * scale).astype(jnp.bfloat16).reshape(some, own, lanes)
        out_ref[to, :own, lanes:] = (b * scale).astype(jnp.bfloat16).reshape(some, own, lanes)


def first_kernel(asked_ref, latent_ref, label_ref, out_ref, sem):
    dests, slots = asked_ref.shape
    part, rows = latent_ref.shape[1], label_ref.shape[1]
    for d in range(dests):
        for s in range(slots):
            pltpu.make_async_copy(
                latent_ref.at[asked_ref[d, s]], out_ref.at[d, pl.ds(s * part, part)], sem
            ).start()
        pltpu.make_async_copy(
            label_ref.at[asked_ref[d, 0]], out_ref.at[d, pl.ds(slots * part, rows)], sem
        ).start()
    pltpu.make_async_copy(out_ref, out_ref, sem).wait()


def second_kernel(asked_ref, label_ref, out_ref, sem):
    for d in range(asked_ref.shape[0]):
        pltpu.make_async_copy(label_ref.at[asked_ref[d, 1]], out_ref.at[d], sem).start()
    pltpu.make_async_copy(out_ref, out_ref, sem).wait()


def pick_kernel(slot_ref, arrived_ref, *refs):
    _, tiles = slot_ref.shape
    sem = refs[-1]
    part = refs[0].shape[1]
    for n, out_ref in enumerate(refs[:-1]):
        for j in range(tiles):
            slot = slot_ref[n, j]
            row = pl.multiple_of(slot % 2 * part, part)
            pltpu.make_async_copy(
                arrived_ref.at[slot // 2, pl.ds(row, part)], out_ref.at[j], sem.at[n]
            ).start()
    for n, out_ref in enumerate(refs[:-1]):
        pltpu.make_async_copy(out_ref, out_ref, sem.at[n]).wait()


def answer_kernel(scale, skip, y_ref, slot_ref, *refs):
    latents, (first_ref, second_ref) = refs[-15:-7], refs[-7:-5]
    out_ref, keys, values, key_sem, sems = refs[-5:]
    pieces = refs[:-15]
    y = y_ref[0]
    blocks, tiles = slot_ref.shape
    rows = keys.shape[2]
    tile_part = rows // PLANES
    piece, block = pl.program_id(0), pl.program_id(1)

    @pl.when((piece == 0) & (block == 0))
    def _():
        for n in range(blocks):
            for turn, ref in enumerate(latents[n * PLANES : (n + 1) * PLANES]):
                row = pl.multiple_of((y + PLANES - turn) % PLANES * tile_part, tile_part)
                pltpu.make_async_copy(ref, keys.at[n, :, pl.ds(row, tile_part)], key_sem.at[n]).start()

            @pl.loop(0, tiles)
            def _(j):
                slot = slot_ref[n, j]
                to = values.at[n, pl.ds(pl.multiple_of(j * rows, rows), rows)]

                @pl.when(slot % 2 == 0)
                def _():
                    pltpu.make_async_copy(first_ref.at[slot // 2, pl.ds(skip, rows)], to, sems.at[n]).start()

                @pl.when(slot % 2 == 1)
                def _():
                    pltpu.make_async_copy(second_ref.at[slot // 2], to, sems.at[n]).start()

    @pl.when(piece == 0)
    def _():
        pltpu.make_async_copy(keys.at[block], keys.at[block], key_sem.at[block]).wait()
        pltpu.make_async_copy(values.at[block], values.at[block], sems.at[block]).wait()

    nt = (((1,), (1,)), ((), ()))
    group = 2
    span = group * rows
    sources = out_ref.shape[0]
    second = pieces[1][...]
    if len(pieces) == 3:
        second = jnp.concatenate([second, pieces[2][...]], axis=0)
    q = jnp.where(piece == 0, pieces[0][...], second)
    part, width = q.shape[1:]
    q = q.reshape(sources * part, width)
    total = jnp.zeros((sources * part, 1), jnp.float32)
    weighted = jnp.zeros((sources * part, values.shape[2]), jnp.float32)
    for at in range(tiles // group):
        k = keys[block, at * group : (at + 1) * group].reshape(span, width)
        s = lax.dot_general(q, k, nt, preferred_element_type=jnp.float32)
        e = jnp.exp2(s * scale)
        total = total + jnp.sum(e, axis=1, keepdims=True)
        weighted = weighted + jnp.dot(
            e.astype(jnp.bfloat16), values[block, at * span : (at + 1) * span], preferred_element_type=jnp.float32
        )
    answer = (weighted / total).astype(jnp.bfloat16).reshape(sources, part, values.shape[2])
    at = pl.multiple_of((2 * piece + block) * part, part)
    out_ref[:, pl.ds(at, part), :] = answer


def unpack_kernel(pos_ref, a_ref, b_ref, out_ref, table, got):
    lanes = 128
    step = 256
    start = 0
    for ref in (a_ref, b_ref):

        @pl.loop(0, ref.shape[0] // step)
        def _(c):
            at = pl.ds(pl.multiple_of(c * step, step), step)
            to = pl.multiple_of(2 * (c * step + start), 2 * step)
            table[pl.ds(to, step, stride=2), :] = ref[at, :lanes].astype(jnp.float32)
            table[pl.ds(to + 1, step, stride=2), :] = ref[at, lanes:].astype(jnp.float32)

        start += ref.shape[0]

    count = out_ref.shape[0]

    @pl.loop(0, count // 32)
    def _(c):
        at = pl.multiple_of(c * 64, 64)
        for r in range(32):
            i = pl.multiple_of(pos_ref[0, c * 32 + r], 2)
            got[pl.ds(at + 2 * r, 2), :] = table[pl.ds(i, 2), :]

    @pl.loop(0, count // step)
    def _(c):
        at = pl.multiple_of(c * step, step)
        out_ref[pl.ds(at, step), :lanes] = got[pl.ds(2 * at, step, stride=2), :].astype(jnp.bfloat16)
        out_ref[pl.ds(at, step), lanes:] = got[pl.ds(2 * at + 1, step, stride=2), :].astype(jnp.bfloat16)


def shards(queries, cluster, anchor_latent, anchor_labels, tile_list):
    dp_count = lax.axis_size("dp")
    y = lax.axis_index("label").astype(jnp.int32)
    y1 = y.reshape(1)
    query_count, width = queries.shape
    blocks_here, tiles_each = tile_list.shape
    blocks = blocks_here * dp_count
    capacity = 2 * query_count // blocks
    part = capacity // PLANES
    tiles_here = anchor_latent.shape[0] // TILE
    tile_part = TILE // PLANES
    columns = anchor_labels.shape[1]
    wanted_count = blocks_here * tiles_each
    slots = 2

    wanted = tile_list.reshape(wanted_count)
    source = wanted // tiles_here
    number = jnp.arange(wanted_count, dtype=jnp.int32)
    order = jnp.sum(
        ((source[:, None] == source[None, :]) & (number[None, :] < number[:, None])).astype(jnp.int32), axis=1
    )
    slot_of = source * slots + order
    slot_table = slot_of.reshape(blocks_here, tiles_each)

    own = blocks_here * part
    sent, pos = pl.pallas_call(
        functools.partial(pack_kernel, blocks, part, tiles_here),
        in_specs=[SMEM, VMEM, VMEM, ANY],
        out_specs=[VMEM, VMEM],
        out_shape=[
            jax.ShapeDtypeStruct((dp_count, own + 8, width), jnp.bfloat16),
            jax.ShapeDtypeStruct((1, query_count), jnp.int32),
        ],
        scratch_shapes=[
            pltpu.VMEM((query_count, width), jnp.bfloat16),
            pltpu.VMEM((2 * query_count, 128), jnp.float32),
            pltpu.VMEM((2 * blocks * part, 128), jnp.float32),
            pltpu.VMEM((blocks, 128), jnp.int32),
            pltpu.SMEM((blocks, 128), jnp.int32),
            pltpu.SemaphoreType.DMA,
            pltpu.SemaphoreType.DMA,
        ],
        compiler_params=params(FULL),
        name="pack",
    )(y1, cluster.reshape(1, query_count), tile_list, queries)
    arrived = lax.all_to_all(sent, "dp", split_axis=0, concat_axis=0, tiled=True)
    asked = arrived[:, own, :: width // slots].astype(jnp.int32)

    quarter = lax.dynamic_slice_in_dim(anchor_latent.reshape(tiles_here, TILE, width), y * tile_part, tile_part, axis=1)
    label_tiles = anchor_labels.reshape(tiles_here, TILE, columns)
    skip = slots * tile_part
    first_out = pl.pallas_call(
        first_kernel,
        in_specs=[SMEM, VMEM, VMEM],
        out_specs=ANY,
        out_shape=jax.ShapeDtypeStruct((dp_count, skip + TILE, columns), jnp.bfloat16),
        scratch_shapes=[pltpu.SemaphoreType.DMA],
        compiler_params=params(8),
        name="first_tiles",
    )(asked, unit_rows(quarter), label_tiles)
    got_first = lax.all_to_all(first_out, "dp", split_axis=0, concat_axis=0, tiled=True)
    second_out = pl.pallas_call(
        second_kernel,
        in_specs=[SMEM, VMEM],
        out_specs=ANY,
        out_shape=jax.ShapeDtypeStruct((dp_count, TILE, columns), jnp.bfloat16),
        scratch_shapes=[pltpu.SemaphoreType.DMA],
        compiler_params=params(8),
        name="second_tiles",
    )(asked, label_tiles)

    def shift(v, by):
        return lax.ppermute(v, "label", [(i, (i + by) % PLANES) for i in range(PLANES)])

    q0 = arrived[:, :own]
    q1, q3 = shift(q0, 1), shift(q0, 3)
    mid = dp_count // 2
    q2a, q2b = shift(q1[:mid], 1), shift(q3[mid:], 3)
    second_out = lax.optimization_barrier((second_out, q1, q3))[0]
    got_second = lax.all_to_all(second_out, "dp", split_axis=0, concat_axis=0, tiled=True)
    k0 = pl.pallas_call(
        pick_kernel,
        in_specs=[SMEM, ANY],
        out_specs=[VMEM] * blocks_here,
        out_shape=[jax.ShapeDtypeStruct((tiles_each, tile_part, width), jnp.bfloat16)] * blocks_here,
        scratch_shapes=[pltpu.SemaphoreType.DMA((blocks_here,))],
        compiler_params=params(FULL),
        name="pick",
    )(slot_table, lax.optimization_barrier((got_first, q2a, q2b))[0])
    k1a, k3b = shift(k0[0], 1), shift(k0[1], 3)
    k1b, k3a = shift(k0[1], 1), shift(k0[0], 3)
    k2a, k2b = shift(k1a, 1), shift(k3b, 3)
    latents = [k0[0], k1a, k2a, k3a, k0[1], k1b, k2b, k3b]

    rows = dp_count * part
    keys = tiles_each * TILE

    def answers(*pieces):
        piece = pl.BlockSpec((dp_count, part, width), lambda p, n: (0, n, 0))
        half = pl.BlockSpec((mid, part, width), lambda p, n: (0, n, 0))
        specs = [piece, piece] if len(pieces) == 2 else [piece, half, half]
        return pl.pallas_call(
            functools.partial(answer_kernel, LOG2E / (width * kernel_width), skip),
            grid=(2, blocks_here),
            in_specs=[SMEM, SMEM] + specs + [ANY] * 10,
            out_specs=pl.BlockSpec((dp_count, 2 * own, columns), lambda p, n: (0, 0, 0)),
            out_shape=jax.ShapeDtypeStruct((dp_count, 2 * own, columns), jnp.bfloat16),
            scratch_shapes=[
                pltpu.VMEM((blocks_here, tiles_each, TILE, width), jnp.bfloat16),
                pltpu.VMEM((blocks_here, keys, columns), jnp.bfloat16),
                pltpu.SemaphoreType.DMA((blocks_here,)),
                pltpu.SemaphoreType.DMA((blocks_here,)),
            ],
            compiler_params=params(FULL),
            cost_estimate=pl.CostEstimate(
                flops=4 * blocks_here * rows * keys * (width + columns),
                transcendentals=2 * blocks_here * rows * keys,
                bytes_accessed=2 * blocks_here * keys * (width + columns),
            ),
            name="answers",
        )(y1, slot_table, *pieces, *latents, got_first, got_second)

    first = answers(arrived, q1)
    back0 = lax.all_to_all(first, "dp", split_axis=0, concat_axis=0, tiled=True)
    rest = answers(*lax.optimization_barrier((q3, q2a, q2b, first))[:3])
    back1 = lax.all_to_all(rest, "dp", split_axis=0, concat_axis=0, tiled=True)
    count0, count1 = (back.shape[0] * back.shape[1] for back in (back0, back1))
    return pl.pallas_call(
        unpack_kernel,
        in_specs=[SMEM, VMEM, VMEM],
        out_specs=VMEM,
        out_shape=jax.ShapeDtypeStruct((query_count, columns), jnp.bfloat16),
        scratch_shapes=[
            pltpu.VMEM((2 * (count0 + count1), 128), jnp.float32),
            pltpu.VMEM((2 * query_count, 128), jnp.float32),
        ],
        compiler_params=params(24),
        name="unpack",
    )(pos, back0.reshape(count0, columns), back1.reshape(count1, columns))


def solution(mesh):
    placed = (P("dp", None), P("dp", None), P("dp", None), P("dp", "label"), P("dp", None))
    return jax.shard_map(shards, mesh=mesh, in_specs=placed, out_specs=P("dp", "label"), check_vma=False)
```

time: 222 us -> 239 us (1.077)
  blocking collectives: 46.9 us -> 69.8 us
  waiting for transfers between devices: 62.7 us -> 73.2 us
  starting transfers between devices: 39.9 us -> 31.8 us
  Pallas kernels: 61 us -> 54.1 us
    all_to_all x0 -> x1, blocking collectives: none -> 32 us  [shards(): back0 = lax.all_to_all(first, 'dp', split_axis=0, concat_axis=0, tiled=True)]
    ppermute x8 -> x10, waiting for transfers between devices: 34.2 us -> 47.1 us  [shift(): lax.ppermute(v, 'label', [(i, (i + by) % PLANES) for i in range(PLANES)])]
    all_to_all x1 -> x0, starting transfers between devices: 9.68 us -> none  [shards(): back0 = lax.all_to_all(first, 'dp', split_axis=0, concat_axis=0, tiled=True)]
    all_to_all x1, blocking collectives: 46.9 us -> 37.8 us  [shards(): back1 = lax.all_to_all(rest, 'dp', split_axis=0, concat_axis=0, tiled=True)]
    pallas_call x1, Pallas kernels: 9.53 us -> 7.1 us  [shards(): pl.pallas_call(unpack_kernel, in_specs=[SMEM, VMEM, VMEM], out_specs=VMEM...]
    ppermute x8 -> x10, starting transfers between devices: 11.8 us -> 12.6 us  [shift(): lax.ppermute(v, 'label', [(i, (i + by) % PLANES) for i in range(PLANES)])]
  transfers between devices with their start and end apart: 12 -> 13, of which waited for: 7 -> 10; matrix products, arithmetic and copies ran while one was open for 3% -> 2% of each run, Pallas kernels for 17% -> 2%
where the time goes in v3:
time: 239 us; the launch traced here: 238 us
  waiting for transfers between devices  73.2 us (31%)
  blocking collectives  69.8 us (29%)
  Pallas kernels  54.1 us (23%)
  starting transfers between devices  31.8 us (13%)
  local copies, waits for them, and re-layouts  5.89 us (2%)
  other arithmetic  3.35 us (1%)
    ppermute x10, waiting for transfers between devices, shift(): lax.ppermute(v, 'label', [(i, (i + by) % PLANES) for i in range(PLANES)])  47.1 us
    all_to_all x1, blocking collectives, shards(): back1 = lax.all_to_all(rest, 'dp', split_axis=0, concat_axis=0, tiled=True)  37.8 us
    all_to_all x1, blocking collectives, shards(): back0 = lax.all_to_all(first, 'dp', split_axis=0, concat_axis=0, tiled=True)  32 us
    pallas_call x2, Pallas kernels, answers(): pl.pallas_call(functools.partial(answer_kernel, LOG2E / (width * kernel_w...  30.6 us
    all_to_all x1, waiting for transfers between devices, shards(): lax.all_to_all(sent, 'dp', split_axis=0, concat_axis=0, tiled=True)  15.9 us
    ppermute x10, starting transfers between devices, shift(): lax.ppermute(v, 'label', [(i, (i + by) % PLANES) for i in range(PLANES)])  12.6 us
    all_to_all x1, waiting for transfers between devices, shards(): lax.all_to_all(first_out, 'dp', split_axis=0, concat_axis=0, tiled=True)  10.3 us
    all_to_all x1, starting transfers between devices, shards(): lax.all_to_all(sent, 'dp', split_axis=0, concat_axis=0, tiled=True)  9.61 us
  transfers between devices with their start and end apart: 13, of which 10 were waited for; matrix products, arithmetic and copies ran while one was open for 2% of the time, Pallas kernels for 2%

profile of v3, /device:TPU:1, one launch (start us, length us, event | category | flops | bytes accessed | tf_op | source)
XLA Modules:
  0.0 238.4 jit_solution(16202200485572419041)
XLA Ops:
  0.0 9.2 %pack.1 = (bf16[32,72,256]{2,1,0:T(8,128)(2,1)}, s32[1,4096]{1,0:T(1,128)}) custom-call(s32[1]{0:T(128)} %bitcast.y_ref, s32[1,4096]{1,0:T(1,128)} %bitcast.15, s32[2,16]{1,0:T(2,128)} %list_ref.1, bf16[4096,256]{1,0:T(8,128)(2,1)} %x_ref.1), custom_call_target="tpu_custom_call" | custom-call | tf_op jit(solution)/shard_map/pack/pallas_call | solution.py:282
  9.2 0.0 copy-start
  9.2 9.6 %all-to-all-start = ((bf16[32,72,256]{2,1,0:T(8,128)(2,1)}), bf16[32,72,256]{2,1,0:T(8,128)(2,1)}, u32[]{:S(2)}, u32[]{:S(2)}) async-start(bf16[32,72,256]{2,1,0:T(8,128)(2,1)} %get-tuple-element.15), calls=%async_computation | async-start | bytes 2359296 | tf_op jit(solution)/shard_map/all_to_all | solution.py:302
  18.8 1.3 fusion
  20.1 1.3 fusion.1.latent_ref
  21.4 15.9 %all-to-all-done.refs_0_ = bf16[32,72,256]{2,1,0:T(8,128)(2,1)} async-done(((bf16[32,72,256]{2,1,0:T(8,128)(2,1)}), bf16[32,72,256]{2,1,0:T(8,128)(2,1)}, u32[]{:S(2)}, u32[]{:S(2)}) %all-to-all-start) | async-done | bytes 1179680 | tf_op jit(solution)/shard_map/all_to_all | solution.py:302
  37.2 1.1 slice.13
  38.3 0.0 copy-done
  38.3 2.5 %first_tiles.1 = bf16[32,192,256]{2,1,0:T(8,128)(2,1)} custom-call(s32[32,2]{1,0:T(8,128)S(1)} %bitcast.11, bf16[32,32,256]{2,1,0:T(8,128)(2,1)S(1)} %fusion.1.latent_ref, bf16[32,128,256]{2,1,0:T(8,128)(2,1)S(1)} %bitcast.9), custom_call_target="tpu_custom_call" | custom-call | tf_op jit(solution)/shard_map/first_tiles/pallas_call | solution.py:308
  40.8 4.6 %all-to-all-start.1 = ((bf16[32,192,256]{2,1,0:T(8,128)(2,1)}), bf16[32,192,256]{2,1,0:T(8,128)(2,1)}, u32[]{:S(2)}, u32[]{:S(2)}) async-start(bf16[32,192,256]{2,1,0:T(8,128)(2,1)} %first_tiles.1), calls=%async_computation.1 | async-start | bytes 6291456 | tf_op jit(solution)/shard_map/all_to_all | solution.py:317
  45.5 1.3 slice.16
  46.8 2.8 %collective-permute-start.2 = (bf16[32,64,256]{2,1,0:T(8,128)(2,1)S(1)}, bf16[32,64,256]{2,1,0:T(8,128)(2,1)S(1)}, u32[]{:S(2)}, u32[]{:S(2)}) collective-permute-start(bf16[32,64,256]{2,1,0:T(8,128)(2,1)S(1)} %slice.16), channel_id=1, source_target_pairs={{0,3},{1,0},{2,1},{3,2},{4,7},{5,4},{6,5},{7,6},{8,11},{9,8},{10,9... | collective-permute-start | bytes 3145736 | tf_op jit(solution)/shard_map/ppermute | solution.py:329
  49.6 0.0 collective-permute-start
  49.6 2.1 second_tiles.1
  51.7 0.0 copy-start.4
  51.7 20.1 %collective-permute-done.2.refs_0_ = bf16[32,64,256]{2,1,0:T(8,128)(2,1)S(1)} collective-permute-done((bf16[32,64,256]{2,1,0:T(8,128)(2,1)S(1)}, bf16[32,64,256]{2,1,0:T(8,128)(2,1)S(1)}, u32[]{:S(2)}, u32[]{:S(2)}) %collective-permute-start.2) | collective-permute-done | bytes 1048608 | tf_op jit(solution)/shard_map/ppermute | solution.py:329
  71.8 0.0 copy-start.3
  71.8 3.2 %collective-permute-done.refs_1_ = bf16[32,64,256]{2,1,0:T(8,128)(2,1)} collective-permute-done((bf16[32,64,256]{2,1,0:T(8,128)(2,1)S(1)}, bf16[32,64,256]{2,1,0:T(8,128)(2,1)}, u32[]{:S(2)}, u32[]{:S(2)}) %collective-permute-start) | collective-permute-done | bytes 1048608 | tf_op jit(solution)/shard_map/ppermute | solution.py:329
  75.0 10.3 %all-to-all-done.1.arrived_ref.refs_10_.refs_11_ = bf16[32,192,256]{2,1,0:T(8,128)(2,1)} async-done(((bf16[32,192,256]{2,1,0:T(8,128)(2,1)}), bf16[32,192,256]{2,1,0:T(8,128)(2,1)}, u32[]{:S(2)}, u32[]{:S(2)}) %all-to-all-start.1) | async-done | bytes 3145760 | tf_op jit(solution)/shard_map/all_to_all | solution.py:317
  85.3 5.0 %all-to-all-start.2 = ((bf16[32,128,256]{2,1,0:T(8,128)(2,1)}), bf16[32,128,256]{2,1,0:T(8,128)(2,1)}, u32[]{:S(2)}, u32[]{:S(2)}) async-start(bf16[32,128,256]{2,1,0:T(8,128)(2,1)} %second_tiles.1), calls=%async_computation.2 | async-start | bytes 4194304 | tf_op jit(solution)/shard_map/all_to_all | solution.py:336
  90.3 0.0 copy-done.4
  90.3 0.1 reshape.91
  90.4 0.0 copy-done.3
  90.5 2.8 %collective-permute-start.3 = (bf16[16,64,256]{2,1,0:T(8,128)(2,1)S(1)}, bf16[16,64,256]{2,1,0:T(8,128)(2,1)S(1)}, u32[]{:S(2)}, u32[]{:S(2)}) collective-permute-start(bf16[16,64,256]{2,1,0:T(8,128)(2,1)S(1)} %slice.18), channel_id=1, source_target_pairs={{0,3},{1,0},{2,1},{3,2},{4,7},{5,4},{6,5},{7,6},{8,11},{9,8},{10,9... | collective-permute-start | bytes 1572872 | tf_op jit(solution)/shard_map/ppermute | solution.py:329
  93.3 1.1 slice.17
  94.3 0.1 collective-permute-start.1
  94.4 0.2 convert_reduce_fusion
  94.6 0.1 reduce_sum.21
  94.7 0.6 multiply_add_fusion.slot_ref
  95.3 8.8 %collective-permute-done.3.refs_2_ = bf16[16,64,256]{2,1,0:T(8,128)(2,1)S(1)} collective-permute-done((bf16[16,64,256]{2,1,0:T(8,128)(2,1)S(1)}, bf16[16,64,256]{2,1,0:T(8,128)(2,1)S(1)}, u32[]{:S(2)}, u32[]{:S(2)}) %collective-permute-start.3) | collective-permute-done | bytes 524320 | tf_op jit(solution)/shard_map/ppermute | solution.py:329
  104.1 0.0 copy-start.5
  104.1 0.8 copy-done.5
  104.9 3.6 %collective-permute-done.1.refs_1_ = bf16[16,64,256]{2,1,0:T(8,128)(2,1)} collective-permute-done((bf16[16,64,256]{2,1,0:T(8,128)(2,1)S(1)}, bf16[16,64,256]{2,1,0:T(8,128)(2,1)}, u32[]{:S(2)}, u32[]{:S(2)}) %collective-permute-start.1) | collective-permute-done | bytes 524320 | tf_op jit(solution)/shard_map/ppermute | solution.py:329
  108.5 2.6 %pick.1 = (bf16[16,32,256]{2,1,0:T(8,128)(2,1)}, bf16[16,32,256]{2,1,0:T(8,128)(2,1)}) custom-call(s32[2,16]{1,0:T(2,128)} %multiply_add_fusion.slot_ref, bf16[32,192,256]{2,1,0:T(8,128)(2,1)} %all-to-all-done.1.arrived_ref.refs_10_.refs_11_), custom_call_target="tpu_custom_call" | custom-call | tf_op jit(solution)/shard_map/pick/pallas_call | solution.py:337
  111.1 0.1 collective-permute-start.4
  111.2 2.7 %collective-permute-start.8 = (bf16[16,32,256]{2,1,0:T(8,128)(2,1)}, bf16[16,32,256]{2,1,0:T(8,128)(2,1)S(1)}, u32[]{:S(2)}, u32[]{:S(2)}) collective-permute-start(bf16[16,32,256]{2,1,0:T(8,128)(2,1)} %get-tuple-element.18.refs_6_.refs_7_), channel_id=1, source_target_pairs={{0,3},{1,0},{2,1},{3,2},{4,7},{5,4},{6,5},{7,6},{8,11},{9,8},{10,9... | collective-permute-start | bytes 786440 | tf_op jit(solution)/shard_map/ppermute | solution.py:329
  113.8 0.0 collective-permute-start.6
  113.9 1.4 collective-permute-start.7
  115.3 3.6 %collective-permute-done.4.refs_3_.refs_4_ = bf16[16,32,256]{2,1,0:T(8,128)(2,1)S(1)} collective-permute-done((bf16[16,32,256]{2,1,0:T(8,128)(2,1)}, bf16[16,32,256]{2,1,0:T(8,128)(2,1)S(1)}, u32[]{:S(2)}, u32[]{:S(2)}) %collective-permute-start.4) | collective-permute-done | bytes 262176 | tf_op jit(solution)/shard_map/ppermute | solution.py:329
  118.9 0.0 copy-start.6
  118.9 0.7 copy-done.6
  119.6 0.0 collective-permute-start.5
  119.6 0.0 collective-permute-done.8.refs_9_.refs_10_
  119.6 0.0 copy-start.7
  119.6 2.7 %collective-permute-start.9 = (bf16[16,32,256]{2,1,0:T(8,128)(2,1)S(1)}, bf16[16,32,256]{2,1,0:T(8,128)(2,1)}, u32[]{:S(2)}, u32[]{:S(2)}) collective-permute-start(bf16[16,32,256]{2,1,0:T(8,128)(2,1)S(1)} %collective-permute-done.8.refs_9_.refs_10_), channel_id=1, source_target_pairs={{0,3},{1,0},{2,1},{3,2},{4,7},{5,4},{6,5},{7,6},{8,11},{9,8},{10,9... | collective-permute-start | bytes 786440 | tf_op jit(solution)/shard_map/ppermute | solution.py:329
  122.3 0.0 all-to-all-done.2.refs_11_.refs_12_
  122.3 1.3 collective-permute-done.6.refs_5_.refs_6_
  123.6 0.0 copy-start.8
  123.6 0.9 collective-permute-done.7.refs_7_.refs_8_
  124.5 5.6 %collective-permute-done.5.refs_4_.refs_5_ = bf16[16,32,256]{2,1,0:T(8,128)(2,1)S(1)} collective-permute-done((bf16[16,32,256]{2,1,0:T(8,128)(2,1)S(1)}, bf16[16,32,256]{2,1,0:T(8,128)(2,1)S(1)}, u32[]{:S(2)}, u32[]{:S(2)}) %collective-permute-start.5) | collective-permute-done | bytes 262176 | tf_op jit(solution)/shard_map/ppermute | solution.py:329
  130.1 0.0 copy-done.7
  130.1 0.0 copy-done.8
  130.1 0.0 copy-done.9
  130.1 0.0 copy-start.10
  130.1 0.7 copy-done.10
  130.8 0.0 collective-permute-done.9.refs_8_.refs_9_
  130.8 15.3 %answers.2 = bf16[32,128,256]{2,1,0:T(8,128)(2,1)} custom-call(s32[1]{0:T(128)} %bitcast.y_ref, s32[2,16]{1,0:T(2,128)} %multiply_add_fusion.slot_ref, bf16[32,72,256]{2,1,0:T(8,128)(2,1)} %all-to-all-done.refs_0_, bf16[32,64,256]{2,1,0:T(8,128)(2,1)} %collective-permute-done.refs_1_, bf16[16,32,256]{2,1,0:T(8,128)(2,1)} %get-tuple-element.17.refs_2_.refs_3_, ...), custom_call_target="tpu_custom_call" | custom-call | flops 8589934592 | bytes 4194304 | tf_op jit(solution)/shard_map/answers/pallas_call | solution.py:358
  146.1 15.3 %answers.3 = bf16[32,128,256]{2,1,0:T(8,128)(2,1)} custom-call(s32[1]{0:T(128)} %bitcast.y_ref, s32[2,16]{1,0:T(2,128)} %multiply_add_fusion.slot_ref, bf16[32,64,256]{2,1,0:T(8,128)(2,1)} %copy-done.3, bf16[16,64,256]{2,1,0:T(8,128)(2,1)} %collective-permute-done.1.refs_1_, bf16[16,64,256]{2,1,0:T(8,128)(2,1)} %copy-done.5, ...), custom_call_target="tpu_custom_call" | custom-call | flops 8589934592 | bytes 4194304 | tf_op jit(solution)/shard_map/answers/pallas_call | solution.py:358
  161.5 0.0 copy-start.2
  161.5 37.8 %all_to_all.25 = bf16[32,128,256]{2,1,0:T(8,128)(2,1)S(1)} all-to-all(bf16[32,128,256]{2,1,0:T(8,128)(2,1)} %answers.3), channel_id=1, replica_groups=mesh['dp'=32,'label'=4] {'dp'}, dimensions={0} | all-to-all | bytes 4194304 | tf_op jit(solution)/shard_map/all_to_all | solution.py:382
  199.3 0.0 copy-done.2
  199.3 32.0 %all_to_all.26 = bf16[32,128,256]{2,1,0:T(8,128)(2,1)S(1)} all-to-all(bf16[32,128,256]{2,1,0:T(8,128)(2,1)S(1)} %copy-done.2), channel_id=1, replica_groups=mesh['dp'=32,'label'=4] {'dp'}, dimensions={0} | all-to-all | bytes 4194304 | tf_op jit(solution)/shard_map/all_to_all | solution.py:380
  231.3 0.0 copy-done.1
  231.3 7.1 %unpack.1 = bf16[4096,256]{1,0:T(8,128)(2,1)} custom-call(s32[1,4096]{1,0:T(1,128)S(1)} %copy-done.1, bf16[4096,256]{1,0:T(8,128)(2,1)S(1)} %bitcast.8, bf16[4096,256]{1,0:T(8,128)(2,1)S(1)} %bitcast.7), custom_call_target="tpu_custom_call" | custom-call | tf_op jit(solution)/shard_map/unpack/pallas_call | solution.py:384
  (6 shorter events, 0.1 us)
Async XLA Ops:
  9.2 29.1 %copy-start = (bf16[4096,256]{1,0:T(8,128)(2,1)S(1)}, bf16[4096,256]{1,0:T(8,128)(2,1)}, u32[]{:S(2)}) copy-start(bf16[4096,256]{1,0:T(8,128)(2,1)} %param.8) | copy-start | bytes 6291460
  9.2 28.0 %all-to-all-start = ((bf16[32,72,256]{2,1,0:T(8,128)(2,1)}), bf16[32,72,256]{2,1,0:T(8,128)(2,1)}, u32[]{:S(2)}, u32[]{:S(2)}) async-start(bf16[32,72,256]{2,1,0:T(8,128)(2,1)} %get-tuple-element.15), calls=%async_computation | async-start | bytes 2359296 | tf_op jit(solution)/shard_map/all_to_all | solution.py:302
  40.8 44.4 %all-to-all-start.1 = ((bf16[32,192,256]{2,1,0:T(8,128)(2,1)}), bf16[32,192,256]{2,1,0:T(8,128)(2,1)}, u32[]{:S(2)}, u32[]{:S(2)}) async-start(bf16[32,192,256]{2,1,0:T(8,128)(2,1)} %first_tiles.1), calls=%async_computation.1 | async-start | bytes 6291456 | tf_op jit(solution)/shard_map/all_to_all | solution.py:317
  46.8 25.0 %collective-permute-start.2 = (bf16[32,64,256]{2,1,0:T(8,128)(2,1)S(1)}, bf16[32,64,256]{2,1,0:T(8,128)(2,1)S(1)}, u32[]{:S(2)}, u32[]{:S(2)}) collective-permute-start(bf16[32,64,256]{2,1,0:T(8,128)(2,1)S(1)} %slice.16), channel_id=1, source_target_pairs={{0,3},{1,0},{2,1},{3,2},{4,7},{5,4},{6,5},{7,6},{8,11},{9,8},{10,9... | collective-permute-start | bytes 3145736 | tf_op jit(solution)/shard_map/ppermute | solution.py:329
  49.6 25.4 %collective-permute-start = (bf16[32,64,256]{2,1,0:T(8,128)(2,1)S(1)}, bf16[32,64,256]{2,1,0:T(8,128)(2,1)}, u32[]{:S(2)}, u32[]{:S(2)}) collective-permute-start(bf16[32,64,256]{2,1,0:T(8,128)(2,1)S(1)} %slice.16), channel_id=1, source_target_pairs={{0,1},{1,2},{2,3},{3,0},{4,5},{5,6},{6,7},{7,4},{8,9},{9,10},{10,1... | collective-permute-start | bytes 3145736 | tf_op jit(solution)/shard_map/ppermute | solution.py:329
  51.7 38.6 %copy-start.4 = (s32[2,16]{1,0:T(2,128)S(1)}, s32[2,16]{1,0:T(2,128)}, u32[]{:S(2)}) copy-start(s32[2,16]{1,0:T(2,128)} %list_ref.1) | copy-start | bytes 388
  71.8 18.6 %copy-start.3 = (bf16[32,64,256]{2,1,0:T(8,128)(2,1)}, bf16[32,64,256]{2,1,0:T(8,128)(2,1)S(1)}, u32[]{:S(2)}) copy-start(bf16[32,64,256]{2,1,0:T(8,128)(2,1)S(1)} %collective-permute-done.2.refs_0_) | copy-start | bytes 3145732
  85.3 37.0 %all-to-all-start.2 = ((bf16[32,128,256]{2,1,0:T(8,128)(2,1)}), bf16[32,128,256]{2,1,0:T(8,128)(2,1)}, u32[]{:S(2)}, u32[]{:S(2)}) async-start(bf16[32,128,256]{2,1,0:T(8,128)(2,1)} %second_tiles.1), calls=%async_computation.2 | async-start | bytes 4194304 | tf_op jit(solution)/shard_map/all_to_all | solution.py:336
  90.5 13.7 %collective-permute-start.3 = (bf16[16,64,256]{2,1,0:T(8,128)(2,1)S(1)}, bf16[16,64,256]{2,1,0:T(8,128)(2,1)S(1)}, u32[]{:S(2)}, u32[]{:S(2)}) collective-permute-start(bf16[16,64,256]{2,1,0:T(8,128)(2,1)S(1)} %slice.18), channel_id=1, source_target_pairs={{0,3},{1,0},{2,1},{3,2},{4,7},{5,4},{6,5},{7,6},{8,11},{9,8},{10,9... | collective-permute-start | bytes 1572872 | tf_op jit(solution)/shard_map/ppermute | solution.py:329
  94.3 14.2 %collective-permute-start.1 = (bf16[16,64,256]{2,1,0:T(8,128)(2,1)S(1)}, bf16[16,64,256]{2,1,0:T(8,128)(2,1)}, u32[]{:S(2)}, u32[]{:S(2)}) collective-permute-start(bf16[16,64,256]{2,1,0:T(8,128)(2,1)S(1)} %slice.17), channel_id=1, source_target_pairs={{0,1},{1,2},{2,3},{3,0},{4,5},{5,6},{6,7},{7,4},{8,9},{9,10},{10,1... | collective-permute-start | bytes 1572872 | tf_op jit(solution)/shard_map/ppermute | solution.py:329
  104.1 0.8 copy-start.5
  111.1 7.8 %collective-permute-start.4 = (bf16[16,32,256]{2,1,0:T(8,128)(2,1)}, bf16[16,32,256]{2,1,0:T(8,128)(2,1)S(1)}, u32[]{:S(2)}, u32[]{:S(2)}) collective-permute-start(bf16[16,32,256]{2,1,0:T(8,128)(2,1)} %get-tuple-element.17.refs_2_.refs_3_), channel_id=1, source_target_pairs={{0,1},{1,2},{2,3},{3,0},{4,5},{5,6},{6,7},{7,4},{8,9},{9,10},{10,1... | collective-permute-start | bytes 786440 | tf_op jit(solution)/shard_map/ppermute | solution.py:329
  111.2 8.4 %collective-permute-start.8 = (bf16[16,32,256]{2,1,0:T(8,128)(2,1)}, bf16[16,32,256]{2,1,0:T(8,128)(2,1)S(1)}, u32[]{:S(2)}, u32[]{:S(2)}) collective-permute-start(bf16[16,32,256]{2,1,0:T(8,128)(2,1)} %get-tuple-element.18.refs_6_.refs_7_), channel_id=1, source_target_pairs={{0,3},{1,0},{2,1},{3,2},{4,7},{5,4},{6,5},{7,6},{8,11},{9,8},{10,9... | collective-permute-start | bytes 786440 | tf_op jit(solution)/shard_map/ppermute | solution.py:329
  113.8 9.8 %collective-permute-start.6 = (bf16[16,32,256]{2,1,0:T(8,128)(2,1)}, bf16[16,32,256]{2,1,0:T(8,128)(2,1)S(1)}, u32[]{:S(2)}, u32[]{:S(2)}) collective-permute-start(bf16[16,32,256]{2,1,0:T(8,128)(2,1)} %get-tuple-element.17.refs_2_.refs_3_), channel_id=1, source_target_pairs={{0,3},{1,0},{2,1},{3,2},{4,7},{5,4},{6,5},{7,6},{8,11},{9,8},{10,9... | collective-permute-start | bytes 786440 | tf_op jit(solution)/shard_map/ppermute | solution.py:329
  113.9 10.6 %collective-permute-start.7 = (bf16[16,32,256]{2,1,0:T(8,128)(2,1)}, bf16[16,32,256]{2,1,0:T(8,128)(2,1)S(1)}, u32[]{:S(2)}, u32[]{:S(2)}) collective-permute-start(bf16[16,32,256]{2,1,0:T(8,128)(2,1)} %get-tuple-element.18.refs_6_.refs_7_), channel_id=1, source_target_pairs={{0,1},{1,2},{2,3},{3,0},{4,5},{5,6},{6,7},{7,4},{8,9},{9,10},{10,1... | collective-permute-start | bytes 786440 | tf_op jit(solution)/shard_map/ppermute | solution.py:329
  118.9 0.7 copy-start.6
  119.6 10.5 %collective-permute-start.5 = (bf16[16,32,256]{2,1,0:T(8,128)(2,1)S(1)}, bf16[16,32,256]{2,1,0:T(8,128)(2,1)S(1)}, u32[]{:S(2)}, u32[]{:S(2)}) collective-permute-start(bf16[16,32,256]{2,1,0:T(8,128)(2,1)S(1)} %collective-permute-done.4.refs_3_.refs_4_), channel_id=1, source_target_pairs={{0,1},{1,2},{2,3},{3,0},{4,5},{5,6},{6,7},{7,4},{8,9},{9,10},{10,1... | collective-permute-start | bytes 786440 | tf_op jit(solution)/shard_map/ppermute | solution.py:329
  119.6 10.5 %copy-start.7 = (bf16[16,32,256]{2,1,0:T(8,128)(2,1)}, bf16[16,32,256]{2,1,0:T(8,128)(2,1)S(1)}, u32[]{:S(2)}) copy-start(bf16[16,32,256]{2,1,0:T(8,128)(2,1)S(1)} %collective-permute-done.8.refs_9_.refs_10_) | copy-start | bytes 786436
  119.6 11.2 %collective-permute-start.9 = (bf16[16,32,256]{2,1,0:T(8,128)(2,1)S(1)}, bf16[16,32,256]{2,1,0:T(8,128)(2,1)}, u32[]{:S(2)}, u32[]{:S(2)}) collective-permute-start(bf16[16,32,256]{2,1,0:T(8,128)(2,1)S(1)} %collective-permute-done.8.refs_9_.refs_10_), channel_id=1, source_target_pairs={{0,3},{1,0},{2,1},{3,2},{4,7},{5,4},{6,5},{7,6},{8,11},{9,8},{10,9... | collective-permute-start | bytes 786440 | tf_op jit(solution)/shard_map/ppermute | solution.py:329
  123.6 6.5 %copy-start.8 = (bf16[16,32,256]{2,1,0:T(8,128)(2,1)}, bf16[16,32,256]{2,1,0:T(8,128)(2,1)S(1)}, u32[]{:S(2)}) copy-start(bf16[16,32,256]{2,1,0:T(8,128)(2,1)S(1)} %collective-permute-done.6.refs_5_.refs_6_) | copy-start | bytes 786436
  124.5 5.6 %copy-start.9 = (bf16[16,32,256]{2,1,0:T(8,128)(2,1)}, bf16[16,32,256]{2,1,0:T(8,128)(2,1)S(1)}, u32[]{:S(2)}) copy-start(bf16[16,32,256]{2,1,0:T(8,128)(2,1)S(1)} %collective-permute-done.7.refs_7_.refs_8_) | copy-start | bytes 786436
  130.1 0.7 copy-start.10
  161.5 37.9 %copy-start.2 = (bf16[32,128,256]{2,1,0:T(8,128)(2,1)S(1)}, bf16[32,128,256]{2,1,0:T(8,128)(2,1)}, u32[]{:S(2)}) copy-start(bf16[32,128,256]{2,1,0:T(8,128)(2,1)} %answers.2) | copy-start | bytes 6291460
  199.3 32.0 %copy-start.1 = (s32[1,4096]{1,0:T(1,128)S(1)}, s32[1,4096]{1,0:T(1,128)}, u32[]{:S(2)}) copy-start(s32[1,4096]{1,0:T(1,128)} %get-tuple-element.14.pos_ref) | copy-start | bytes 49156

commit v4 on v3

--- a/solution.py
+++ b/solution.py
@@ -77,9 +77,8 @@
         turn = (y + PLANES - rank // part) % PLANES
         place = jnp.where(turn < 2, turn, 5 - turn)
         pos_ref[:, c * step : (c + 1) * step] = 2 * (
-            place // 2 * (2 * blocks * part)
-            + ids // 2 * (4 * part)
-            + place % 2 * (2 * part)
+            ids // 2 * (2 * PLANES * part)
+            + place * (2 * part)
             + ids % 2 * part
             + rank % part
         )
@@ -128,23 +127,18 @@
         out_ref[to, :own, lanes:] = (b * scale).astype(jnp.bfloat16).reshape(some, own, lanes)
 
 
-def first_kernel(asked_ref, latent_ref, label_ref, out_ref, sem):
+def slots_kernel(asked_ref, tile_ref, out_ref, sem):
     dests, slots = asked_ref.shape
-    part, rows = latent_ref.shape[1], label_ref.shape[1]
+    part = tile_ref.shape[1]
     for d in range(dests):
         for s in range(slots):
-            pltpu.make_async_copy(
-                latent_ref.at[asked_ref[d, s]], out_ref.at[d, pl.ds(s * part, part)], sem
-            ).start()
-        pltpu.make_async_copy(
-            label_ref.at[asked_ref[d, 0]], out_ref.at[d, pl.ds(slots * part, rows)], sem
-        ).start()
+            pltpu.make_async_copy(tile_ref.at[asked_ref[d, s]], out_ref.at[d, pl.ds(s * part, part)], sem).start()
     pltpu.make_async_copy(out_ref, out_ref, sem).wait()
 
 
-def second_kernel(asked_ref, label_ref, out_ref, sem):
+def one_slot_kernel(slot, asked_ref, tile_ref, out_ref, sem):
     for d in range(asked_ref.shape[0]):
-        pltpu.make_async_copy(label_ref.at[asked_ref[d, 1]], out_ref.at[d], sem).start()
+        pltpu.make_async_copy(tile_ref.at[asked_ref[d, slot]], out_ref.at[d], sem).start()
     pltpu.make_async_copy(out_ref, out_ref, sem).wait()
 
 
@@ -163,10 +157,9 @@
         pltpu.make_async_copy(out_ref, out_ref, sem.at[n]).wait()
 
 
-def answer_kernel(scale, skip, y_ref, slot_ref, *refs):
-    latents, (first_ref, second_ref) = refs[-15:-7], refs[-7:-5]
-    out_ref, keys, values, key_sem, sems = refs[-5:]
-    pieces = refs[:-15]
+def first_pass_kernel(scale, count, y_ref, slot_ref, *refs):
+    out_ref, total_ref, answer_ref, keys, values, key_sem, sems = refs[-7:]
+    latents, first_ref, pieces = refs[:8], refs[8], refs[9 : 9 + count]
     y = y_ref[0]
     blocks, tiles = slot_ref.shape
     rows = keys.shape[2]
@@ -182,61 +175,136 @@
 
             @pl.loop(0, tiles)
             def _(j):
-                slot = slot_ref[n, j]
                 to = values.at[n, pl.ds(pl.multiple_of(j * rows, rows), rows)]
-
-                @pl.when(slot % 2 == 0)
-                def _():
-                    pltpu.make_async_copy(first_ref.at[slot // 2, pl.ds(skip, rows)], to, sems.at[n]).start()
-
-                @pl.when(slot % 2 == 1)
-                def _():
-                    pltpu.make_async_copy(second_ref.at[slot // 2], to, sems.at[n]).start()
+                pltpu.make_async_copy(first_ref.at[slot_ref[n, j] // 2], to, sems.at[n]).start()
 
     @pl.when(piece == 0)
     def _():
         pltpu.make_async_copy(keys.at[block], keys.at[block], key_sem.at[block]).wait()
         pltpu.make_async_copy(values.at[block], values.at[block], sems.at[block]).wait()
 
+        @pl.loop(0, tiles)
+        def _(j):
+            @pl.when(slot_ref[block, j] % 2 == 1)
+            def _():
+                values[block, pl.ds(pl.multiple_of(j * rows, rows), rows), :] = jnp.zeros(
+                    (rows, values.shape[2]), values.dtype
+                )
+
     nt = (((1,), (1,)), ((), ()))
     group = 2
     span = group * rows
-    sources = out_ref.shape[0]
-    second = pieces[1][...]
-    if len(pieces) == 3:
-        second = jnp.concatenate([second, pieces[2][...]], axis=0)
-    q = jnp.where(piece == 0, pieces[0][...], second)
-    part, width = q.shape[1:]
+    first = pieces[0][...]
+    if len(pieces) == 4:
+        first = jnp.concatenate([first, pieces[1][...]], axis=0)
+    second = jnp.concatenate([pieces[-2][...], pieces[-1][...]], axis=0)
+    q = jnp.where(piece == 0, first, second)
+    sources, part, width = q.shape
     q = q.reshape(sources * part, width)
-    total = jnp.zeros((sources * part, 1), jnp.float32)
+    total = jnp.zeros((sources * part, rows), jnp.float32)
     weighted = jnp.zeros((sources * part, values.shape[2]), jnp.float32)
     for at in range(tiles // group):
         k = keys[block, at * group : (at + 1) * group].reshape(span, width)
         s = lax.dot_general(q, k, nt, preferred_element_type=jnp.float32)
         e = jnp.exp2(s * scale)
-        total = total + jnp.sum(e, axis=1, keepdims=True)
+        for g in range(group):
+            counted = (slot_ref[block, at * group + g] % 2 == 0).astype(jnp.float32)
+            total = total + e[:, g * rows : (g + 1) * rows] * counted
         weighted = weighted + jnp.dot(
             e.astype(jnp.bfloat16), values[block, at * span : (at + 1) * span], preferred_element_type=jnp.float32
         )
-    answer = (weighted / total).astype(jnp.bfloat16).reshape(sources, part, values.shape[2])
-    at = pl.multiple_of((2 * piece + block) * part, part)
-    out_ref[:, pl.ds(at, part), :] = answer
-
-
-def unpack_kernel(pos_ref, a_ref, b_ref, out_ref, table, got):
+    total = jnp.sum(total, axis=1, keepdims=True)
+    out_ref[0] = weighted
+    total_ref[0] = jnp.broadcast_to(total, total_ref.shape[1:])
+    answer_ref[...] = (weighted * (1.0 / total)).astype(jnp.bfloat16).reshape(answer_ref.shape)
+
+
+def finish_kernel(scale, turns_ref, y_ref, slot_ref, sum_ref, total_ref, *refs):
+    pieces, latents, second_ref = refs[:7], refs[7:15], refs[15]
+    out_ref, weighted, total, queries, keys, values, sems, tile_sem = refs[17:]
+    y = y_ref[0]
+    blocks, tiles = slot_ref.shape
+    rows = keys.shape[1]
+    tile_part = rows // PLANES
+    turn_no, piece = pl.program_id(0), pl.program_id(1)
+    block = turns_ref[turn_no]
+    live = (turn_no == 0) | (block != turns_ref[0])
+    sources, part, width = queries.shape[1:]
+    chunk = 256
+
+    @pl.when((piece == 0) & live)
+    def _():
+        own = pl.ds(pl.multiple_of(block * part, part), part)
+        for p in range(PLANES):
+            if p == 0:
+                pltpu.make_async_copy(pieces[p].at[:, own], queries.at[p], sems.at[p]).start()
+            else:
+                mid = sources // 2
+                for h in range(2):
+                    to = queries.at[p, pl.ds(h * mid, mid)]
+                    pltpu.make_async_copy(pieces[2 * p - 1 + h].at[:, own], to, sems.at[p]).start()
+            for at in range(0, weighted.shape[1], chunk):
+                some = pl.ds(at, chunk)
+                pltpu.make_async_copy(sum_ref.at[blocks * p + block, some], weighted.at[p, some], sems.at[p]).start()
+                pltpu.make_async_copy(total_ref.at[blocks * p + block, some], total.at[p, some], sems.at[p]).start()
+            if p > 0:
+                continue
+            for n in range(blocks):
+
+                @pl.when(block == n)
+                def _():
+                    @pl.loop(0, tiles)
+                    def _(j):
+                        slot = slot_ref[n, j]
+
+                        @pl.when(slot % 2 == 1)
+                        def _():
+                            for turn, ref in enumerate(latents[n * PLANES : (n + 1) * PLANES]):
+                                row = pl.multiple_of((y + PLANES - turn) % PLANES * tile_part, tile_part)
+                                pltpu.make_async_copy(ref.at[j], keys.at[j, pl.ds(row, tile_part)], tile_sem).start()
+                            pltpu.make_async_copy(second_ref.at[slot // 2], values.at[j], tile_sem).start()
+
+        @pl.loop(0, tiles)
+        def _(j):
+            @pl.when(slot_ref[block, j] % 2 == 1)
+            def _():
+                pltpu.make_async_copy(keys.at[j], keys.at[j], tile_sem).wait()
+                pltpu.make_async_copy(values.at[j], values.at[j], tile_sem).wait()
+
+    @pl.when(live)
+    def _():
+        for held in (queries, weighted, total):
+            pltpu.make_async_copy(held.at[piece], held.at[piece], sems.at[piece]).wait()
+        nt = (((1,), (1,)), ((), ()))
+        lanes = total.shape[2]
+
+        @pl.loop(0, tiles)
+        def _(j):
+            @pl.when(slot_ref[block, j] % 2 == 1)
+            def _():
+                q = queries[piece].reshape(sources * part, width)
+                s = lax.dot_general(q, keys[j], nt, preferred_element_type=jnp.float32)
+                e = jnp.exp2(s * scale)
+                total[piece] += jnp.sum(e, axis=1, keepdims=True)
+                weighted[piece] += jnp.dot(e.astype(jnp.bfloat16), values[j], preferred_element_type=jnp.float32)
+
+        share = 1.0 / total[piece]
+        for at in range(0, weighted.shape[2], lanes):
+            out_ref[:, :, at : at + lanes] = (
+                (weighted[piece, :, at : at + lanes] * share).astype(jnp.bfloat16).reshape(sources, part, lanes)
+            )
+
+
+def unpack_kernel(pos_ref, in_ref, out_ref, table, got):
     lanes = 128
     step = 256
-    start = 0
-    for ref in (a_ref, b_ref):
-
-        @pl.loop(0, ref.shape[0] // step)
-        def _(c):
-            at = pl.ds(pl.multiple_of(c * step, step), step)
-            to = pl.multiple_of(2 * (c * step + start), 2 * step)
-            table[pl.ds(to, step, stride=2), :] = ref[at, :lanes].astype(jnp.float32)
-            table[pl.ds(to + 1, step, stride=2), :] = ref[at, lanes:].astype(jnp.float32)
-
-        start += ref.shape[0]
+
+    @pl.loop(0, in_ref.shape[0] // step)
+    def _(c):
+        at = pl.ds(pl.multiple_of(c * step, step), step)
+        to = pl.multiple_of(2 * c * step, 2 * step)
+        table[pl.ds(to, step, stride=2), :] = in_ref[at, :lanes].astype(jnp.float32)
+        table[pl.ds(to + 1, step, stride=2), :] = in_ref[at, lanes:].astype(jnp.float32)
 
     count = out_ref.shape[0]
 
@@ -304,36 +372,31 @@
 
     quarter = lax.dynamic_slice_in_dim(anchor_latent.reshape(tiles_here, TILE, width), y * tile_part, tile_part, axis=1)
     label_tiles = anchor_labels.reshape(tiles_here, TILE, columns)
-    skip = slots * tile_part
-    first_out = pl.pallas_call(
-        first_kernel,
-        in_specs=[SMEM, VMEM, VMEM],
-        out_specs=ANY,
-        out_shape=jax.ShapeDtypeStruct((dp_count, skip + TILE, columns), jnp.bfloat16),
-        scratch_shapes=[pltpu.SemaphoreType.DMA],
-        compiler_params=params(8),
-        name="first_tiles",
-    )(asked, unit_rows(quarter), label_tiles)
-    got_first = lax.all_to_all(first_out, "dp", split_axis=0, concat_axis=0, tiled=True)
-    second_out = pl.pallas_call(
-        second_kernel,
-        in_specs=[SMEM, VMEM],
-        out_specs=ANY,
-        out_shape=jax.ShapeDtypeStruct((dp_count, TILE, columns), jnp.bfloat16),
-        scratch_shapes=[pltpu.SemaphoreType.DMA],
-        compiler_params=params(8),
-        name="second_tiles",
-    )(asked, label_tiles)
+
+    def exchange(v):
+        return lax.all_to_all(v, "dp", split_axis=0, concat_axis=0, tiled=True)
+
+    def tiles_out(kernel, tiles, rows):
+        return pl.pallas_call(
+            kernel,
+            in_specs=[SMEM, VMEM],
+            out_specs=ANY,
+            out_shape=jax.ShapeDtypeStruct((dp_count, rows, tiles.shape[2]), jnp.bfloat16),
+            scratch_shapes=[pltpu.SemaphoreType.DMA],
+            compiler_params=params(8),
+        )(asked, tiles)
+
+    got_latents = exchange(tiles_out(slots_kernel, unit_rows(quarter), slots * tile_part))
+    first_out = tiles_out(functools.partial(one_slot_kernel, 0), label_tiles, TILE)
+    second_out = tiles_out(functools.partial(one_slot_kernel, 1), label_tiles, TILE)
 
     def shift(v, by):
         return lax.ppermute(v, "label", [(i, (i + by) % PLANES) for i in range(PLANES)])
 
-    q0 = arrived[:, :own]
-    q1, q3 = shift(q0, 1), shift(q0, 3)
     mid = dp_count // 2
-    q2a, q2b = shift(q1[:mid], 1), shift(q3[mid:], 3)
-    second_out = lax.optimization_barrier((second_out, q1, q3))[0]
-    got_second = lax.all_to_all(second_out, "dp", split_axis=0, concat_axis=0, tiled=True)
+    q0a, q0b = arrived[:mid, :own], arrived[mid:, :own]
+    q1a, q3b, q1b, q3a = shift(q0a, 1), shift(q0b, 3), shift(q0b, 1), shift(q0a, 3)
+    got_first = exchange(first_out)
     k0 = pl.pallas_call(
         pick_kernel,
         in_specs=[SMEM, ANY],
@@ -342,57 +405,100 @@
         scratch_shapes=[pltpu.SemaphoreType.DMA((blocks_here,))],
         compiler_params=params(FULL),
         name="pick",
-    )(slot_table, lax.optimization_barrier((got_first, q2a, q2b))[0])
+    )(slot_table, got_latents)
     k1a, k3b = shift(k0[0], 1), shift(k0[1], 3)
     k1b, k3a = shift(k0[1], 1), shift(k0[0], 3)
     k2a, k2b = shift(k1a, 1), shift(k3b, 3)
+    got_second = exchange(second_out)
     latents = [k0[0], k1a, k2a, k3a, k0[1], k1b, k2b, k3b]
+    q2a, q2b = shift(q1a, 1), shift(q3b, 3)
 
     rows = dp_count * part
     keys = tiles_each * TILE
-
-    def answers(*pieces):
+    scale = LOG2E / (width * kernel_width)
+
+    def first_pass(begin, pieces, sums):
         piece = pl.BlockSpec((dp_count, part, width), lambda p, n: (0, n, 0))
         half = pl.BlockSpec((mid, part, width), lambda p, n: (0, n, 0))
-        specs = [piece, piece] if len(pieces) == 2 else [piece, half, half]
+        specs = [piece, half, half] if len(pieces) == 3 else [half] * 4
+        given = 2 + 9 + len(pieces)
         return pl.pallas_call(
-            functools.partial(answer_kernel, LOG2E / (width * kernel_width), skip),
+            functools.partial(first_pass_kernel, scale, len(pieces)),
             grid=(2, blocks_here),
-            in_specs=[SMEM, SMEM] + specs + [ANY] * 10,
-            out_specs=pl.BlockSpec((dp_count, 2 * own, columns), lambda p, n: (0, 0, 0)),
-            out_shape=jax.ShapeDtypeStruct((dp_count, 2 * own, columns), jnp.bfloat16),
+            in_specs=[SMEM, SMEM] + [ANY] * 9 + specs + [ANY] * len(sums),
+            out_specs=[
+                pl.BlockSpec((1, rows, columns), lambda p, n: (blocks_here * (begin + p) + n, 0, 0)),
+                pl.BlockSpec((1, rows, 128), lambda p, n: (blocks_here * (begin + p) + n, 0, 0)),
+                pl.BlockSpec((dp_count, part, columns), lambda p, n: (0, blocks_here * (begin + p) + n, 0)),
+            ],
+            out_shape=[
+                jax.ShapeDtypeStruct((PLANES * blocks_here, rows, columns), jnp.float32),
+                jax.ShapeDtypeStruct((PLANES * blocks_here, rows, 128), jnp.float32),
+                jax.ShapeDtypeStruct((dp_count, PLANES * own, columns), jnp.bfloat16),
+            ],
             scratch_shapes=[
                 pltpu.VMEM((blocks_here, tiles_each, TILE, width), jnp.bfloat16),
                 pltpu.VMEM((blocks_here, keys, columns), jnp.bfloat16),
                 pltpu.SemaphoreType.DMA((blocks_here,)),
                 pltpu.SemaphoreType.DMA((blocks_here,)),
             ],
+            input_output_aliases={given + i: i for i in range(len(sums))},
             compiler_params=params(FULL),
             cost_estimate=pl.CostEstimate(
                 flops=4 * blocks_here * rows * keys * (width + columns),
                 transcendentals=2 * blocks_here * rows * keys,
                 bytes_accessed=2 * blocks_here * keys * (width + columns),
             ),
-            name="answers",
-        )(y1, slot_table, *pieces, *latents, got_first, got_second)
-
-    first = answers(arrived, q1)
-    back0 = lax.all_to_all(first, "dp", split_axis=0, concat_axis=0, tiled=True)
-    rest = answers(*lax.optimization_barrier((q3, q2a, q2b, first))[:3])
-    back1 = lax.all_to_all(rest, "dp", split_axis=0, concat_axis=0, tiled=True)
-    count0, count1 = (back.shape[0] * back.shape[1] for back in (back0, back1))
+            name="first_pass",
+        )(y1, slot_table, *latents, got_first, *pieces, *sums)
+
+    sums = first_pass(0, (arrived, q1a, q1b), ())
+    *sums, answers = first_pass(2, (q3a, q3b, q2a, q2b), sums)
+
+    has = jnp.sum(slot_table % 2, axis=1) > 0
+    lead = jnp.where(has[0], 0, jnp.where(has[1], 1, 0))
+    turns = jnp.stack([lead, jnp.where(has[0] & has[1], 1, lead)]).astype(jnp.int32)
+
+    def answer_block(n, p, t):
+        repeated = (n > 0) & (t[n] == t[0])
+        return (0, jnp.where(repeated, blocks_here * (PLANES - 1) + t[0], blocks_here * p + t[n]), 0)
+
+    answers = pl.pallas_call(
+        functools.partial(finish_kernel, scale),
+        grid_spec=pltpu.PrefetchScalarGridSpec(
+            num_scalar_prefetch=1,
+            grid=(blocks_here, PLANES),
+            in_specs=[SMEM, SMEM] + [ANY] * 19,
+            out_specs=pl.BlockSpec((dp_count, part, columns), answer_block),
+            scratch_shapes=[
+                pltpu.VMEM((PLANES, rows, columns), jnp.float32),
+                pltpu.VMEM((PLANES, rows, 128), jnp.float32),
+                pltpu.VMEM((PLANES, dp_count, part, width), jnp.bfloat16),
+                pltpu.VMEM((tiles_each, TILE, width), jnp.bfloat16),
+                pltpu.VMEM((tiles_each, TILE, columns), jnp.bfloat16),
+                pltpu.SemaphoreType.DMA((PLANES,)),
+                pltpu.SemaphoreType.DMA,
+            ],
+        ),
+        out_shape=jax.ShapeDtypeStruct((dp_count, PLANES * own, columns), jnp.bfloat16),
+        input_output_aliases={5 + 7 + 9: 0},
+        compiler_params=params(FULL),
+        name="finish",
+    )(turns, y1, slot_table, *sums, arrived, q1a, q1b, q3a, q3b, q2a, q2b, *latents, got_second, answers)
+    back = exchange(answers)
+    count = back.shape[0] * back.shape[1]
     return pl.pallas_call(
         unpack_kernel,
-        in_specs=[SMEM, VMEM, VMEM],
+        in_specs=[SMEM, VMEM],
         out_specs=VMEM,
         out_shape=jax.ShapeDtypeStruct((query_count, columns), jnp.bfloat16),
         scratch_shapes=[
-            pltpu.VMEM((2 * (count0 + count1), 128), jnp.float32),
+            pltpu.VMEM((2 * count, 128), jnp.float32),
             pltpu.VMEM((2 * query_count, 128), jnp.float32),
         ],
         compiler_params=params(24),
         name="unpack",
-    )(pos, back0.reshape(count0, columns), back1.reshape(count1, columns))
+    )(pos, back.reshape(count, columns))
 
 
 def solution(mesh):

time: 239 us -> 227 us (0.950)
  waiting for transfers between devices: 73.2 us -> 48.2 us
  Pallas kernels: 54.1 us -> 66.3 us
  blocking collectives: 69.8 us -> 59 us
  starting transfers between devices: 31.8 us -> 38.2 us
  between operations: 0.22 us -> 2.9 us
  local copies, waits for them, and re-layouts: 5.89 us -> 8.51 us
    ppermute x10 -> x12, waiting for transfers between devices: 47.1 us -> 6.5 us  [shift(): lax.ppermute(v, 'label', [(i, (i + by) % PLANES) for i in range(PLANES)])]
    all_to_all x2 -> x3, waiting for transfers between devices: 10.3 us -> 23.8 us  [exchange(): return lax.all_to_all(v, 'dp', split_axis=0, concat_axis=0, tiled=True)]
    pallas_call x5 -> x7, Pallas kernels: 42.3 us -> 54.5 us  [the longest x2 31.6 us: first_pass(): pl.pallas_call(functools.partial(first_pass_kernel, scale, len(pieces)),...]
    all_to_all x2 -> x1, blocking collectives: 69.8 us -> 59 us  [exchange(): return lax.all_to_all(v, 'dp', split_axis=0, concat_axis=0, tiled=True)]
    all_to_all x2 -> x3, starting transfers between devices: 9.65 us -> 13.6 us  [exchange(): return lax.all_to_all(v, 'dp', split_axis=0, concat_axis=0, tiled=True)]
    ppermute x10 -> x12, starting transfers between devices: 12.6 us -> 15 us  [shift(): lax.ppermute(v, 'label', [(i, (i + by) % PLANES) for i in range(PLANES)])]
  transfers between devices with their start and end apart: 13 -> 16, of which waited for: 10 -> 6; matrix products, arithmetic and copies ran while one was open for 2% -> 2% of each run, Pallas kernels for 2% -> 18%
where the time goes in v4:
time: 227 us; the launch traced here: 225 us
  Pallas kernels  66.3 us (29%)
  blocking collectives  59 us (26%)
  waiting for transfers between devices  48.2 us (21%)
  starting transfers between devices  38.2 us (17%)
  local copies, waits for them, and re-layouts  8.51 us (4%)
  between operations  2.9 us (1%)
  other arithmetic  2.44 us (1%)
    all_to_all x1, blocking collectives, exchange(): return lax.all_to_all(v, 'dp', split_axis=0, concat_axis=0, tiled=True)  59 us
    pallas_call x2, Pallas kernels, first_pass(): pl.pallas_call(functools.partial(first_pass_kernel, scale, len(pieces)),...  31.6 us
    all_to_all x3, waiting for transfers between devices, exchange(): return lax.all_to_all(v, 'dp', split_axis=0, concat_axis=0, tiled=True)  23.8 us
    all_to_all x1, waiting for transfers between devices, shards(): lax.all_to_all(sent, 'dp', split_axis=0, concat_axis=0, tiled=True)  17.9 us
    ppermute x12, starting transfers between devices, shift(): lax.ppermute(v, 'label', [(i, (i + by) % PLANES) for i in range(PLANES)])  15 us
    all_to_all x3, starting transfers between devices, exchange(): return lax.all_to_all(v, 'dp', split_axis=0, concat_axis=0, tiled=True)  13.6 us
    all_to_all x1, starting transfers between devices, shards(): lax.all_to_all(sent, 'dp', split_axis=0, concat_axis=0, tiled=True)  9.61 us
    pallas_call x1, Pallas kernels, shards(): pl.pallas_call(functools.partial(pack_kernel, blocks, part, tiles_here),...  9.18 us
  transfers between devices with their start and end apart: 16, of which 6 were waited for; matrix products, arithmetic and copies ran while one was open for 2% of the time, Pallas kernels for 18%

profile of v4, /device:TPU:1, one launch (start us, length us, event | category | flops | bytes accessed | tf_op | source)
XLA Modules:
  0.0 225.5 jit_solution(8134981928789156587)
XLA Ops:
  0.0 9.2 %pack.1 = (bf16[32,72,256]{2,1,0:T(8,128)(2,1)}, s32[1,4096]{1,0:T(1,128)}) custom-call(s32[1]{0:T(128)} %bitcast.y_ref, s32[1,4096]{1,0:T(1,128)} %bitcast.18, s32[2,16]{1,0:T(2,128)} %list_ref.1, bf16[4096,256]{1,0:T(8,128)(2,1)} %x_ref.1), custom_call_target="tpu_custom_call" | custom-call | tf_op jit(solution)/shard_map/pack/pallas_call | solution.py:350
  9.2 0.0 copy-start.7
  9.2 9.6 %all-to-all-start = ((bf16[32,72,256]{2,1,0:T(8,128)(2,1)}), bf16[32,72,256]{2,1,0:T(8,128)(2,1)}, u32[]{:S(2)}, u32[]{:S(2)}) async-start(bf16[32,72,256]{2,1,0:T(8,128)(2,1)} %get-tuple-element.16), calls=%async_computation | async-start | bytes 2359296 | tf_op jit(solution)/shard_map/all_to_all | solution.py:370
  18.8 0.0 copy-done.7
  18.8 0.2 fusion
  19.1 0.2 fusion.1.tile_ref
  19.3 0.0 copy-start
  19.3 17.9 %all-to-all-done.refs_9_.refs_0_ = bf16[32,72,256]{2,1,0:T(8,128)(2,1)} async-done(((bf16[32,72,256]{2,1,0:T(8,128)(2,1)}), bf16[32,72,256]{2,1,0:T(8,128)(2,1)}, u32[]{:S(2)}, u32[]{:S(2)}) %all-to-all-start) | async-done | bytes 1179680 | tf_op jit(solution)/shard_map/all_to_all | solution.py:370
  37.2 1.1 slice.19
  38.3 1.8 shard_map.55
  40.1 3.9 %all-to-all-start.1 = ((bf16[32,64,256]{2,1,0:T(8,128)(2,1)}), bf16[32,64,256]{2,1,0:T(8,128)(2,1)S(1)}, u32[]{:S(2)}, u32[]{:S(2)}) async-start(bf16[32,64,256]{2,1,0:T(8,128)(2,1)} %shard_map.55), calls=%async_computation.1 | async-start | bytes 2097152 | tf_op jit(solution)/shard_map/all_to_all | solution.py:377
  44.0 3.6 %shard_map.56 = bf16[32,128,256]{2,1,0:T(8,128)(2,1)S(1)} custom-call(s32[32,2]{1,0:T(8,128)S(1)} %bitcast.14, bf16[32,128,256]{2,1,0:T(8,128)(2,1)S(1)} %bitcast.11), custom_call_target="tpu_custom_call" | custom-call | tf_op jit(solution)/shard_map/pallas_call | solution.py:380
  47.7 0.0 copy-start.2
  47.7 1.3 copy-done.2
  49.0 11.9 %all-to-all-done.1.arrived_ref = bf16[32,64,256]{2,1,0:T(8,128)(2,1)S(1)} async-done(((bf16[32,64,256]{2,1,0:T(8,128)(2,1)}), bf16[32,64,256]{2,1,0:T(8,128)(2,1)S(1)}, u32[]{:S(2)}, u32[]{:S(2)}) %all-to-all-start.1) | async-done | bytes 1048608 | tf_op jit(solution)/shard_map/all_to_all | solution.py:377
  60.9 4.5 %all-to-all-start.2 = ((bf16[32,128,256]{2,1,0:T(8,128)(2,1)}), bf16[32,128,256]{2,1,0:T(8,128)(2,1)}, u32[]{:S(2)}, u32[]{:S(2)}) async-start(bf16[32,128,256]{2,1,0:T(8,128)(2,1)} %copy-done.2), calls=%async_computation.2 | async-start | bytes 4194304 | tf_op jit(solution)/shard_map/all_to_all | solution.py:377
  65.5 0.0 copy-done.15
  65.5 0.1 reshape.88
  65.6 2.3 %fusion.5 = (bf16[16,64,256]{2,1,0:T(8,128)(2,1)}, bf16[16,64,256]{2,1,0:T(8,128)(2,1)}) fusion(bf16[32,72,256]{2,1,0:T(8,128)(2,1)} %all-to-all-done.refs_9_.refs_0_), kind=kLoop, calls=%fused_computation.24 | loop fusion | bytes 2097152 | tf_op jit(solution)/shard_map/slice | solution.py:397
  67.9 2.7 %collective-permute-start.7 = (bf16[16,64,256]{2,1,0:T(8,128)(2,1)}, bf16[16,64,256]{2,1,0:T(8,128)(2,1)}, u32[]{:S(2)}, u32[]{:S(2)}) collective-permute-start(bf16[16,64,256]{2,1,0:T(8,128)(2,1)} %get-tuple-element.27), channel_id=1, source_target_pairs={{0,3},{1,0},{2,1},{3,2},{4,7},{5,4},{6,5},{7,6},{8,11},{9,8},{10,9... | collective-permute-start | bytes 1572872 | tf_op jit(solution)/shard_map/ppermute | solution.py:394
  70.6 0.0 collective-permute-start.8
  70.6 0.2 convert_reduce_fusion
  70.8 0.1 reduce_sum.30
  70.9 1.2 fusion.4
  72.1 2.6 %pick.1 = (bf16[16,32,256]{2,1,0:T(8,128)(2,1)}, bf16[16,32,256]{2,1,0:T(8,128)(2,1)}) custom-call(s32[2,16]{1,0:T(2,128)} %get-tuple-element.26.slot_ref, bf16[32,64,256]{2,1,0:T(8,128)(2,1)} %copy-done.6), custom_call_target="tpu_custom_call" | custom-call | tf_op jit(solution)/shard_map/pick/pallas_call | solution.py:400
  74.7 0.1 collective-permute-start
  74.8 2.7 %collective-permute-start.4 = (bf16[16,32,256]{2,1,0:T(8,128)(2,1)}, bf16[16,32,256]{2,1,0:T(8,128)(2,1)S(1)}, u32[]{:S(2)}, u32[]{:S(2)}) collective-permute-start(bf16[16,32,256]{2,1,0:T(8,128)(2,1)} %get-tuple-element.18.refs_4_.refs_11_), channel_id=1, source_target_pairs={{0,3},{1,0},{2,1},{3,2},{4,7},{5,4},{6,5},{7,6},{8,11},{9,8},{10,9... | collective-permute-start | bytes 786440 | tf_op jit(solution)/shard_map/ppermute | solution.py:394
  77.5 0.0 collective-permute-start.11
  77.5 1.6 copy-done.1
  79.1 0.7 copy-done.4
  79.8 2.2 shard_map.57
  82.0 11.9 %all-to-all-done.2.refs_8_ = bf16[32,128,256]{2,1,0:T(8,128)(2,1)} async-done(((bf16[32,128,256]{2,1,0:T(8,128)(2,1)}), bf16[32,128,256]{2,1,0:T(8,128)(2,1)}, u32[]{:S(2)}, u32[]{:S(2)}) %all-to-all-start.2) | async-done | bytes 2097184 | tf_op jit(solution)/shard_map/all_to_all | solution.py:377
  93.9 5.2 %all-to-all-start.3 = ((bf16[32,128,256]{2,1,0:T(8,128)(2,1)}), bf16[32,128,256]{2,1,0:T(8,128)(2,1)}, u32[]{:S(2)}, u32[]{:S(2)}) async-start(bf16[32,128,256]{2,1,0:T(8,128)(2,1)} %shard_map.57), calls=%async_computation.3 | async-start | bytes 4194304 | tf_op jit(solution)/shard_map/all_to_all | solution.py:377
  99.1 0.0 collective-permute-done.7.refs_10_.refs_4_
  99.1 2.8 %collective-permute-start.2 = (bf16[16,32,256]{2,1,0:T(8,128)(2,1)S(1)}, bf16[16,32,256]{2,1,0:T(8,128)(2,1)S(1)}, u32[]{:S(2)}, u32[]{:S(2)}) collective-permute-start(bf16[16,32,256]{2,1,0:T(8,128)(2,1)S(1)} %copy-done.8), channel_id=1, source_target_pairs={{0,3},{1,0},{2,1},{3,2},{4,7},{5,4},{6,5},{7,6},{8,11},{9,8},{10,9... | collective-permute-start | bytes 786440 | tf_op jit(solution)/shard_map/ppermute | solution.py:394
  101.9 0.0 collective-permute-done.8.refs_10_.refs_1_
  101.9 0.0 collective-permute-start.3
  101.9 0.0 collective-permute-done.refs_1_.refs_8_
  101.9 0.0 copy-start.10
  101.9 0.1 collective-permute-start.1
  102.0 0.0 collective-permute-done.4.refs_7_.refs_14_
  102.0 2.6 %collective-permute-start.5 = (bf16[16,32,256]{2,1,0:T(8,128)(2,1)S(1)}, bf16[16,32,256]{2,1,0:T(8,128)(2,1)}, u32[]{:S(2)}, u32[]{:S(2)}) collective-permute-start(bf16[16,32,256]{2,1,0:T(8,128)(2,1)S(1)} %collective-permute-done.4.refs_7_.refs_14_), channel_id=1, source_target_pairs={{0,3},{1,0},{2,1},{3,2},{4,7},{5,4},{6,5},{7,6},{8,11},{9,8},{10,9... | collective-permute-start | bytes 786440 | tf_op jit(solution)/shard_map/ppermute | solution.py:394
  104.7 0.6 fusion.6
  107.8 0.6 pad_add_fusion.turns_ref
  108.5 0.0 collective-permute-done.11.refs_11_.refs_2_
  108.5 1.4 collective-permute-start.6
  109.8 0.0 collective-permute-done.2.refs_3_.refs_10_
  109.8 0.1 collective-permute-start.9
  109.9 0.4 collective-permute-done.3.refs_5_.refs_12_
  110.4 2.4 %collective-permute-start.10 = (bf16[16,64,256]{2,1,0:T(8,128)(2,1)}, bf16[16,64,256]{2,1,0:T(8,128)(2,1)}, u32[]{:S(2)}, u32[]{:S(2)}) collective-permute-start(bf16[16,64,256]{2,1,0:T(8,128)(2,1)} %collective-permute-done.7.refs_10_.refs_4_), channel_id=1, source_target_pairs={{0,3},{1,0},{2,1},{3,2},{4,7},{5,4},{6,5},{7,6},{8,11},{9,8},{10,9... | collective-permute-start | bytes 1572872 | tf_op jit(solution)/shard_map/ppermute | solution.py:394
  112.8 3.2 %collective-permute-done.1.refs_2_.refs_9_ = bf16[16,32,256]{2,1,0:T(8,128)(2,1)S(1)} collective-permute-done((bf16[16,32,256]{2,1,0:T(8,128)(2,1)S(1)}, bf16[16,32,256]{2,1,0:T(8,128)(2,1)S(1)}, u32[]{:S(2)}, u32[]{:S(2)}) %collective-permute-start.1) | collective-permute-done | bytes 262176 | tf_op jit(solution)/shard_map/ppermute | solution.py:394
  116.0 0.0 copy-done.12
  116.0 0.7 copy-done.14
  116.7 0.0 collective-permute-done.5.refs_6_.refs_13_
  116.7 15.8 %first_pass.2 = (f32[8,1024,256]{2,1,0:T(8,128)}, f32[8,1024,128]{2,1,0:T(8,128)}, bf16[32,256,256]{2,1,0:T(8,128)(2,1)}) custom-call(s32[1]{0:T(128)} %bitcast.y_ref, s32[2,16]{1,0:T(2,128)} %get-tuple-element.26.slot_ref, bf16[16,32,256]{2,1,0:T(8,128)(2,1)} %get-tuple-element.17.refs_0_.refs_7_, bf16[16,32,256]{2,1,0:T(8,128)(2,1)} %copy-done.10, ...), custom_call_target="tpu_custom_call" | custom-call | flops 8589934592 | bytes 4194304 | tf_op jit(solution)/shard_map/first_pass/pallas_call | solution.py:425
  132.5 0.0 collective-permute-done.6.refs_9_.refs_3_
  132.5 0.0 collective-permute-done.9.refs_11_.refs_5_
  132.5 2.8 %collective-permute-done.10.refs_12_.refs_6_ = bf16[16,64,256]{2,1,0:T(8,128)(2,1)} collective-permute-done((bf16[16,64,256]{2,1,0:T(8,128)(2,1)}, bf16[16,64,256]{2,1,0:T(8,128)(2,1)}, u32[]{:S(2)}, u32[]{:S(2)}) %collective-permute-start.10) | collective-permute-done | bytes 524320 | tf_op jit(solution)/shard_map/ppermute | solution.py:394
  135.3 15.8 %first_pass.3 = (f32[8,1024,256]{2,1,0:T(8,128)}, f32[8,1024,128]{2,1,0:T(8,128)}, bf16[32,256,256]{2,1,0:T(8,128)(2,1)}) custom-call(s32[1]{0:T(128)} %bitcast.y_ref, s32[2,16]{1,0:T(2,128)} %get-tuple-element.26.slot_ref, bf16[16,32,256]{2,1,0:T(8,128)(2,1)} %get-tuple-element.17.refs_0_.refs_7_, ...), custom_call_target="tpu_custom_call", output_to_operand_aliasing={{0}: (15, {}), {1}: (16, {}), {2}: (17, {})} | custom-call | flops 8589934592 | bytes 4194304 | tf_op jit(solution)/shard_map/first_pass/pallas_call | solution.py:425
  151.2 0.0 all-to-all-done.3.refs_15_
  151.2 8.2 %finish.1 = bf16[32,256,256]{2,1,0:T(8,128)(2,1)} custom-call(s32[2]{0:T(128)} %pad_add_fusion.turns_ref, s32[1]{0:T(128)} %bitcast.y_ref, s32[2,16]{1,0:T(2,128)} %get-tuple-element.26.slot_ref, f32[8,1024,256]{2,1,0:T(8,128)} %get-tuple-element.22.sum_ref, f32[8,1024,128]{2,1,0:T(8,128)} %get-tuple-element.23.total_ref, ...), custom_call_target="tpu_custom_call", output_to_operand_aliasing={{}: (21, {})} | custom-call | tf_op jit(solution)/shard_map/finish/pallas_call | solution.py:466
  159.4 0.0 copy-start.5
  159.4 59.0 %all_to_all.25 = bf16[32,256,256]{2,1,0:T(8,128)(2,1)S(1)} all-to-all(bf16[32,256,256]{2,1,0:T(8,128)(2,1)} %finish.1), channel_id=1, replica_groups=mesh['dp'=32,'label'=4] {'dp'}, dimensions={0} | all-to-all | bytes 8388608 | tf_op jit(solution)/shard_map/all_to_all | solution.py:377
  218.4 7.1 %unpack.1 = bf16[4096,256]{1,0:T(8,128)(2,1)} custom-call(s32[1,4096]{1,0:T(1,128)S(1)} %copy-done.5, bf16[8192,256]{1,0:T(8,128)(2,1)S(1)} %bitcast.10), custom_call_target="tpu_custom_call" | custom-call | tf_op jit(solution)/shard_map/unpack/pallas_call | solution.py:490
  (26 shorter events, 0.1 us)
Async XLA Ops:
  9.2 9.6 %copy-start.7 = (bf16[4096,256]{1,0:T(8,128)(2,1)S(1)}, bf16[4096,256]{1,0:T(8,128)(2,1)}, u32[]{:S(2)}) copy-start(bf16[4096,256]{1,0:T(8,128)(2,1)} %param.7) | copy-start | bytes 6291460
  9.2 28.0 %all-to-all-start = ((bf16[32,72,256]{2,1,0:T(8,128)(2,1)}), bf16[32,72,256]{2,1,0:T(8,128)(2,1)}, u32[]{:S(2)}, u32[]{:S(2)}) async-start(bf16[32,72,256]{2,1,0:T(8,128)(2,1)} %get-tuple-element.16), calls=%async_computation | async-start | bytes 2359296 | tf_op jit(solution)/shard_map/all_to_all | solution.py:370
  19.3 24.8 %copy-start = (bf16[4096,256]{1,0:T(8,128)(2,1)S(1)}, bf16[4096,256]{1,0:T(8,128)(2,1)}, u32[]{:S(2)}) copy-start(bf16[4096,256]{1,0:T(8,128)(2,1)} %param.8) | copy-start | bytes 6291460
  38.3 9.4 %copy-start.3 = (s32[32,1,2]{2,1,0:T(1,128)}, s32[32,1,2]{2,1,0:T(1,128)S(1)}, u32[]{:S(2)}) copy-start(s32[32,1,2]{2,1,0:T(1,128)S(1)} %convert_element_type.19) | copy-start | bytes 772
  40.1 20.8 %all-to-all-start.1 = ((bf16[32,64,256]{2,1,0:T(8,128)(2,1)}), bf16[32,64,256]{2,1,0:T(8,128)(2,1)S(1)}, u32[]{:S(2)}, u32[]{:S(2)}) async-start(bf16[32,64,256]{2,1,0:T(8,128)(2,1)} %shard_map.55), calls=%async_computation.1 | async-start | bytes 2097152 | tf_op jit(solution)/shard_map/all_to_all | solution.py:377
  47.7 1.3 copy-start.2
  49.0 16.5 %copy-start.15 = (s32[2,16]{1,0:T(2,128)S(1)}, s32[2,16]{1,0:T(2,128)}, u32[]{:S(2)}) copy-start(s32[2,16]{1,0:T(2,128)} %list_ref.1) | copy-start | bytes 388
  60.9 4.7 %copy-start.6 = (bf16[32,64,256]{2,1,0:T(8,128)(2,1)}, bf16[32,64,256]{2,1,0:T(8,128)(2,1)S(1)}, u32[]{:S(2)}) copy-start(bf16[32,64,256]{2,1,0:T(8,128)(2,1)S(1)} %all-to-all-done.1.arrived_ref) | copy-start | bytes 3145732
  60.9 32.9 %all-to-all-start.2 = ((bf16[32,128,256]{2,1,0:T(8,128)(2,1)}), bf16[32,128,256]{2,1,0:T(8,128)(2,1)}, u32[]{:S(2)}, u32[]{:S(2)}) async-start(bf16[32,128,256]{2,1,0:T(8,128)(2,1)} %copy-done.2), calls=%async_computation.2 | async-start | bytes 4194304 | tf_op jit(solution)/shard_map/all_to_all | solution.py:377
  67.9 31.2 %collective-permute-start.7 = (bf16[16,64,256]{2,1,0:T(8,128)(2,1)}, bf16[16,64,256]{2,1,0:T(8,128)(2,1)}, u32[]{:S(2)}, u32[]{:S(2)}) collective-permute-start(bf16[16,64,256]{2,1,0:T(8,128)(2,1)} %get-tuple-element.27), channel_id=1, source_target_pairs={{0,3},{1,0},{2,1},{3,2},{4,7},{5,4},{6,5},{7,6},{8,11},{9,8},{10,9... | collective-permute-start | bytes 1572872 | tf_op jit(solution)/shard_map/ppermute | solution.py:394
  70.6 31.2 %collective-permute-start.8 = (bf16[16,64,256]{2,1,0:T(8,128)(2,1)}, bf16[16,64,256]{2,1,0:T(8,128)(2,1)}, u32[]{:S(2)}, u32[]{:S(2)}) collective-permute-start(bf16[16,64,256]{2,1,0:T(8,128)(2,1)} %get-tuple-element.28), channel_id=1, source_target_pairs={{0,1},{1,2},{2,3},{3,0},{4,5},{5,6},{6,7},{7,4},{8,9},{9,10},{10,1... | collective-permute-start | bytes 1572872 | tf_op jit(solution)/shard_map/ppermute | solution.py:394
  74.7 27.2 %collective-permute-start = (bf16[16,32,256]{2,1,0:T(8,128)(2,1)}, bf16[16,32,256]{2,1,0:T(8,128)(2,1)S(1)}, u32[]{:S(2)}, u32[]{:S(2)}) collective-permute-start(bf16[16,32,256]{2,1,0:T(8,128)(2,1)} %get-tuple-element.17.refs_0_.refs_7_), channel_id=1, source_target_pairs={{0,1},{1,2},{2,3},{3,0},{4,5},{5,6},{6,7},{7,4},{8,9},{9,10},{10,1... | collective-permute-start | bytes 786440 | tf_op jit(solution)/shard_map/ppermute | solution.py:394
  74.8 27.2 %collective-permute-start.4 = (bf16[16,32,256]{2,1,0:T(8,128)(2,1)}, bf16[16,32,256]{2,1,0:T(8,128)(2,1)S(1)}, u32[]{:S(2)}, u32[]{:S(2)}) collective-permute-start(bf16[16,32,256]{2,1,0:T(8,128)(2,1)} %get-tuple-element.18.refs_4_.refs_11_), channel_id=1, source_target_pairs={{0,3},{1,0},{2,1},{3,2},{4,7},{5,4},{6,5},{7,6},{8,11},{9,8},{10,9... | collective-permute-start | bytes 786440 | tf_op jit(solution)/shard_map/ppermute | solution.py:394
  77.5 31.0 %collective-permute-start.11 = (bf16[16,64,256]{2,1,0:T(8,128)(2,1)}, bf16[16,64,256]{2,1,0:T(8,128)(2,1)}, u32[]{:S(2)}, u32[]{:S(2)}) collective-permute-start(bf16[16,64,256]{2,1,0:T(8,128)(2,1)} %get-tuple-element.27), channel_id=1, source_target_pairs={{0,1},{1,2},{2,3},{3,0},{4,5},{5,6},{6,7},{7,4},{8,9},{9,10},{10,1... | collective-permute-start | bytes 1572872 | tf_op jit(solution)/shard_map/ppermute | solution.py:394
  77.5 1.6 copy-start.1
  79.1 0.7 copy-start.4
  82.0 17.1 %copy-start.8 = (bf16[16,32,256]{2,1,0:T(8,128)(2,1)S(1)}, bf16[16,32,256]{2,1,0:T(8,128)(2,1)}, u32[]{:S(2)}) copy-start(bf16[16,32,256]{2,1,0:T(8,128)(2,1)} %get-tuple-element.17.refs_0_.refs_7_) | copy-start | bytes 786436
  82.0 19.9 %copy-start.9 = (bf16[16,32,256]{2,1,0:T(8,128)(2,1)S(1)}, bf16[16,32,256]{2,1,0:T(8,128)(2,1)}, u32[]{:S(2)}) copy-start(bf16[16,32,256]{2,1,0:T(8,128)(2,1)} %get-tuple-element.18.refs_4_.refs_11_) | copy-start | bytes 786436
  82.0 22.7 %copy-start.16 = (s32[2]{0:T(128)S(1)}, s32[2]{0:T(128)}, u32[]{:S(2)}) copy-start(s32[2]{0:T(128)} %get-tuple-element.25) | copy-start | bytes 28
  93.9 57.3 %all-to-all-start.3 = ((bf16[32,128,256]{2,1,0:T(8,128)(2,1)}), bf16[32,128,256]{2,1,0:T(8,128)(2,1)}, u32[]{:S(2)}, u32[]{:S(2)}) async-start(bf16[32,128,256]{2,1,0:T(8,128)(2,1)} %shard_map.57), calls=%async_computation.3 | async-start | bytes 4194304 | tf_op jit(solution)/shard_map/all_to_all | solution.py:377
  99.1 10.8 %collective-permute-start.2 = (bf16[16,32,256]{2,1,0:T(8,128)(2,1)S(1)}, bf16[16,32,256]{2,1,0:T(8,128)(2,1)S(1)}, u32[]{:S(2)}, u32[]{:S(2)}) collective-permute-start(bf16[16,32,256]{2,1,0:T(8,128)(2,1)S(1)} %copy-done.8), channel_id=1, source_target_pairs={{0,3},{1,0},{2,1},{3,2},{4,7},{5,4},{6,5},{7,6},{8,11},{9,8},{10,9... | collective-permute-start | bytes 786440 | tf_op jit(solution)/shard_map/ppermute | solution.py:394
  101.9 8.5 %collective-permute-start.3 = (bf16[16,32,256]{2,1,0:T(8,128)(2,1)S(1)}, bf16[16,32,256]{2,1,0:T(8,128)(2,1)S(1)}, u32[]{:S(2)}, u32[]{:S(2)}) collective-permute-start(bf16[16,32,256]{2,1,0:T(8,128)(2,1)S(1)} %copy-done.9), channel_id=1, source_target_pairs={{0,1},{1,2},{2,3},{3,0},{4,5},{5,6},{6,7},{7,4},{8,9},{9,10},{10,1... | collective-permute-start | bytes 786440 | tf_op jit(solution)/shard_map/ppermute | solution.py:394
  101.9 8.5 %copy-start.10 = (bf16[16,32,256]{2,1,0:T(8,128)(2,1)}, bf16[16,32,256]{2,1,0:T(8,128)(2,1)S(1)}, u32[]{:S(2)}) copy-start(bf16[16,32,256]{2,1,0:T(8,128)(2,1)S(1)} %collective-permute-done.refs_1_.refs_8_) | copy-start | bytes 786436
  101.9 14.1 %collective-permute-start.1 = (bf16[16,32,256]{2,1,0:T(8,128)(2,1)S(1)}, bf16[16,32,256]{2,1,0:T(8,128)(2,1)S(1)}, u32[]{:S(2)}, u32[]{:S(2)}) collective-permute-start(bf16[16,32,256]{2,1,0:T(8,128)(2,1)S(1)} %collective-permute-done.refs_1_.refs_8_), channel_id=1, source_target_pairs={{0,1},{1,2},{2,3},{3,0},{4,5},{5,6},{6,7},{7,4},{8,9},{9,10},{10,1... | collective-permute-start | bytes 786440 | tf_op jit(solution)/shard_map/ppermute | solution.py:394
  102.0 14.0 %copy-start.11 = (bf16[16,32,256]{2,1,0:T(8,128)(2,1)}, bf16[16,32,256]{2,1,0:T(8,128)(2,1)S(1)}, u32[]{:S(2)}) copy-start(bf16[16,32,256]{2,1,0:T(8,128)(2,1)S(1)} %collective-permute-done.4.refs_7_.refs_14_) | copy-start | bytes 786436
  102.0 14.7 %collective-permute-start.5 = (bf16[16,32,256]{2,1,0:T(8,128)(2,1)S(1)}, bf16[16,32,256]{2,1,0:T(8,128)(2,1)}, u32[]{:S(2)}, u32[]{:S(2)}) collective-permute-start(bf16[16,32,256]{2,1,0:T(8,128)(2,1)S(1)} %collective-permute-done.4.refs_7_.refs_14_), channel_id=1, source_target_pairs={{0,3},{1,0},{2,1},{3,2},{4,7},{5,4},{6,5},{7,6},{8,11},{9,8},{10,9... | collective-permute-start | bytes 786440 | tf_op jit(solution)/shard_map/ppermute | solution.py:394
  108.5 24.0 %collective-permute-start.6 = (bf16[16,64,256]{2,1,0:T(8,128)(2,1)}, bf16[16,64,256]{2,1,0:T(8,128)(2,1)}, u32[]{:S(2)}, u32[]{:S(2)}) collective-permute-start(bf16[16,64,256]{2,1,0:T(8,128)(2,1)} %get-tuple-element.28), channel_id=1, source_target_pairs={{0,3},{1,0},{2,1},{3,2},{4,7},{5,4},{6,5},{7,6},{8,11},{9,8},{10,9... | collective-permute-start | bytes 1572872 | tf_op jit(solution)/shard_map/ppermute | solution.py:394
  109.8 6.2 %copy-start.12 = (bf16[16,32,256]{2,1,0:T(8,128)(2,1)}, bf16[16,32,256]{2,1,0:T(8,128)(2,1)S(1)}, u32[]{:S(2)}) copy-start(bf16[16,32,256]{2,1,0:T(8,128)(2,1)S(1)} %collective-permute-done.2.refs_3_.refs_10_) | copy-start | bytes 786436
  109.8 22.6 %collective-permute-start.9 = (bf16[16,64,256]{2,1,0:T(8,128)(2,1)}, bf16[16,64,256]{2,1,0:T(8,128)(2,1)}, u32[]{:S(2)}, u32[]{:S(2)}) collective-permute-start(bf16[16,64,256]{2,1,0:T(8,128)(2,1)} %collective-permute-done.8.refs_10_.refs_1_), channel_id=1, source_target_pairs={{0,1},{1,2},{2,3},{3,0},{4,5},{5,6},{6,7},{7,4},{8,9},{9,10},{10,1... | collective-permute-start | bytes 1572872 | tf_op jit(solution)/shard_map/ppermute | solution.py:394
  110.4 5.6 %copy-start.13 = (bf16[16,32,256]{2,1,0:T(8,128)(2,1)}, bf16[16,32,256]{2,1,0:T(8,128)(2,1)S(1)}, u32[]{:S(2)}) copy-start(bf16[16,32,256]{2,1,0:T(8,128)(2,1)S(1)} %collective-permute-done.3.refs_5_.refs_12_) | copy-start | bytes 786436
  110.4 24.9 %collective-permute-start.10 = (bf16[16,64,256]{2,1,0:T(8,128)(2,1)}, bf16[16,64,256]{2,1,0:T(8,128)(2,1)}, u32[]{:S(2)}, u32[]{:S(2)}) collective-permute-start(bf16[16,64,256]{2,1,0:T(8,128)(2,1)} %collective-permute-done.7.refs_10_.refs_4_), channel_id=1, source_target_pairs={{0,3},{1,0},{2,1},{3,2},{4,7},{5,4},{6,5},{7,6},{8,11},{9,8},{10,9... | collective-permute-start | bytes 1572872 | tf_op jit(solution)/shard_map/ppermute | solution.py:394
  116.0 0.7 copy-start.14
  159.4 59.0 %copy-start.5 = (s32[1,4096]{1,0:T(1,128)S(1)}, s32[1,4096]{1,0:T(1,128)}, u32[]{:S(2)}) copy-start(s32[1,4096]{1,0:T(1,128)} %get-tuple-element.15.pos_ref) | copy-start | bytes 49156

commit v5 on v4

--- a/solution.py
+++ b/solution.py
@@ -143,23 +143,27 @@
 
 
 def pick_kernel(slot_ref, arrived_ref, *refs):
-    _, tiles = slot_ref.shape
-    sem = refs[-1]
+    blocks, tiles = slot_ref.shape
+    turns_ref, sem = refs[-2:]
     part = refs[0].shape[1]
-    for n, out_ref in enumerate(refs[:-1]):
+    for n, out_ref in enumerate(refs[:-2]):
         for j in range(tiles):
             slot = slot_ref[n, j]
             row = pl.multiple_of(slot % 2 * part, part)
             pltpu.make_async_copy(
                 arrived_ref.at[slot // 2, pl.ds(row, part)], out_ref.at[j], sem.at[n]
             ).start()
-    for n, out_ref in enumerate(refs[:-1]):
+    one, two = (sum(slot_ref[n, j] % 2 for j in range(tiles)) for n in range(blocks))
+    lead = jnp.where((one == 0) & (two > 0), 1, 0)
+    turns_ref[0] = lead
+    turns_ref[1] = jnp.where((one > 0) & (two > 0), 1, lead)
+    for n, out_ref in enumerate(refs[:-2]):
         pltpu.make_async_copy(out_ref, out_ref, sem.at[n]).wait()
 
 
-def first_pass_kernel(scale, count, y_ref, slot_ref, *refs):
+def first_pass_kernel(scale, y_ref, slot_ref, *refs):
     out_ref, total_ref, answer_ref, keys, values, key_sem, sems = refs[-7:]
-    latents, first_ref, pieces = refs[:8], refs[8], refs[9 : 9 + count]
+    latents, first_ref, pieces = refs[:8], refs[8], refs[9:16]
     y = y_ref[0]
     blocks, tiles = slot_ref.shape
     rows = keys.shape[2]
@@ -194,11 +198,10 @@
     nt = (((1,), (1,)), ((), ()))
     group = 2
     span = group * rows
-    first = pieces[0][...]
-    if len(pieces) == 4:
-        first = jnp.concatenate([first, pieces[1][...]], axis=0)
-    second = jnp.concatenate([pieces[-2][...], pieces[-1][...]], axis=0)
-    q = jnp.where(piece == 0, first, second)
+    q = pieces[0][...]
+    for p in range(1, PLANES):
+        other = jnp.concatenate([pieces[2 * p - 1][...], pieces[2 * p][...]], axis=0)
+        q = jnp.where(piece == p, other, q)
     sources, part, width = q.shape
     q = q.reshape(sources * part, width)
     total = jnp.zeros((sources * part, rows), jnp.float32)
@@ -397,11 +400,12 @@
     q0a, q0b = arrived[:mid, :own], arrived[mid:, :own]
     q1a, q3b, q1b, q3a = shift(q0a, 1), shift(q0b, 3), shift(q0b, 1), shift(q0a, 3)
     got_first = exchange(first_out)
-    k0 = pl.pallas_call(
+    *k0, turns = pl.pallas_call(
         pick_kernel,
         in_specs=[SMEM, ANY],
-        out_specs=[VMEM] * blocks_here,
-        out_shape=[jax.ShapeDtypeStruct((tiles_each, tile_part, width), jnp.bfloat16)] * blocks_here,
+        out_specs=[VMEM] * blocks_here + [SMEM],
+        out_shape=[jax.ShapeDtypeStruct((tiles_each, tile_part, width), jnp.bfloat16)] * blocks_here
+        + [jax.ShapeDtypeStruct((blocks_here,), jnp.int32)],
         scratch_shapes=[pltpu.SemaphoreType.DMA((blocks_here,))],
         compiler_params=params(FULL),
         name="pick",
@@ -417,47 +421,44 @@
     keys = tiles_each * TILE
     scale = LOG2E / (width * kernel_width)
 
-    def first_pass(begin, pieces, sums):
-        piece = pl.BlockSpec((dp_count, part, width), lambda p, n: (0, n, 0))
-        half = pl.BlockSpec((mid, part, width), lambda p, n: (0, n, 0))
-        specs = [piece, half, half] if len(pieces) == 3 else [half] * 4
-        given = 2 + 9 + len(pieces)
-        return pl.pallas_call(
-            functools.partial(first_pass_kernel, scale, len(pieces)),
-            grid=(2, blocks_here),
-            in_specs=[SMEM, SMEM] + [ANY] * 9 + specs + [ANY] * len(sums),
-            out_specs=[
-                pl.BlockSpec((1, rows, columns), lambda p, n: (blocks_here * (begin + p) + n, 0, 0)),
-                pl.BlockSpec((1, rows, 128), lambda p, n: (blocks_here * (begin + p) + n, 0, 0)),
-                pl.BlockSpec((dp_count, part, columns), lambda p, n: (0, blocks_here * (begin + p) + n, 0)),
-            ],
-            out_shape=[
-                jax.ShapeDtypeStruct((PLANES * blocks_here, rows, columns), jnp.float32),
-                jax.ShapeDtypeStruct((PLANES * blocks_here, rows, 128), jnp.float32),
-                jax.ShapeDtypeStruct((dp_count, PLANES * own, columns), jnp.bfloat16),
-            ],
-            scratch_shapes=[
-                pltpu.VMEM((blocks_here, tiles_each, TILE, width), jnp.bfloat16),
-                pltpu.VMEM((blocks_here, keys, columns), jnp.bfloat16),
-                pltpu.SemaphoreType.DMA((blocks_here,)),
-                pltpu.SemaphoreType.DMA((blocks_here,)),
-            ],
-            input_output_aliases={given + i: i for i in range(len(sums))},
-            compiler_params=params(FULL),
-            cost_estimate=pl.CostEstimate(
-                flops=4 * blocks_here * rows * keys * (width + columns),
-                transcendentals=2 * blocks_here * rows * keys,
-                bytes_accessed=2 * blocks_here * keys * (width + columns),
-            ),
-            name="first_pass",
-        )(y1, slot_table, *latents, got_first, *pieces, *sums)
-
-    sums = first_pass(0, (arrived, q1a, q1b), ())
-    *sums, answers = first_pass(2, (q3a, q3b, q2a, q2b), sums)
-
-    has = jnp.sum(slot_table % 2, axis=1) > 0
-    lead = jnp.where(has[0], 0, jnp.where(has[1], 1, 0))
-    turns = jnp.stack([lead, jnp.where(has[0] & has[1], 1, lead)]).astype(jnp.int32)
+    def rows_of(piece, sources):
+        return pl.BlockSpec(
+            (sources, part, width),
+            lambda p, n: (0, jnp.where(p == piece, n, jnp.where(p < piece, 0, blocks_here - 1)), 0),
+        )
+
+    pieces = [arrived, q1a, q1b, q3a, q3b, q2a, q2b]
+    *sums, answers = pl.pallas_call(
+        functools.partial(first_pass_kernel, scale),
+        grid=(PLANES, blocks_here),
+        in_specs=[SMEM, SMEM]
+        + [ANY] * 9
+        + [rows_of(0, dp_count)]
+        + [rows_of(p, mid) for p in range(1, PLANES) for _ in range(2)],
+        out_specs=[
+            pl.BlockSpec((1, rows, columns), lambda p, n: (blocks_here * p + n, 0, 0)),
+            pl.BlockSpec((1, rows, 128), lambda p, n: (blocks_here * p + n, 0, 0)),
+            pl.BlockSpec((dp_count, part, columns), lambda p, n: (0, blocks_here * p + n, 0)),
+        ],
+        out_shape=[
+            jax.ShapeDtypeStruct((PLANES * blocks_here, rows, columns), jnp.float32),
+            jax.ShapeDtypeStruct((PLANES * blocks_here, rows, 128), jnp.float32),
+            jax.ShapeDtypeStruct((dp_count, PLANES * own, columns), jnp.bfloat16),
+        ],
+        scratch_shapes=[
+            pltpu.VMEM((blocks_here, tiles_each, TILE, width), jnp.bfloat16),
+            pltpu.VMEM((blocks_here, keys, columns), jnp.bfloat16),
+            pltpu.SemaphoreType.DMA((blocks_here,)),
+            pltpu.SemaphoreType.DMA((blocks_here,)),
+        ],
+        compiler_params=params(FULL),
+        cost_estimate=pl.CostEstimate(
+            flops=2 * PLANES * blocks_here * rows * keys * (width + columns),
+            transcendentals=PLANES * blocks_here * rows * keys,
+            bytes_accessed=6 * PLANES * blocks_here * rows * columns,
+        ),
+        name="first_pass",
+    )(y1, slot_table, *latents, got_first, *pieces)
 
     def answer_block(n, p, t):
         repeated = (n > 0) & (t[n] == t[0])
@@ -484,7 +485,7 @@
         input_output_aliases={5 + 7 + 9: 0},
         compiler_params=params(FULL),
         name="finish",
-    )(turns, y1, slot_table, *sums, arrived, q1a, q1b, q3a, q3b, q2a, q2b, *latents, got_second, answers)
+    )(turns, y1, slot_table, *sums, *pieces, *latents, got_second, answers)
     back = exchange(answers)
     count = back.shape[0] * back.shape[1]
     return pl.pallas_call(

time: 227 us -> 236 us (1.040)
  waiting for transfers between devices: 48.2 us -> 59.7 us
  starting transfers between devices: 38.2 us -> 43.7 us
  Pallas kernels: 66.3 us -> 63.1 us
  between operations: 2.9 us -> 0.35 us
    ppermute x12, waiting for transfers between devices: 6.5 us -> 29.8 us  [shift(): lax.ppermute(v, 'label', [(i, (i + by) % PLANES) for i in range(PLANES)])]
    all_to_all x3, waiting for transfers between devices: 23.8 us -> 11.9 us  [exchange(): return lax.all_to_all(v, 'dp', split_axis=0, concat_axis=0, tiled=True)]
    all_to_all x3, starting transfers between devices: 13.6 us -> 17.7 us  [exchange(): return lax.all_to_all(v, 'dp', split_axis=0, concat_axis=0, tiled=True)]
    pallas_call x2 -> x1, Pallas kernels: 31.6 us -> 28.3 us  [shards(): pl.pallas_call(functools.partial(first_pass_kernel, scale), grid=(PLANES,...]
  transfers between devices with their start and end apart: 16 -> 16, of which waited for: 6 -> 7; matrix products, arithmetic and copies ran while one was open for 2% -> 2% of each run, Pallas kernels for 18% -> 16%
where the time goes in v5:
time: 236 us; the launch traced here: 235 us
  Pallas kernels  63.1 us (27%)
  waiting for transfers between devices  59.7 us (25%)
  blocking collectives  58.9 us (25%)
  starting transfers between devices  43.7 us (19%)
  local copies, waits for them, and re-layouts  7.92 us (3%)
    all_to_all x1, blocking collectives, exchange(): return lax.all_to_all(v, 'dp', split_axis=0, concat_axis=0, tiled=True)  58.9 us
    ppermute x12, waiting for transfers between devices, shift(): lax.ppermute(v, 'label', [(i, (i + by) % PLANES) for i in range(PLANES)])  29.8 us
    pallas_call x1, Pallas kernels, shards(): pl.pallas_call(functools.partial(first_pass_kernel, scale), grid=(PLANES,...  28.3 us
    all_to_all x1, waiting for transfers between devices, shards(): lax.all_to_all(sent, 'dp', split_axis=0, concat_axis=0, tiled=True)  17.9 us
    all_to_all x3, starting transfers between devices, exchange(): return lax.all_to_all(v, 'dp', split_axis=0, concat_axis=0, tiled=True)  17.7 us
    ppermute x12, starting transfers between devices, shift(): lax.ppermute(v, 'label', [(i, (i + by) % PLANES) for i in range(PLANES)])  16.4 us
    all_to_all x3, waiting for transfers between devices, exchange(): return lax.all_to_all(v, 'dp', split_axis=0, concat_axis=0, tiled=True)  11.9 us
    all_to_all x1, starting transfers between devices, shards(): lax.all_to_all(sent, 'dp', split_axis=0, concat_axis=0, tiled=True)  9.61 us
  transfers between devices with their start and end apart: 16, of which 7 were waited for; matrix products, arithmetic and copies ran while one was open for 2% of the time, Pallas kernels for 16%

profile of v5, /device:TPU:1, one launch (start us, length us, event | category | flops | bytes accessed | tf_op | source)
XLA Modules:
  0.0 234.9 jit_solution(3613243631817886664)
XLA Ops:
  0.0 9.2 %pack.1 = (bf16[32,72,256]{2,1,0:T(8,128)(2,1)}, s32[1,4096]{1,0:T(1,128)}) custom-call(s32[1]{0:T(128)} %bitcast.y_ref, s32[1,4096]{1,0:T(1,128)} %bitcast.14, s32[2,16]{1,0:T(2,128)} %list_ref.1, bf16[4096,256]{1,0:T(8,128)(2,1)} %x_ref.1), custom_call_target="tpu_custom_call" | custom-call | tf_op jit(solution)/shard_map/pack/pallas_call | solution.py:353
  9.2 0.0 copy-start.7
  9.2 9.6 %all-to-all-start = ((bf16[32,72,256]{2,1,0:T(8,128)(2,1)}), bf16[32,72,256]{2,1,0:T(8,128)(2,1)}, u32[]{:S(2)}, u32[]{:S(2)}) async-start(bf16[32,72,256]{2,1,0:T(8,128)(2,1)} %get-tuple-element.14), calls=%async_computation | async-start | bytes 2359296 | tf_op jit(solution)/shard_map/all_to_all | solution.py:373
  18.8 0.2 fusion
  19.1 0.2 fusion.1.tile_ref
  19.3 0.0 copy-start
  19.3 17.9 %all-to-all-done.refs_9_.refs_0_ = bf16[32,72,256]{2,1,0:T(8,128)(2,1)} async-done(((bf16[32,72,256]{2,1,0:T(8,128)(2,1)}), bf16[32,72,256]{2,1,0:T(8,128)(2,1)}, u32[]{:S(2)}, u32[]{:S(2)}) %all-to-all-start) | async-done | bytes 1179680 | tf_op jit(solution)/shard_map/all_to_all | solution.py:373
  37.2 1.1 slice.9
  38.3 1.8 shard_map.55
  40.1 3.9 %all-to-all-start.1 = ((bf16[32,64,256]{2,1,0:T(8,128)(2,1)}), bf16[32,64,256]{2,1,0:T(8,128)(2,1)S(1)}, u32[]{:S(2)}, u32[]{:S(2)}) async-start(bf16[32,64,256]{2,1,0:T(8,128)(2,1)} %shard_map.55), calls=%async_computation.1 | async-start | bytes 2097152 | tf_op jit(solution)/shard_map/all_to_all | solution.py:380
  44.0 3.6 %shard_map.56 = bf16[32,128,256]{2,1,0:T(8,128)(2,1)S(1)} custom-call(s32[32,2]{1,0:T(8,128)S(1)} %bitcast.10, bf16[32,128,256]{2,1,0:T(8,128)(2,1)S(1)} %bitcast.7), custom_call_target="tpu_custom_call" | custom-call | tf_op jit(solution)/shard_map/pallas_call | solution.py:383
  47.7 0.0 copy-done.3
  47.7 0.0 copy-start.2
  47.7 1.3 copy-done.2
  49.0 11.9 %all-to-all-done.1.arrived_ref = bf16[32,64,256]{2,1,0:T(8,128)(2,1)S(1)} async-done(((bf16[32,64,256]{2,1,0:T(8,128)(2,1)}), bf16[32,64,256]{2,1,0:T(8,128)(2,1)S(1)}, u32[]{:S(2)}, u32[]{:S(2)}) %all-to-all-start.1) | async-done | bytes 1048608 | tf_op jit(solution)/shard_map/all_to_all | solution.py:380
  60.9 4.6 %all-to-all-start.2 = ((bf16[32,128,256]{2,1,0:T(8,128)(2,1)}), bf16[32,128,256]{2,1,0:T(8,128)(2,1)}, u32[]{:S(2)}, u32[]{:S(2)}) async-start(bf16[32,128,256]{2,1,0:T(8,128)(2,1)} %copy-done.2), calls=%async_computation.2 | async-start | bytes 4194304 | tf_op jit(solution)/shard_map/all_to_all | solution.py:380
  65.5 0.0 copy-start.15
  65.5 2.3 fusion.3
  67.8 2.7 %collective-permute-start.9 = (bf16[16,64,256]{2,1,0:T(8,128)(2,1)}, bf16[16,64,256]{2,1,0:T(8,128)(2,1)}, u32[]{:S(2)}, u32[]{:S(2)}) collective-permute-start(bf16[16,64,256]{2,1,0:T(8,128)(2,1)} %get-tuple-element.21), channel_id=1, source_target_pairs={{0,3},{1,0},{2,1},{3,2},{4,7},{5,4},{6,5},{7,6},{8,11},{9,8},{10,9... | collective-permute-start | bytes 1572872 | tf_op jit(solution)/shard_map/ppermute | solution.py:397
  70.6 0.0 copy-done.15
  70.6 0.1 reshape.88
  70.7 0.0 collective-permute-start.7
  70.7 0.1 collective-permute-start.6
  70.8 2.7 %collective-permute-start.8 = (bf16[16,64,256]{2,1,0:T(8,128)(2,1)}, bf16[16,64,256]{2,1,0:T(8,128)(2,1)}, u32[]{:S(2)}, u32[]{:S(2)}) collective-permute-start(bf16[16,64,256]{2,1,0:T(8,128)(2,1)} %get-tuple-element.22), channel_id=1, source_target_pairs={{0,3},{1,0},{2,1},{3,2},{4,7},{5,4},{6,5},{7,6},{8,11},{9,8},{10,9... | collective-permute-start | bytes 1572872 | tf_op jit(solution)/shard_map/ppermute | solution.py:397
  73.5 8.4 %collective-permute-done.9.refs_13_.refs_4_ = bf16[16,64,256]{2,1,0:T(8,128)(2,1)} collective-permute-done((bf16[16,64,256]{2,1,0:T(8,128)(2,1)}, bf16[16,64,256]{2,1,0:T(8,128)(2,1)}, u32[]{:S(2)}, u32[]{:S(2)}) %collective-permute-start.9) | collective-permute-done | bytes 524320 | tf_op jit(solution)/shard_map/ppermute | solution.py:397
  81.9 3.4 %collective-permute-start.11 = (bf16[16,64,256]{2,1,0:T(8,128)(2,1)}, bf16[16,64,256]{2,1,0:T(8,128)(2,1)}, u32[]{:S(2)}, u32[]{:S(2)}) collective-permute-start(bf16[16,64,256]{2,1,0:T(8,128)(2,1)} %collective-permute-done.9.refs_13_.refs_4_), channel_id=1, source_target_pairs={{0,3},{1,0},{2,1},{3,2},{4,7},{5,4},{6,5},{7,6},{8,11},{9,8},{10,9... | collective-permute-start | bytes 1572872 | tf_op jit(solution)/shard_map/ppermute | solution.py:397
  85.3 0.2 convert_reduce_fusion
  85.4 0.1 reduce_sum.21
  85.5 0.6 multiply_add_fusion.slot_ref
  86.1 10.2 %collective-permute-done.6.refs_10_.refs_1_ = bf16[16,64,256]{2,1,0:T(8,128)(2,1)} collective-permute-done((bf16[16,64,256]{2,1,0:T(8,128)(2,1)}, bf16[16,64,256]{2,1,0:T(8,128)(2,1)}, u32[]{:S(2)}, u32[]{:S(2)}) %collective-permute-start.6) | collective-permute-done | bytes 524320 | tf_op jit(solution)/shard_map/ppermute | solution.py:397
  96.3 0.0 collective-permute-start.10
  96.3 2.6 %pick.1 = (bf16[16,32,256]{2,1,0:T(8,128)(2,1)}, bf16[16,32,256]{2,1,0:T(8,128)(2,1)}, s32[2]{0:T(128)}) custom-call(s32[2,16]{1,0:T(2,128)} %multiply_add_fusion.slot_ref, bf16[32,64,256]{2,1,0:T(8,128)(2,1)} %copy-done.6), custom_call_target="tpu_custom_call" | custom-call | tf_op jit(solution)/shard_map/pick/pallas_call | solution.py:403
  98.9 0.1 collective-permute-start
  99.0 0.0 collective-permute-done.7.refs_11_.refs_2_
  99.0 2.7 %collective-permute-start.4 = (bf16[16,32,256]{2,1,0:T(8,128)(2,1)}, bf16[16,32,256]{2,1,0:T(8,128)(2,1)S(1)}, u32[]{:S(2)}, u32[]{:S(2)}) collective-permute-start(bf16[16,32,256]{2,1,0:T(8,128)(2,1)} %get-tuple-element.17.refs_4_.refs_11_), channel_id=1, source_target_pairs={{0,3},{1,0},{2,1},{3,2},{4,7},{5,4},{6,5},{7,6},{8,11},{9,8},{10,9... | collective-permute-start | bytes 786440 | tf_op jit(solution)/shard_map/ppermute | solution.py:397
  101.7 1.6 copy-done.1
  103.3 0.7 copy-done.4
  104.0 2.2 shard_map.57
  106.2 0.0 copy-start.8
  106.2 0.0 copy-start.9
  106.3 0.0 all-to-all-done.2.refs_8_
  106.3 9.2 %all-to-all-start.3 = ((bf16[32,128,256]{2,1,0:T(8,128)(2,1)}), bf16[32,128,256]{2,1,0:T(8,128)(2,1)}, u32[]{:S(2)}, u32[]{:S(2)}) async-start(bf16[32,128,256]{2,1,0:T(8,128)(2,1)} %shard_map.57), calls=%async_computation.3 | async-start | bytes 4194304 | tf_op jit(solution)/shard_map/all_to_all | solution.py:380
  115.5 0.0 collective-permute-done.8.refs_12_.refs_3_
  115.5 1.7 collective-permute-start.2
  117.2 0.0 collective-permute-done.11.refs_15_.refs_6_
  117.2 0.0 collective-permute-start.3
  117.2 0.0 collective-permute-done.refs_1_.refs_8_
  117.3 0.0 copy-start.10
  117.3 0.1 collective-permute-start.1
  117.4 0.0 collective-permute-done.4.refs_7_.refs_14_
  117.4 2.8 %collective-permute-start.5 = (bf16[16,32,256]{2,1,0:T(8,128)(2,1)S(1)}, bf16[16,32,256]{2,1,0:T(8,128)(2,1)}, u32[]{:S(2)}, u32[]{:S(2)}) collective-permute-start(bf16[16,32,256]{2,1,0:T(8,128)(2,1)S(1)} %collective-permute-done.4.refs_7_.refs_14_), channel_id=1, source_target_pairs={{0,3},{1,0},{2,1},{3,2},{4,7},{5,4},{6,5},{7,6},{8,11},{9,8},{10,9... | collective-permute-start | bytes 786440 | tf_op jit(solution)/shard_map/ppermute | solution.py:397
  120.2 0.0 collective-permute-done.10.refs_14_.refs_5_
  120.2 3.0 %collective-permute-done.2.refs_3_.refs_10_ = bf16[16,32,256]{2,1,0:T(8,128)(2,1)S(1)} collective-permute-done((bf16[16,32,256]{2,1,0:T(8,128)(2,1)S(1)}, bf16[16,32,256]{2,1,0:T(8,128)(2,1)S(1)}, u32[]{:S(2)}, u32[]{:S(2)}) %collective-permute-start.2) | collective-permute-done | bytes 262176 | tf_op jit(solution)/shard_map/ppermute | solution.py:397
  123.2 2.6 %collective-permute-done.3.refs_5_.refs_12_ = bf16[16,32,256]{2,1,0:T(8,128)(2,1)S(1)} collective-permute-done((bf16[16,32,256]{2,1,0:T(8,128)(2,1)S(1)}, bf16[16,32,256]{2,1,0:T(8,128)(2,1)S(1)}, u32[]{:S(2)}, u32[]{:S(2)}) %collective-permute-start.3) | collective-permute-done | bytes 262176 | tf_op jit(solution)/shard_map/ppermute | solution.py:397
  125.8 0.0 copy-done.10
  125.8 5.6 %collective-permute-done.1.refs_2_.refs_9_ = bf16[16,32,256]{2,1,0:T(8,128)(2,1)S(1)} collective-permute-done((bf16[16,32,256]{2,1,0:T(8,128)(2,1)S(1)}, bf16[16,32,256]{2,1,0:T(8,128)(2,1)S(1)}, u32[]{:S(2)}, u32[]{:S(2)}) %collective-permute-start.1) | collective-permute-done | bytes 262176 | tf_op jit(solution)/shard_map/ppermute | solution.py:397
  131.5 0.0 copy-done.12
  131.5 0.7 copy-done.14
  132.2 0.0 collective-permute-done.5.refs_6_.refs_13_
  132.2 28.3 %first_pass.1 = (f32[8,1024,256]{2,1,0:T(8,128)}, f32[8,1024,128]{2,1,0:T(8,128)}, bf16[32,256,256]{2,1,0:T(8,128)(2,1)}) custom-call(s32[1]{0:T(128)} %bitcast.y_ref, s32[2,16]{1,0:T(2,128)} %multiply_add_fusion.slot_ref, bf16[16,32,256]{2,1,0:T(8,128)(2,1)} %get-tuple-element.16.refs_0_.refs_7_, bf16[16,32,256]{2,1,0:T(8,128)(2,1)} %copy-done.10, ...), custom_call_target="tpu_custom_call" | custom-call | flops 17179869184 | bytes 12582912 | tf_op jit(solution)/shard_map/first_pass/pallas_call | solution.py:431
  160.5 0.0 all-to-all-done.3.refs_15_
  160.5 8.3 %finish.1 = bf16[32,256,256]{2,1,0:T(8,128)(2,1)} custom-call(s32[2]{0:T(128)} %get-tuple-element.15.turns_ref, s32[1]{0:T(128)} %bitcast.y_ref, s32[2,16]{1,0:T(2,128)} %multiply_add_fusion.slot_ref, f32[8,1024,256]{2,1,0:T(8,128)} %get-tuple-element.18.sum_ref, f32[8,1024,128]{2,1,0:T(8,128)} %get-tuple-element.19.total_ref, ...), custom_call_target="tpu_custom_call", output_to_operand_aliasing={{}: (21, {})} | custom-call | tf_op jit(solution)/shard_map/finish/pallas_call | solution.py:467
  168.8 58.9 %all_to_all.25 = bf16[32,256,256]{2,1,0:T(8,128)(2,1)S(1)} all-to-all(bf16[32,256,256]{2,1,0:T(8,128)(2,1)} %finish.1), channel_id=1, replica_groups=mesh['dp'=32,'label'=4] {'dp'}, dimensions={0} | all-to-all | bytes 8388608 | tf_op jit(solution)/shard_map/all_to_all | solution.py:380
  227.8 7.1 %unpack.1 = bf16[4096,256]{1,0:T(8,128)(2,1)} custom-call(s32[1,4096]{1,0:T(1,128)S(1)} %copy-done.5, bf16[8192,256]{1,0:T(8,128)(2,1)S(1)} %bitcast.6), custom_call_target="tpu_custom_call" | custom-call | tf_op jit(solution)/shard_map/unpack/pallas_call | solution.py:491
  (20 shorter events, 0.1 us)
Async XLA Ops:
  9.2 9.6 %copy-start.7 = (bf16[4096,256]{1,0:T(8,128)(2,1)S(1)}, bf16[4096,256]{1,0:T(8,128)(2,1)}, u32[]{:S(2)}) copy-start(bf16[4096,256]{1,0:T(8,128)(2,1)} %param.7) | copy-start | bytes 6291460
  9.2 28.0 %all-to-all-start = ((bf16[32,72,256]{2,1,0:T(8,128)(2,1)}), bf16[32,72,256]{2,1,0:T(8,128)(2,1)}, u32[]{:S(2)}, u32[]{:S(2)}) async-start(bf16[32,72,256]{2,1,0:T(8,128)(2,1)} %get-tuple-element.14), calls=%async_computation | async-start | bytes 2359296 | tf_op jit(solution)/shard_map/all_to_all | solution.py:373
  19.3 24.8 %copy-start = (bf16[4096,256]{1,0:T(8,128)(2,1)S(1)}, bf16[4096,256]{1,0:T(8,128)(2,1)}, u32[]{:S(2)}) copy-start(bf16[4096,256]{1,0:T(8,128)(2,1)} %param.8) | copy-start | bytes 6291460
  38.3 9.4 %copy-start.3 = (s32[32,1,2]{2,1,0:T(1,128)}, s32[32,1,2]{2,1,0:T(1,128)S(1)}, u32[]{:S(2)}) copy-start(s32[32,1,2]{2,1,0:T(1,128)S(1)} %convert_element_type.19) | copy-start | bytes 772
  40.1 20.8 %all-to-all-start.1 = ((bf16[32,64,256]{2,1,0:T(8,128)(2,1)}), bf16[32,64,256]{2,1,0:T(8,128)(2,1)S(1)}, u32[]{:S(2)}, u32[]{:S(2)}) async-start(bf16[32,64,256]{2,1,0:T(8,128)(2,1)} %shard_map.55), calls=%async_computation.1 | async-start | bytes 2097152 | tf_op jit(solution)/shard_map/all_to_all | solution.py:380
  47.7 1.3 copy-start.2
  60.9 6.9 %copy-start.6 = (bf16[32,64,256]{2,1,0:T(8,128)(2,1)}, bf16[32,64,256]{2,1,0:T(8,128)(2,1)S(1)}, u32[]{:S(2)}) copy-start(bf16[32,64,256]{2,1,0:T(8,128)(2,1)S(1)} %all-to-all-done.1.arrived_ref) | copy-start | bytes 3145732
  60.9 45.3 %all-to-all-start.2 = ((bf16[32,128,256]{2,1,0:T(8,128)(2,1)}), bf16[32,128,256]{2,1,0:T(8,128)(2,1)}, u32[]{:S(2)}, u32[]{:S(2)}) async-start(bf16[32,128,256]{2,1,0:T(8,128)(2,1)} %copy-done.2), calls=%async_computation.2 | async-start | bytes 4194304 | tf_op jit(solution)/shard_map/all_to_all | solution.py:380
  65.5 5.1 %copy-start.15 = (s32[2,16]{1,0:T(2,128)S(1)}, s32[2,16]{1,0:T(2,128)}, u32[]{:S(2)}) copy-start(s32[2,16]{1,0:T(2,128)} %list_ref.1) | copy-start | bytes 388
  67.8 14.0 %collective-permute-start.9 = (bf16[16,64,256]{2,1,0:T(8,128)(2,1)}, bf16[16,64,256]{2,1,0:T(8,128)(2,1)}, u32[]{:S(2)}, u32[]{:S(2)}) collective-permute-start(bf16[16,64,256]{2,1,0:T(8,128)(2,1)} %get-tuple-element.21), channel_id=1, source_target_pairs={{0,3},{1,0},{2,1},{3,2},{4,7},{5,4},{6,5},{7,6},{8,11},{9,8},{10,9... | collective-permute-start | bytes 1572872 | tf_op jit(solution)/shard_map/ppermute | solution.py:397
  70.7 28.3 %collective-permute-start.7 = (bf16[16,64,256]{2,1,0:T(8,128)(2,1)}, bf16[16,64,256]{2,1,0:T(8,128)(2,1)}, u32[]{:S(2)}, u32[]{:S(2)}) collective-permute-start(bf16[16,64,256]{2,1,0:T(8,128)(2,1)} %get-tuple-element.21), channel_id=1, source_target_pairs={{0,1},{1,2},{2,3},{3,0},{4,5},{5,6},{6,7},{7,4},{8,9},{9,10},{10,1... | collective-permute-start | bytes 1572872 | tf_op jit(solution)/shard_map/ppermute | solution.py:397
  70.7 25.6 %collective-permute-start.6 = (bf16[16,64,256]{2,1,0:T(8,128)(2,1)}, bf16[16,64,256]{2,1,0:T(8,128)(2,1)}, u32[]{:S(2)}, u32[]{:S(2)}) collective-permute-start(bf16[16,64,256]{2,1,0:T(8,128)(2,1)} %get-tuple-element.22), channel_id=1, source_target_pairs={{0,1},{1,2},{2,3},{3,0},{4,5},{5,6},{6,7},{7,4},{8,9},{9,10},{10,1... | collective-permute-start | bytes 1572872 | tf_op jit(solution)/shard_map/ppermute | solution.py:397
  70.8 44.7 %collective-permute-start.8 = (bf16[16,64,256]{2,1,0:T(8,128)(2,1)}, bf16[16,64,256]{2,1,0:T(8,128)(2,1)}, u32[]{:S(2)}, u32[]{:S(2)}) collective-permute-start(bf16[16,64,256]{2,1,0:T(8,128)(2,1)} %get-tuple-element.22), channel_id=1, source_target_pairs={{0,3},{1,0},{2,1},{3,2},{4,7},{5,4},{6,5},{7,6},{8,11},{9,8},{10,9... | collective-permute-start | bytes 1572872 | tf_op jit(solution)/shard_map/ppermute | solution.py:397
  81.9 35.4 %collective-permute-start.11 = (bf16[16,64,256]{2,1,0:T(8,128)(2,1)}, bf16[16,64,256]{2,1,0:T(8,128)(2,1)}, u32[]{:S(2)}, u32[]{:S(2)}) collective-permute-start(bf16[16,64,256]{2,1,0:T(8,128)(2,1)} %collective-permute-done.9.refs_13_.refs_4_), channel_id=1, source_target_pairs={{0,3},{1,0},{2,1},{3,2},{4,7},{5,4},{6,5},{7,6},{8,11},{9,8},{10,9... | collective-permute-start | bytes 1572872 | tf_op jit(solution)/shard_map/ppermute | solution.py:397
  96.3 23.9 %collective-permute-start.10 = (bf16[16,64,256]{2,1,0:T(8,128)(2,1)}, bf16[16,64,256]{2,1,0:T(8,128)(2,1)}, u32[]{:S(2)}, u32[]{:S(2)}) collective-permute-start(bf16[16,64,256]{2,1,0:T(8,128)(2,1)} %collective-permute-done.6.refs_10_.refs_1_), channel_id=1, source_target_pairs={{0,1},{1,2},{2,3},{3,0},{4,5},{5,6},{6,7},{7,4},{8,9},{9,10},{10,1... | collective-permute-start | bytes 1572872 | tf_op jit(solution)/shard_map/ppermute | solution.py:397
  98.9 18.4 %collective-permute-start = (bf16[16,32,256]{2,1,0:T(8,128)(2,1)}, bf16[16,32,256]{2,1,0:T(8,128)(2,1)S(1)}, u32[]{:S(2)}, u32[]{:S(2)}) collective-permute-start(bf16[16,32,256]{2,1,0:T(8,128)(2,1)} %get-tuple-element.16.refs_0_.refs_7_), channel_id=1, source_target_pairs={{0,1},{1,2},{2,3},{3,0},{4,5},{5,6},{6,7},{7,4},{8,9},{9,10},{10,1... | collective-permute-start | bytes 786440 | tf_op jit(solution)/shard_map/ppermute | solution.py:397
  99.0 18.4 %collective-permute-start.4 = (bf16[16,32,256]{2,1,0:T(8,128)(2,1)}, bf16[16,32,256]{2,1,0:T(8,128)(2,1)S(1)}, u32[]{:S(2)}, u32[]{:S(2)}) collective-permute-start(bf16[16,32,256]{2,1,0:T(8,128)(2,1)} %get-tuple-element.17.refs_4_.refs_11_), channel_id=1, source_target_pairs={{0,3},{1,0},{2,1},{3,2},{4,7},{5,4},{6,5},{7,6},{8,11},{9,8},{10,9... | collective-permute-start | bytes 786440 | tf_op jit(solution)/shard_map/ppermute | solution.py:397
  101.7 1.6 copy-start.1
  103.3 0.7 copy-start.4
  106.2 9.3 %copy-start.8 = (bf16[16,32,256]{2,1,0:T(8,128)(2,1)S(1)}, bf16[16,32,256]{2,1,0:T(8,128)(2,1)}, u32[]{:S(2)}) copy-start(bf16[16,32,256]{2,1,0:T(8,128)(2,1)} %get-tuple-element.16.refs_0_.refs_7_) | copy-start | bytes 786436
  106.2 11.0 %copy-start.9 = (bf16[16,32,256]{2,1,0:T(8,128)(2,1)S(1)}, bf16[16,32,256]{2,1,0:T(8,128)(2,1)}, u32[]{:S(2)}) copy-start(bf16[16,32,256]{2,1,0:T(8,128)(2,1)} %get-tuple-element.17.refs_4_.refs_11_) | copy-start | bytes 786436
  106.3 54.3 %all-to-all-start.3 = ((bf16[32,128,256]{2,1,0:T(8,128)(2,1)}), bf16[32,128,256]{2,1,0:T(8,128)(2,1)}, u32[]{:S(2)}, u32[]{:S(2)}) async-start(bf16[32,128,256]{2,1,0:T(8,128)(2,1)} %shard_map.57), calls=%async_computation.3 | async-start | bytes 4194304 | tf_op jit(solution)/shard_map/all_to_all | solution.py:380
  115.5 7.7 %collective-permute-start.2 = (bf16[16,32,256]{2,1,0:T(8,128)(2,1)S(1)}, bf16[16,32,256]{2,1,0:T(8,128)(2,1)S(1)}, u32[]{:S(2)}, u32[]{:S(2)}) collective-permute-start(bf16[16,32,256]{2,1,0:T(8,128)(2,1)S(1)} %copy-done.8), channel_id=1, source_target_pairs={{0,3},{1,0},{2,1},{3,2},{4,7},{5,4},{6,5},{7,6},{8,11},{9,8},{10,9... | collective-permute-start | bytes 786440 | tf_op jit(solution)/shard_map/ppermute | solution.py:397
  117.2 8.6 %collective-permute-start.3 = (bf16[16,32,256]{2,1,0:T(8,128)(2,1)S(1)}, bf16[16,32,256]{2,1,0:T(8,128)(2,1)S(1)}, u32[]{:S(2)}, u32[]{:S(2)}) collective-permute-start(bf16[16,32,256]{2,1,0:T(8,128)(2,1)S(1)} %copy-done.9), channel_id=1, source_target_pairs={{0,1},{1,2},{2,3},{3,0},{4,5},{5,6},{6,7},{7,4},{8,9},{9,10},{10,1... | collective-permute-start | bytes 786440 | tf_op jit(solution)/shard_map/ppermute | solution.py:397
  117.3 8.6 %copy-start.10 = (bf16[16,32,256]{2,1,0:T(8,128)(2,1)}, bf16[16,32,256]{2,1,0:T(8,128)(2,1)S(1)}, u32[]{:S(2)}) copy-start(bf16[16,32,256]{2,1,0:T(8,128)(2,1)S(1)} %collective-permute-done.refs_1_.refs_8_) | copy-start | bytes 786436
  117.3 14.2 %collective-permute-start.1 = (bf16[16,32,256]{2,1,0:T(8,128)(2,1)S(1)}, bf16[16,32,256]{2,1,0:T(8,128)(2,1)S(1)}, u32[]{:S(2)}, u32[]{:S(2)}) collective-permute-start(bf16[16,32,256]{2,1,0:T(8,128)(2,1)S(1)} %collective-permute-done.refs_1_.refs_8_), channel_id=1, source_target_pairs={{0,1},{1,2},{2,3},{3,0},{4,5},{5,6},{6,7},{7,4},{8,9},{9,10},{10,1... | collective-permute-start | bytes 786440 | tf_op jit(solution)/shard_map/ppermute | solution.py:397
  117.4 14.1 %copy-start.11 = (bf16[16,32,256]{2,1,0:T(8,128)(2,1)}, bf16[16,32,256]{2,1,0:T(8,128)(2,1)S(1)}, u32[]{:S(2)}) copy-start(bf16[16,32,256]{2,1,0:T(8,128)(2,1)S(1)} %collective-permute-done.4.refs_7_.refs_14_) | copy-start | bytes 786436
  117.4 14.8 %collective-permute-start.5 = (bf16[16,32,256]{2,1,0:T(8,128)(2,1)S(1)}, bf16[16,32,256]{2,1,0:T(8,128)(2,1)}, u32[]{:S(2)}, u32[]{:S(2)}) collective-permute-start(bf16[16,32,256]{2,1,0:T(8,128)(2,1)S(1)} %collective-permute-done.4.refs_7_.refs_14_), channel_id=1, source_target_pairs={{0,3},{1,0},{2,1},{3,2},{4,7},{5,4},{6,5},{7,6},{8,11},{9,8},{10,9... | collective-permute-start | bytes 786440 | tf_op jit(solution)/shard_map/ppermute | solution.py:397
  123.2 8.2 %copy-start.12 = (bf16[16,32,256]{2,1,0:T(8,128)(2,1)}, bf16[16,32,256]{2,1,0:T(8,128)(2,1)S(1)}, u32[]{:S(2)}) copy-start(bf16[16,32,256]{2,1,0:T(8,128)(2,1)S(1)} %collective-permute-done.2.refs_3_.refs_10_) | copy-start | bytes 786436
  125.8 5.6 %copy-start.13 = (bf16[16,32,256]{2,1,0:T(8,128)(2,1)}, bf16[16,32,256]{2,1,0:T(8,128)(2,1)S(1)}, u32[]{:S(2)}) copy-start(bf16[16,32,256]{2,1,0:T(8,128)(2,1)S(1)} %collective-permute-done.3.refs_5_.refs_12_) | copy-start | bytes 786436
  131.5 0.7 copy-start.14
  168.8 59.0 %copy-start.5 = (s32[1,4096]{1,0:T(1,128)S(1)}, s32[1,4096]{1,0:T(1,128)}, u32[]{:S(2)}) copy-start(s32[1,4096]{1,0:T(1,128)} %get-tuple-element.13.pos_ref) | copy-start | bytes 49156

commit v6 on v5

--- a/solution.py
+++ b/solution.py
@@ -237,6 +237,21 @@
 
     @pl.when((piece == 0) & live)
     def _():
+        for n in range(blocks):
+
+            @pl.when(block == n)
+            def _():
+                @pl.loop(0, tiles)
+                def _(j):
+                    slot = slot_ref[n, j]
+
+                    @pl.when(slot % 2 == 1)
+                    def _():
+                        for turn, ref in enumerate(latents[n * PLANES : (n + 1) * PLANES]):
+                            row = pl.multiple_of((y + PLANES - turn) % PLANES * tile_part, tile_part)
+                            pltpu.make_async_copy(ref.at[j], keys.at[j, pl.ds(row, tile_part)], tile_sem).start()
+                        pltpu.make_async_copy(second_ref.at[slot // 2], values.at[j], tile_sem).start()
+
         own = pl.ds(pl.multiple_of(block * part, part), part)
         for p in range(PLANES):
             if p == 0:
@@ -250,22 +265,6 @@
                 some = pl.ds(at, chunk)
                 pltpu.make_async_copy(sum_ref.at[blocks * p + block, some], weighted.at[p, some], sems.at[p]).start()
                 pltpu.make_async_copy(total_ref.at[blocks * p + block, some], total.at[p, some], sems.at[p]).start()
-            if p > 0:
-                continue
-            for n in range(blocks):
-
-                @pl.when(block == n)
-                def _():
-                    @pl.loop(0, tiles)
-                    def _(j):
-                        slot = slot_ref[n, j]
-
-                        @pl.when(slot % 2 == 1)
-                        def _():
-                            for turn, ref in enumerate(latents[n * PLANES : (n + 1) * PLANES]):
-                                row = pl.multiple_of((y + PLANES - turn) % PLANES * tile_part, tile_part)
-                                pltpu.make_async_copy(ref.at[j], keys.at[j, pl.ds(row, tile_part)], tile_sem).start()
-                            pltpu.make_async_copy(second_ref.at[slot // 2], values.at[j], tile_sem).start()
 
         @pl.loop(0, tiles)
         def _(j):
@@ -301,21 +300,24 @@
 def unpack_kernel(pos_ref, in_ref, out_ref, table, got):
     lanes = 128
     step = 256
-
-    @pl.loop(0, in_ref.shape[0] // step)
-    def _(c):
-        at = pl.ds(pl.multiple_of(c * step, step), step)
-        to = pl.multiple_of(2 * c * step, 2 * step)
-        table[pl.ds(to, step, stride=2), :] = in_ref[at, :lanes].astype(jnp.float32)
-        table[pl.ds(to + 1, step, stride=2), :] = in_ref[at, lanes:].astype(jnp.float32)
-
     count = out_ref.shape[0]
+    begin = pl.program_id(0) * count
+
+    @pl.when(pl.program_id(0) == 0)
+    def _():
+        @pl.loop(0, in_ref.shape[0] // step)
+        def _(c):
+            at = pl.ds(pl.multiple_of(c * step, step), step)
+            to = pl.multiple_of(2 * c * step, 2 * step)
+            table[pl.ds(to, step, stride=2), :] = in_ref[at, :lanes].astype(jnp.float32)
+            table[pl.ds(to + 1, step, stride=2), :] = in_ref[at, lanes:].astype(jnp.float32)
 
     @pl.loop(0, count // 32)
     def _(c):
         at = pl.multiple_of(c * 64, 64)
+        first = begin + c * 32
         for r in range(32):
-            i = pl.multiple_of(pos_ref[0, c * 32 + r], 2)
+            i = pl.multiple_of(pos_ref[0, first + r], 2)
             got[pl.ds(at + 2 * r, 2), :] = table[pl.ds(i, 2), :]
 
     @pl.loop(0, count // step)
@@ -488,14 +490,16 @@
     )(turns, y1, slot_table, *sums, *pieces, *latents, got_second, answers)
     back = exchange(answers)
     count = back.shape[0] * back.shape[1]
+    chunk = 1024
     return pl.pallas_call(
         unpack_kernel,
+        grid=(query_count // chunk,),
         in_specs=[SMEM, VMEM],
-        out_specs=VMEM,
+        out_specs=pl.BlockSpec((chunk, columns), lambda c: (c, 0)),
         out_shape=jax.ShapeDtypeStruct((query_count, columns), jnp.bfloat16),
         scratch_shapes=[
             pltpu.VMEM((2 * count, 128), jnp.float32),
-            pltpu.VMEM((2 * query_count, 128), jnp.float32),
+            pltpu.VMEM((2 * chunk, 128), jnp.float32),
         ],
         compiler_params=params(24),
         name="unpack",

time: 236 us -> 236 us (level)
  no operation moved by 1% of the time
where the time goes in v6:
time: 236 us; the launch traced here: 235 us
  Pallas kernels  63.1 us (27%)
  waiting for transfers between devices  59.7 us (25%)
  blocking collectives  58.9 us (25%)
  starting transfers between devices  43.7 us (19%)
  local copies, waits for them, and re-layouts  7.92 us (3%)
    all_to_all x1, blocking collectives, exchange(): return lax.all_to_all(v, 'dp', split_axis=0, concat_axis=0, tiled=True)  58.9 us
    ppermute x12, waiting for transfers between devices, shift(): lax.ppermute(v, 'label', [(i, (i + by) % PLANES) for i in range(PLANES)])  29.8 us
    pallas_call x1, Pallas kernels, shards(): pl.pallas_call(functools.partial(first_pass_kernel, scale), grid=(PLANES,...  28.3 us
    all_to_all x1, waiting for transfers between devices, shards(): lax.all_to_all(sent, 'dp', split_axis=0, concat_axis=0, tiled=True)  17.9 us
    all_to_all x3, starting transfers between devices, exchange(): return lax.all_to_all(v, 'dp', split_axis=0, concat_axis=0, tiled=True)  17.7 us
    ppermute x12, starting transfers between devices, shift(): lax.ppermute(v, 'label', [(i, (i + by) % PLANES) for i in range(PLANES)])  16.4 us
    all_to_all x3, waiting for transfers between devices, exchange(): return lax.all_to_all(v, 'dp', split_axis=0, concat_axis=0, tiled=True)  11.9 us
    all_to_all x1, starting transfers between devices, shards(): lax.all_to_all(sent, 'dp', split_axis=0, concat_axis=0, tiled=True)  9.61 us
  transfers between devices with their start and end apart: 16, of which 7 were waited for; matrix products, arithmetic and copies ran while one was open for 2% of the time, Pallas kernels for 16%

profile of v6, /device:TPU:1, one launch (start us, length us, event | category | flops | bytes accessed | tf_op | source)
XLA Modules:
  0.0 234.8 jit_solution(7631141262762223757)
XLA Ops:
  0.0 9.2 %pack.1 = (bf16[32,72,256]{2,1,0:T(8,128)(2,1)}, s32[1,4096]{1,0:T(1,128)}) custom-call(s32[1]{0:T(128)} %bitcast.y_ref, s32[1,4096]{1,0:T(1,128)} %bitcast.14, s32[2,16]{1,0:T(2,128)} %list_ref.1, bf16[4096,256]{1,0:T(8,128)(2,1)} %x_ref.1), custom_call_target="tpu_custom_call" | custom-call | tf_op jit(solution)/shard_map/pack/pallas_call | solution.py:355
  9.2 0.0 copy-start.7
  9.2 9.6 %all-to-all-start = ((bf16[32,72,256]{2,1,0:T(8,128)(2,1)}), bf16[32,72,256]{2,1,0:T(8,128)(2,1)}, u32[]{:S(2)}, u32[]{:S(2)}) async-start(bf16[32,72,256]{2,1,0:T(8,128)(2,1)} %get-tuple-element.14), calls=%async_computation | async-start | bytes 2359296 | tf_op jit(solution)/shard_map/all_to_all | solution.py:375
  18.8 0.2 fusion
  19.1 0.2 fusion.1.tile_ref
  19.3 0.0 copy-start
  19.3 17.9 %all-to-all-done.refs_9_.refs_0_ = bf16[32,72,256]{2,1,0:T(8,128)(2,1)} async-done(((bf16[32,72,256]{2,1,0:T(8,128)(2,1)}), bf16[32,72,256]{2,1,0:T(8,128)(2,1)}, u32[]{:S(2)}, u32[]{:S(2)}) %all-to-all-start) | async-done | bytes 1179680 | tf_op jit(solution)/shard_map/all_to_all | solution.py:375
  37.2 1.1 slice.9
  38.3 1.8 shard_map.55
  40.1 3.9 %all-to-all-start.1 = ((bf16[32,64,256]{2,1,0:T(8,128)(2,1)}), bf16[32,64,256]{2,1,0:T(8,128)(2,1)S(1)}, u32[]{:S(2)}, u32[]{:S(2)}) async-start(bf16[32,64,256]{2,1,0:T(8,128)(2,1)} %shard_map.55), calls=%async_computation.1 | async-start | bytes 2097152 | tf_op jit(solution)/shard_map/all_to_all | solution.py:382
  44.0 3.6 %shard_map.56 = bf16[32,128,256]{2,1,0:T(8,128)(2,1)S(1)} custom-call(s32[32,2]{1,0:T(8,128)S(1)} %bitcast.10, bf16[32,128,256]{2,1,0:T(8,128)(2,1)S(1)} %bitcast.7), custom_call_target="tpu_custom_call" | custom-call | tf_op jit(solution)/shard_map/pallas_call | solution.py:385
  47.7 0.0 copy-done.3
  47.7 0.0 copy-start.2
  47.7 1.3 copy-done.2
  49.0 11.9 %all-to-all-done.1.arrived_ref = bf16[32,64,256]{2,1,0:T(8,128)(2,1)S(1)} async-done(((bf16[32,64,256]{2,1,0:T(8,128)(2,1)}), bf16[32,64,256]{2,1,0:T(8,128)(2,1)S(1)}, u32[]{:S(2)}, u32[]{:S(2)}) %all-to-all-start.1) | async-done | bytes 1048608 | tf_op jit(solution)/shard_map/all_to_all | solution.py:382
  60.9 4.6 %all-to-all-start.2 = ((bf16[32,128,256]{2,1,0:T(8,128)(2,1)}), bf16[32,128,256]{2,1,0:T(8,128)(2,1)}, u32[]{:S(2)}, u32[]{:S(2)}) async-start(bf16[32,128,256]{2,1,0:T(8,128)(2,1)} %copy-done.2), calls=%async_computation.2 | async-start | bytes 4194304 | tf_op jit(solution)/shard_map/all_to_all | solution.py:382
  65.5 0.0 copy-start.15
  65.5 2.3 fusion.3
  67.8 2.7 %collective-permute-start.9 = (bf16[16,64,256]{2,1,0:T(8,128)(2,1)}, bf16[16,64,256]{2,1,0:T(8,128)(2,1)}, u32[]{:S(2)}, u32[]{:S(2)}) collective-permute-start(bf16[16,64,256]{2,1,0:T(8,128)(2,1)} %get-tuple-element.21), channel_id=1, source_target_pairs={{0,3},{1,0},{2,1},{3,2},{4,7},{5,4},{6,5},{7,6},{8,11},{9,8},{10,9... | collective-permute-start | bytes 1572872 | tf_op jit(solution)/shard_map/ppermute | solution.py:399
  70.6 0.0 copy-done.15
  70.6 0.1 reshape.88
  70.7 0.0 collective-permute-start.7
  70.7 0.1 collective-permute-start.6
  70.8 2.7 %collective-permute-start.8 = (bf16[16,64,256]{2,1,0:T(8,128)(2,1)}, bf16[16,64,256]{2,1,0:T(8,128)(2,1)}, u32[]{:S(2)}, u32[]{:S(2)}) collective-permute-start(bf16[16,64,256]{2,1,0:T(8,128)(2,1)} %get-tuple-element.22), channel_id=1, source_target_pairs={{0,3},{1,0},{2,1},{3,2},{4,7},{5,4},{6,5},{7,6},{8,11},{9,8},{10,9... | collective-permute-start | bytes 1572872 | tf_op jit(solution)/shard_map/ppermute | solution.py:399
  73.5 8.4 %collective-permute-done.9.refs_13_.refs_4_ = bf16[16,64,256]{2,1,0:T(8,128)(2,1)} collective-permute-done((bf16[16,64,256]{2,1,0:T(8,128)(2,1)}, bf16[16,64,256]{2,1,0:T(8,128)(2,1)}, u32[]{:S(2)}, u32[]{:S(2)}) %collective-permute-start.9) | collective-permute-done | bytes 524320 | tf_op jit(solution)/shard_map/ppermute | solution.py:399
  81.9 3.4 %collective-permute-start.11 = (bf16[16,64,256]{2,1,0:T(8,128)(2,1)}, bf16[16,64,256]{2,1,0:T(8,128)(2,1)}, u32[]{:S(2)}, u32[]{:S(2)}) collective-permute-start(bf16[16,64,256]{2,1,0:T(8,128)(2,1)} %collective-permute-done.9.refs_13_.refs_4_), channel_id=1, source_target_pairs={{0,3},{1,0},{2,1},{3,2},{4,7},{5,4},{6,5},{7,6},{8,11},{9,8},{10,9... | collective-permute-start | bytes 1572872 | tf_op jit(solution)/shard_map/ppermute | solution.py:399
  85.3 0.2 convert_reduce_fusion
  85.4 0.1 reduce_sum.21
  85.5 0.6 multiply_add_fusion.slot_ref
  86.1 10.2 %collective-permute-done.6.refs_10_.refs_1_ = bf16[16,64,256]{2,1,0:T(8,128)(2,1)} collective-permute-done((bf16[16,64,256]{2,1,0:T(8,128)(2,1)}, bf16[16,64,256]{2,1,0:T(8,128)(2,1)}, u32[]{:S(2)}, u32[]{:S(2)}) %collective-permute-start.6) | collective-permute-done | bytes 524320 | tf_op jit(solution)/shard_map/ppermute | solution.py:399
  96.3 0.0 collective-permute-start.10
  96.3 2.6 %pick.1 = (bf16[16,32,256]{2,1,0:T(8,128)(2,1)}, bf16[16,32,256]{2,1,0:T(8,128)(2,1)}, s32[2]{0:T(128)}) custom-call(s32[2,16]{1,0:T(2,128)} %multiply_add_fusion.slot_ref, bf16[32,64,256]{2,1,0:T(8,128)(2,1)} %copy-done.6), custom_call_target="tpu_custom_call" | custom-call | tf_op jit(solution)/shard_map/pick/pallas_call | solution.py:405
  98.9 0.1 collective-permute-start
  99.0 0.0 collective-permute-done.7.refs_11_.refs_2_
  99.0 2.7 %collective-permute-start.4 = (bf16[16,32,256]{2,1,0:T(8,128)(2,1)}, bf16[16,32,256]{2,1,0:T(8,128)(2,1)S(1)}, u32[]{:S(2)}, u32[]{:S(2)}) collective-permute-start(bf16[16,32,256]{2,1,0:T(8,128)(2,1)} %get-tuple-element.17.refs_4_.refs_11_), channel_id=1, source_target_pairs={{0,3},{1,0},{2,1},{3,2},{4,7},{5,4},{6,5},{7,6},{8,11},{9,8},{10,9... | collective-permute-start | bytes 786440 | tf_op jit(solution)/shard_map/ppermute | solution.py:399
  101.7 1.6 copy-done.1
  103.3 0.7 copy-done.4
  104.0 2.2 shard_map.57
  106.2 0.0 copy-start.8
  106.2 0.0 copy-start.9
  106.3 0.0 all-to-all-done.2.refs_8_
  106.3 9.2 %all-to-all-start.3 = ((bf16[32,128,256]{2,1,0:T(8,128)(2,1)}), bf16[32,128,256]{2,1,0:T(8,128)(2,1)}, u32[]{:S(2)}, u32[]{:S(2)}) async-start(bf16[32,128,256]{2,1,0:T(8,128)(2,1)} %shard_map.57), calls=%async_computation.3 | async-start | bytes 4194304 | tf_op jit(solution)/shard_map/all_to_all | solution.py:382
  115.5 0.0 collective-permute-done.8.refs_12_.refs_3_
  115.5 1.7 collective-permute-start.2
  117.2 0.0 collective-permute-done.11.refs_15_.refs_6_
  117.2 0.0 collective-permute-start.3
  117.2 0.0 collective-permute-done.refs_1_.refs_8_
  117.3 0.0 copy-start.10
  117.3 0.1 collective-permute-start.1
  117.4 0.0 collective-permute-done.4.refs_7_.refs_14_
  117.4 2.8 %collective-permute-start.5 = (bf16[16,32,256]{2,1,0:T(8,128)(2,1)S(1)}, bf16[16,32,256]{2,1,0:T(8,128)(2,1)}, u32[]{:S(2)}, u32[]{:S(2)}) collective-permute-start(bf16[16,32,256]{2,1,0:T(8,128)(2,1)S(1)} %collective-permute-done.4.refs_7_.refs_14_), channel_id=1, source_target_pairs={{0,3},{1,0},{2,1},{3,2},{4,7},{5,4},{6,5},{7,6},{8,11},{9,8},{10,9... | collective-permute-start | bytes 786440 | tf_op jit(solution)/shard_map/ppermute | solution.py:399
  120.2 0.0 collective-permute-done.10.refs_14_.refs_5_
  120.2 3.0 %collective-permute-done.2.refs_3_.refs_10_ = bf16[16,32,256]{2,1,0:T(8,128)(2,1)S(1)} collective-permute-done((bf16[16,32,256]{2,1,0:T(8,128)(2,1)S(1)}, bf16[16,32,256]{2,1,0:T(8,128)(2,1)S(1)}, u32[]{:S(2)}, u32[]{:S(2)}) %collective-permute-start.2) | collective-permute-done | bytes 262176 | tf_op jit(solution)/shard_map/ppermute | solution.py:399
  123.2 2.6 %collective-permute-done.3.refs_5_.refs_12_ = bf16[16,32,256]{2,1,0:T(8,128)(2,1)S(1)} collective-permute-done((bf16[16,32,256]{2,1,0:T(8,128)(2,1)S(1)}, bf16[16,32,256]{2,1,0:T(8,128)(2,1)S(1)}, u32[]{:S(2)}, u32[]{:S(2)}) %collective-permute-start.3) | collective-permute-done | bytes 262176 | tf_op jit(solution)/shard_map/ppermute | solution.py:399
  125.8 0.0 copy-done.10
  125.8 5.6 %collective-permute-done.1.refs_2_.refs_9_ = bf16[16,32,256]{2,1,0:T(8,128)(2,1)S(1)} collective-permute-done((bf16[16,32,256]{2,1,0:T(8,128)(2,1)S(1)}, bf16[16,32,256]{2,1,0:T(8,128)(2,1)S(1)}, u32[]{:S(2)}, u32[]{:S(2)}) %collective-permute-start.1) | collective-permute-done | bytes 262176 | tf_op jit(solution)/shard_map/ppermute | solution.py:399
  131.5 0.0 copy-done.12
  131.5 0.7 copy-done.14
  132.2 0.0 collective-permute-done.5.refs_6_.refs_13_
  132.2 28.3 %first_pass.1 = (f32[8,1024,256]{2,1,0:T(8,128)}, f32[8,1024,128]{2,1,0:T(8,128)}, bf16[32,256,256]{2,1,0:T(8,128)(2,1)}) custom-call(s32[1]{0:T(128)} %bitcast.y_ref, s32[2,16]{1,0:T(2,128)} %multiply_add_fusion.slot_ref, bf16[16,32,256]{2,1,0:T(8,128)(2,1)} %get-tuple-element.16.refs_0_.refs_7_, bf16[16,32,256]{2,1,0:T(8,128)(2,1)} %copy-done.10, ...), custom_call_target="tpu_custom_call" | custom-call | flops 17179869184 | bytes 12582912 | tf_op jit(solution)/shard_map/first_pass/pallas_call | solution.py:433
  160.5 0.0 all-to-all-done.3.refs_15_
  160.5 8.8 %finish.1 = bf16[32,256,256]{2,1,0:T(8,128)(2,1)} custom-call(s32[2]{0:T(128)} %get-tuple-element.15.turns_ref, s32[1]{0:T(128)} %bitcast.y_ref, s32[2,16]{1,0:T(2,128)} %multiply_add_fusion.slot_ref, f32[8,1024,256]{2,1,0:T(8,128)} %get-tuple-element.18.sum_ref, f32[8,1024,128]{2,1,0:T(8,128)} %get-tuple-element.19.total_ref, ...), custom_call_target="tpu_custom_call", output_to_operand_aliasing={{}: (21, {})} | custom-call | tf_op jit(solution)/shard_map/finish/pallas_call | solution.py:469
  169.3 58.9 %all_to_all.25 = bf16[32,256,256]{2,1,0:T(8,128)(2,1)S(1)} all-to-all(bf16[32,256,256]{2,1,0:T(8,128)(2,1)} %finish.1), channel_id=1, replica_groups=mesh['dp'=32,'label'=4] {'dp'}, dimensions={0} | all-to-all | bytes 8388608 | tf_op jit(solution)/shard_map/all_to_all | solution.py:382
  228.2 6.6 %unpack.1 = bf16[4096,256]{1,0:T(8,128)(2,1)} custom-call(s32[1,4096]{1,0:T(1,128)S(1)} %copy-done.5, bf16[8192,256]{1,0:T(8,128)(2,1)S(1)} %bitcast.6), custom_call_target="tpu_custom_call" | custom-call | tf_op jit(solution)/shard_map/unpack/pallas_call | solution.py:494
  (20 shorter events, 0.1 us)
Async XLA Ops:
  9.2 9.6 %copy-start.7 = (bf16[4096,256]{1,0:T(8,128)(2,1)S(1)}, bf16[4096,256]{1,0:T(8,128)(2,1)}, u32[]{:S(2)}) copy-start(bf16[4096,256]{1,0:T(8,128)(2,1)} %param.7) | copy-start | bytes 6291460
  9.2 28.0 %all-to-all-start = ((bf16[32,72,256]{2,1,0:T(8,128)(2,1)}), bf16[32,72,256]{2,1,0:T(8,128)(2,1)}, u32[]{:S(2)}, u32[]{:S(2)}) async-start(bf16[32,72,256]{2,1,0:T(8,128)(2,1)} %get-tuple-element.14), calls=%async_computation | async-start | bytes 2359296 | tf_op jit(solution)/shard_map/all_to_all | solution.py:375
  19.3 24.8 %copy-start = (bf16[4096,256]{1,0:T(8,128)(2,1)S(1)}, bf16[4096,256]{1,0:T(8,128)(2,1)}, u32[]{:S(2)}) copy-start(bf16[4096,256]{1,0:T(8,128)(2,1)} %param.8) | copy-start | bytes 6291460
  38.3 9.4 %copy-start.3 = (s32[32,1,2]{2,1,0:T(1,128)}, s32[32,1,2]{2,1,0:T(1,128)S(1)}, u32[]{:S(2)}) copy-start(s32[32,1,2]{2,1,0:T(1,128)S(1)} %convert_element_type.19) | copy-start | bytes 772
  40.1 20.8 %all-to-all-start.1 = ((bf16[32,64,256]{2,1,0:T(8,128)(2,1)}), bf16[32,64,256]{2,1,0:T(8,128)(2,1)S(1)}, u32[]{:S(2)}, u32[]{:S(2)}) async-start(bf16[32,64,256]{2,1,0:T(8,128)(2,1)} %shard_map.55), calls=%async_computation.1 | async-start | bytes 2097152 | tf_op jit(solution)/shard_map/all_to_all | solution.py:382
  47.7 1.3 copy-start.2
  60.9 6.9 %copy-start.6 = (bf16[32,64,256]{2,1,0:T(8,128)(2,1)}, bf16[32,64,256]{2,1,0:T(8,128)(2,1)S(1)}, u32[]{:S(2)}) copy-start(bf16[32,64,256]{2,1,0:T(8,128)(2,1)S(1)} %all-to-all-done.1.arrived_ref) | copy-start | bytes 3145732
  60.9 45.3 %all-to-all-start.2 = ((bf16[32,128,256]{2,1,0:T(8,128)(2,1)}), bf16[32,128,256]{2,1,0:T(8,128)(2,1)}, u32[]{:S(2)}, u32[]{:S(2)}) async-start(bf16[32,128,256]{2,1,0:T(8,128)(2,1)} %copy-done.2), calls=%async_computation.2 | async-start | bytes 4194304 | tf_op jit(solution)/shard_map/all_to_all | solution.py:382
  65.5 5.1 %copy-start.15 = (s32[2,16]{1,0:T(2,128)S(1)}, s32[2,16]{1,0:T(2,128)}, u32[]{:S(2)}) copy-start(s32[2,16]{1,0:T(2,128)} %list_ref.1) | copy-start | bytes 388
  67.8 14.0 %collective-permute-start.9 = (bf16[16,64,256]{2,1,0:T(8,128)(2,1)}, bf16[16,64,256]{2,1,0:T(8,128)(2,1)}, u32[]{:S(2)}, u32[]{:S(2)}) collective-permute-start(bf16[16,64,256]{2,1,0:T(8,128)(2,1)} %get-tuple-element.21), channel_id=1, source_target_pairs={{0,3},{1,0},{2,1},{3,2},{4,7},{5,4},{6,5},{7,6},{8,11},{9,8},{10,9... | collective-permute-start | bytes 1572872 | tf_op jit(solution)/shard_map/ppermute | solution.py:399
  70.7 28.3 %collective-permute-start.7 = (bf16[16,64,256]{2,1,0:T(8,128)(2,1)}, bf16[16,64,256]{2,1,0:T(8,128)(2,1)}, u32[]{:S(2)}, u32[]{:S(2)}) collective-permute-start(bf16[16,64,256]{2,1,0:T(8,128)(2,1)} %get-tuple-element.21), channel_id=1, source_target_pairs={{0,1},{1,2},{2,3},{3,0},{4,5},{5,6},{6,7},{7,4},{8,9},{9,10},{10,1... | collective-permute-start | bytes 1572872 | tf_op jit(solution)/shard_map/ppermute | solution.py:399
  70.7 25.6 %collective-permute-start.6 = (bf16[16,64,256]{2,1,0:T(8,128)(2,1)}, bf16[16,64,256]{2,1,0:T(8,128)(2,1)}, u32[]{:S(2)}, u32[]{:S(2)}) collective-permute-start(bf16[16,64,256]{2,1,0:T(8,128)(2,1)} %get-tuple-element.22), channel_id=1, source_target_pairs={{0,1},{1,2},{2,3},{3,0},{4,5},{5,6},{6,7},{7,4},{8,9},{9,10},{10,1... | collective-permute-start | bytes 1572872 | tf_op jit(solution)/shard_map/ppermute | solution.py:399
  70.8 44.7 %collective-permute-start.8 = (bf16[16,64,256]{2,1,0:T(8,128)(2,1)}, bf16[16,64,256]{2,1,0:T(8,128)(2,1)}, u32[]{:S(2)}, u32[]{:S(2)}) collective-permute-start(bf16[16,64,256]{2,1,0:T(8,128)(2,1)} %get-tuple-element.22), channel_id=1, source_target_pairs={{0,3},{1,0},{2,1},{3,2},{4,7},{5,4},{6,5},{7,6},{8,11},{9,8},{10,9... | collective-permute-start | bytes 1572872 | tf_op jit(solution)/shard_map/ppermute | solution.py:399
  81.9 35.4 %collective-permute-start.11 = (bf16[16,64,256]{2,1,0:T(8,128)(2,1)}, bf16[16,64,256]{2,1,0:T(8,128)(2,1)}, u32[]{:S(2)}, u32[]{:S(2)}) collective-permute-start(bf16[16,64,256]{2,1,0:T(8,128)(2,1)} %collective-permute-done.9.refs_13_.refs_4_), channel_id=1, source_target_pairs={{0,3},{1,0},{2,1},{3,2},{4,7},{5,4},{6,5},{7,6},{8,11},{9,8},{10,9... | collective-permute-start | bytes 1572872 | tf_op jit(solution)/shard_map/ppermute | solution.py:399
  96.3 23.9 %collective-permute-start.10 = (bf16[16,64,256]{2,1,0:T(8,128)(2,1)}, bf16[16,64,256]{2,1,0:T(8,128)(2,1)}, u32[]{:S(2)}, u32[]{:S(2)}) collective-permute-start(bf16[16,64,256]{2,1,0:T(8,128)(2,1)} %collective-permute-done.6.refs_10_.refs_1_), channel_id=1, source_target_pairs={{0,1},{1,2},{2,3},{3,0},{4,5},{5,6},{6,7},{7,4},{8,9},{9,10},{10,1... | collective-permute-start | bytes 1572872 | tf_op jit(solution)/shard_map/ppermute | solution.py:399
  98.9 18.4 %collective-permute-start = (bf16[16,32,256]{2,1,0:T(8,128)(2,1)}, bf16[16,32,256]{2,1,0:T(8,128)(2,1)S(1)}, u32[]{:S(2)}, u32[]{:S(2)}) collective-permute-start(bf16[16,32,256]{2,1,0:T(8,128)(2,1)} %get-tuple-element.16.refs_0_.refs_7_), channel_id=1, source_target_pairs={{0,1},{1,2},{2,3},{3,0},{4,5},{5,6},{6,7},{7,4},{8,9},{9,10},{10,1... | collective-permute-start | bytes 786440 | tf_op jit(solution)/shard_map/ppermute | solution.py:399
  99.0 18.4 %collective-permute-start.4 = (bf16[16,32,256]{2,1,0:T(8,128)(2,1)}, bf16[16,32,256]{2,1,0:T(8,128)(2,1)S(1)}, u32[]{:S(2)}, u32[]{:S(2)}) collective-permute-start(bf16[16,32,256]{2,1,0:T(8,128)(2,1)} %get-tuple-element.17.refs_4_.refs_11_), channel_id=1, source_target_pairs={{0,3},{1,0},{2,1},{3,2},{4,7},{5,4},{6,5},{7,6},{8,11},{9,8},{10,9... | collective-permute-start | bytes 786440 | tf_op jit(solution)/shard_map/ppermute | solution.py:399
  101.7 1.6 copy-start.1
  103.3 0.7 copy-start.4
  106.2 9.3 %copy-start.8 = (bf16[16,32,256]{2,1,0:T(8,128)(2,1)S(1)}, bf16[16,32,256]{2,1,0:T(8,128)(2,1)}, u32[]{:S(2)}) copy-start(bf16[16,32,256]{2,1,0:T(8,128)(2,1)} %get-tuple-element.16.refs_0_.refs_7_) | copy-start | bytes 786436
  106.2 11.0 %copy-start.9 = (bf16[16,32,256]{2,1,0:T(8,128)(2,1)S(1)}, bf16[16,32,256]{2,1,0:T(8,128)(2,1)}, u32[]{:S(2)}) copy-start(bf16[16,32,256]{2,1,0:T(8,128)(2,1)} %get-tuple-element.17.refs_4_.refs_11_) | copy-start | bytes 786436
  106.3 54.3 %all-to-all-start.3 = ((bf16[32,128,256]{2,1,0:T(8,128)(2,1)}), bf16[32,128,256]{2,1,0:T(8,128)(2,1)}, u32[]{:S(2)}, u32[]{:S(2)}) async-start(bf16[32,128,256]{2,1,0:T(8,128)(2,1)} %shard_map.57), calls=%async_computation.3 | async-start | bytes 4194304 | tf_op jit(solution)/shard_map/all_to_all | solution.py:382
  115.5 7.7 %collective-permute-start.2 = (bf16[16,32,256]{2,1,0:T(8,128)(2,1)S(1)}, bf16[16,32,256]{2,1,0:T(8,128)(2,1)S(1)}, u32[]{:S(2)}, u32[]{:S(2)}) collective-permute-start(bf16[16,32,256]{2,1,0:T(8,128)(2,1)S(1)} %copy-done.8), channel_id=1, source_target_pairs={{0,3},{1,0},{2,1},{3,2},{4,7},{5,4},{6,5},{7,6},{8,11},{9,8},{10,9... | collective-permute-start | bytes 786440 | tf_op jit(solution)/shard_map/ppermute | solution.py:399
  117.2 8.6 %collective-permute-start.3 = (bf16[16,32,256]{2,1,0:T(8,128)(2,1)S(1)}, bf16[16,32,256]{2,1,0:T(8,128)(2,1)S(1)}, u32[]{:S(2)}, u32[]{:S(2)}) collective-permute-start(bf16[16,32,256]{2,1,0:T(8,128)(2,1)S(1)} %copy-done.9), channel_id=1, source_target_pairs={{0,1},{1,2},{2,3},{3,0},{4,5},{5,6},{6,7},{7,4},{8,9},{9,10},{10,1... | collective-permute-start | bytes 786440 | tf_op jit(solution)/shard_map/ppermute | solution.py:399
  117.3 8.6 %copy-start.10 = (bf16[16,32,256]{2,1,0:T(8,128)(2,1)}, bf16[16,32,256]{2,1,0:T(8,128)(2,1)S(1)}, u32[]{:S(2)}) copy-start(bf16[16,32,256]{2,1,0:T(8,128)(2,1)S(1)} %collective-permute-done.refs_1_.refs_8_) | copy-start | bytes 786436
  117.3 14.2 %collective-permute-start.1 = (bf16[16,32,256]{2,1,0:T(8,128)(2,1)S(1)}, bf16[16,32,256]{2,1,0:T(8,128)(2,1)S(1)}, u32[]{:S(2)}, u32[]{:S(2)}) collective-permute-start(bf16[16,32,256]{2,1,0:T(8,128)(2,1)S(1)} %collective-permute-done.refs_1_.refs_8_), channel_id=1, source_target_pairs={{0,1},{1,2},{2,3},{3,0},{4,5},{5,6},{6,7},{7,4},{8,9},{9,10},{10,1... | collective-permute-start | bytes 786440 | tf_op jit(solution)/shard_map/ppermute | solution.py:399
  117.4 14.1 %copy-start.11 = (bf16[16,32,256]{2,1,0:T(8,128)(2,1)}, bf16[16,32,256]{2,1,0:T(8,128)(2,1)S(1)}, u32[]{:S(2)}) copy-start(bf16[16,32,256]{2,1,0:T(8,128)(2,1)S(1)} %collective-permute-done.4.refs_7_.refs_14_) | copy-start | bytes 786436
  117.4 14.8 %collective-permute-start.5 = (bf16[16,32,256]{2,1,0:T(8,128)(2,1)S(1)}, bf16[16,32,256]{2,1,0:T(8,128)(2,1)}, u32[]{:S(2)}, u32[]{:S(2)}) collective-permute-start(bf16[16,32,256]{2,1,0:T(8,128)(2,1)S(1)} %collective-permute-done.4.refs_7_.refs_14_), channel_id=1, source_target_pairs={{0,3},{1,0},{2,1},{3,2},{4,7},{5,4},{6,5},{7,6},{8,11},{9,8},{10,9... | collective-permute-start | bytes 786440 | tf_op jit(solution)/shard_map/ppermute | solution.py:399
  123.2 8.2 %copy-start.12 = (bf16[16,32,256]{2,1,0:T(8,128)(2,1)}, bf16[16,32,256]{2,1,0:T(8,128)(2,1)S(1)}, u32[]{:S(2)}) copy-start(bf16[16,32,256]{2,1,0:T(8,128)(2,1)S(1)} %collective-permute-done.2.refs_3_.refs_10_) | copy-start | bytes 786436
  125.8 5.6 %copy-start.13 = (bf16[16,32,256]{2,1,0:T(8,128)(2,1)}, bf16[16,32,256]{2,1,0:T(8,128)(2,1)S(1)}, u32[]{:S(2)}) copy-start(bf16[16,32,256]{2,1,0:T(8,128)(2,1)S(1)} %collective-permute-done.3.refs_5_.refs_12_) | copy-start | bytes 786436
  131.5 0.7 copy-start.14
  169.3 58.9 %copy-start.5 = (s32[1,4096]{1,0:T(1,128)S(1)}, s32[1,4096]{1,0:T(1,128)}, u32[]{:S(2)}) copy-start(s32[1,4096]{1,0:T(1,128)} %get-tuple-element.13.pos_ref) | copy-start | bytes 49156
